TPU v7x, 32 devices: a whole 2x2x4 slice. The times are simulated.
32 devices in a mesh: fsdp: 32 (over z, y, x, core).
Axes of the slice: x: 2, y: 2, z: 4, core: 2. Of those that a mesh axis runs over, the one named last changes fastest.
Arguments:
- inputs: bfloat16 [2, 32, 128, 1024], P(None, 'fsdp'), may hold values from -6 to 6
- lengths: int32 [2, 32], P(None, 'fsdp'), may hold values from 32 to 128, as said below
- cotangent: bfloat16 [2, 32, 128, 1024], P(None, 'fsdp'), may hold values from -6 to 6
- v_weight: bfloat16 [1024, 2048], P('fsdp'), may hold values from -0.1875 to 0.1875
- mx_weight: bfloat16 [1024, 4224], P('fsdp'), may hold values from -0.1875 to 0.1875
- h_weight: bfloat16 [2048, 1024], P('fsdp'), may hold values from -0.5 to 0.5
- up_weight: bfloat16 [1024, 4096], P('fsdp'), may hold values from -0.1875 to 0.1875
- down_weight: bfloat16 [4096, 1024], P('fsdp'), may hold values from -0.09375 to 0.09375
- small_params: bfloat16 [83712], P('fsdp'), may hold values from -4 to 4
Outputs:
- outputs: bfloat16 [2, 32, 128, 1024], P(None, 'fsdp')
- input_grads: bfloat16 [2, 32, 128, 1024], P(None, 'fsdp')
- v_weight_grad: float32 [1024, 2048], P('fsdp')
- mx_weight_grad: float32 [1024, 4224], P('fsdp')
- h_weight_grad: float32 [2048, 1024], P('fsdp')
- up_weight_grad: float32 [1024, 4096], P('fsdp')
- down_weight_grad: float32 [4096, 1024], P('fsdp')
- small_params_grad: float32 [83712], P('fsdp')
Inputs may be any that keep to these rules, and one draw needn't show every extreme that they name: lengths[i, s] counts the valid slots of sequence s of micro-batch i from its first slot; some sequence has 128 and some 32.
All inputs are finite; a program needn't handle non-finite values.
Results may differ from a plain program's by a relative error of at most 0.011.
Values may be sent and summed in bfloat16 or wider, within the bound.
A program may use at most 320 MiB of HBM per device.

v0:
```python
from functools import partial
import math

import jax
import jax.numpy as jnp
from jax import lax
from jax.sharding import PartitionSpec as P

D = 1024
Z = 128
VALUE_WIDTH = 2048
H = 16
FF = 4096
STRETCH = 128


epsilon = 1e-05
highest_precision = lax.Precision.HIGHEST


def split_vector(flat_vector):
    extents = (
        2 * D,
        2 * D,
        D,
        4 * Z,
        STRETCH,
        VALUE_WIDTH,
        2 * D + Z + VALUE_WIDTH,
        D,
        FF,
        D,
        4 * D * H,
    )
    pieces = []
    offset = 0
    for extent in extents:
        pieces.append(flat_vector[offset : offset + extent])
        offset = offset + extent
    return pieces


def normalize(features, norm_gain, norm_shift):
    average = jnp.mean(features, axis=-1, keepdims=True)
    centered = features - average
    spread = jnp.mean(centered * centered, axis=-1, keepdims=True)
    return centered * lax.rsqrt(spread + epsilon) * norm_gain + norm_shift


def smooth_signal(signal, ema_params):
    sequence_length, width_all = signal.shape
    block = min(32, sequence_length)
    count = sequence_length // block
    gate_rate = jax.nn.sigmoid(ema_params[0])
    retain = 1.0 - gate_rate * jax.nn.sigmoid(ema_params[1])
    weight = gate_rate * ema_params[2] * ema_params[3] * (1.0 / math.sqrt(ema_params.shape[2]))
    lag_steps = jnp.arange(block).astype(jnp.float32)
    powers = jnp.exp(lag_steps[:, None, None] * jnp.log(retain)[None, :, :])
    kernel = jnp.einsum("jch,ch->cj", powers, weight, precision=highest_precision)
    pattern = jnp.concatenate(
        [kernel[:, :1], jnp.zeros((width_all, block - 1), jnp.float32), kernel[:, 1:][:, ::-1]],
        axis=1,
    )
    tiled = jnp.tile(pattern, (1, block))[:, : block * (2 * block - 2)]
    toeplitz = tiled.reshape(width_all, block, 2 * block - 2)[:, :, :block]
    blocks = signal.reshape(count, block, width_all)
    inside = jnp.einsum("cts,nsc->ntc", toeplitz, blocks, precision=highest_precision)
    local_sums = jnp.einsum("nsc,sch->nch", blocks, powers[::-1], precision=highest_precision)
    whole_decay = powers[-1] * retain

    def advance(state, piece):
        return (whole_decay * state + piece, state)

    final_state, starts = lax.scan(advance, jnp.zeros(retain.shape, jnp.float32), local_sums)
    carried = jnp.einsum(
        "nch,tch->ntc", starts * weight, powers * retain[None], precision=highest_precision
    )
    return (inside + carried).reshape(sequence_length, width_all)


def offset_table(relative):
    places = jnp.arange(STRETCH)
    offsets = places[:, None] - places[None, :]
    onehot = (offsets[:, :, None] == places[None, None, :]).astype(jnp.float32)
    table = jnp.dot(
        onehot.reshape(STRETCH * STRETCH, STRETCH), relative, precision=highest_precision
    ).reshape(STRETCH, STRETCH)
    return (table, offsets >= 0)


def attention_weights(raw_scores, relative):
    table, causal = offset_table(relative)
    scores = jnp.where(causal, raw_scores * (1.0 / math.sqrt(Z)) + table, -1e30)
    largest = jnp.max(scores, axis=-1, keepdims=True)
    raised = jnp.exp(scores - largest)
    return raised / jnp.sum(raised, axis=-1, keepdims=True)


def first_piece(valid, inputs_row, gain_one, shift_one, omega_scale, ema_params):
    normed = normalize(inputs_row, gain_one, shift_one)
    masked = normed * valid
    mixed = jax.nn.silu(smooth_signal(masked, ema_params) + omega_scale * masked)
    return (normed, mixed)


def second_piece(values_mm, v_bias, base_mm, mx_bias, affine):
    values = jax.nn.silu(values_mm + v_bias)
    base = base_mm + mx_bias
    update = jax.nn.sigmoid(base[:, :D])
    shared = jax.nn.silu(base[:, D : D + Z + VALUE_WIDTH])
    hidden_x = base[:, D + Z + VALUE_WIDTH :]
    latent = shared[:, :Z]
    reset = shared[:, Z:]
    query = latent * (1.0 + affine[0]) + affine[2]
    keys_float = latent * (1.0 + affine[1]) + affine[3]
    return (values, update, reset, hidden_x, query, keys_float)


def fifth_piece(valid, hidden_mm, hidden_x, h_bias, update, inputs_row, gain_two, shift_two):
    hidden = jax.nn.silu(hidden_x + hidden_mm + h_bias)
    first = inputs_row + valid * update * (hidden - inputs_row)
    return (first, normalize(first, gain_two, shift_two))


def activate(up_mm, up_bias):
    return jax.nn.silu(up_mm + up_bias)


def forward_rows(inputs_row, valid, weights):
    v_full, mx_full, h_full, up_full, down_full, small_full = weights
    parts = [piece.astype(jnp.float32) for piece in split_vector(small_full)]
    (
        gains,
        shifts,
        omega_scale,
        affine,
        relative,
        v_bias,
        mx_bias,
        h_bias,
        up_bias,
        down_bias,
        ema_flat,
    ) = parts
    gains = gains.reshape(2, D)
    shifts = shifts.reshape(2, D)
    affine = affine.reshape(4, Z)
    sequence_length = inputs_row.shape[0]
    blocks = sequence_length // STRETCH
    row_float = inputs_row.astype(jnp.float32)
    (normed, mixed), pull_first = jax.vjp(
        partial(first_piece, valid),
        row_float,
        gains[0],
        shifts[0],
        omega_scale,
        ema_flat.reshape(4, D, H),
    )
    normed_low = normed.astype(jnp.bfloat16)
    mixed_low = mixed.astype(jnp.bfloat16)
    values_mm = jnp.dot(normed_low, v_full, preferred_element_type=jnp.float32)
    base_mm = jnp.dot(mixed_low, mx_full, preferred_element_type=jnp.float32)
    (values, update, reset, hidden_x, query, keys_float), pull_second = jax.vjp(
        second_piece, values_mm, v_bias, base_mm, mx_bias, affine
    )
    query_low = query.astype(jnp.bfloat16).reshape(blocks, STRETCH, Z)
    keys_low = keys_float.astype(jnp.bfloat16).reshape(blocks, STRETCH, Z)
    values_reduced = values.astype(jnp.bfloat16).reshape(blocks, STRETCH, VALUE_WIDTH)
    raw_scores = jnp.einsum("nqz,nkz->nqk", query_low, keys_low, preferred_element_type=jnp.float32)
    softmax_probs, pull_third = jax.vjp(attention_weights, raw_scores, relative)
    softmax_probs_reduced = softmax_probs.astype(jnp.bfloat16)
    attended_values = jnp.einsum(
        "dug,dgl->dul", softmax_probs_reduced, values_reduced, preferred_element_type=jnp.float32
    ).reshape(sequence_length, VALUE_WIDTH)
    gated_low = (attended_values * reset).astype(jnp.bfloat16)
    hidden_mm = jnp.dot(gated_low, h_full, preferred_element_type=jnp.float32)
    (first, second), pull_fifth = jax.vjp(
        partial(fifth_piece, valid),
        hidden_mm,
        hidden_x,
        h_bias,
        update,
        row_float,
        gains[1],
        shifts[1],
    )
    second_low = second.astype(jnp.bfloat16)
    up_mm = jnp.dot(second_low, up_full, preferred_element_type=jnp.float32)
    inner, pull_sixth = jax.vjp(activate, up_mm, up_bias)
    inner_low = inner.astype(jnp.bfloat16)
    down_mm = jnp.dot(inner_low, down_full, preferred_element_type=jnp.float32)
    result = (first + valid * (down_mm + down_bias)).astype(jnp.bfloat16)
    kept = (
        valid,
        normed_low,
        mixed_low,
        query_low,
        keys_low,
        values_reduced,
        softmax_probs_reduced,
        attended_values,
        reset,
        gated_low,
        second_low,
        inner_low,
        pull_first,
        pull_second,
        pull_third,
        pull_fifth,
        pull_sixth,
    )
    return (result, kept)


def backward_rows(kept, cot_row, weights):
    v_full, mx_full, h_full, up_full, down_full, small_full = weights
    (
        valid,
        normed_low,
        mixed_low,
        query_low,
        keys_low,
        values_reduced,
        softmax_probs_reduced,
        attended_values,
        reset,
        gated_low,
        second_low,
        inner_low,
        pull_first,
        pull_second,
        pull_third,
        pull_fifth,
        pull_sixth,
    ) = kept
    sequence_length = cot_row.shape[0]
    blocks = sequence_length // STRETCH
    grad_out = cot_row.astype(jnp.float32)
    down_grad = valid * grad_out
    down_bias_grad = jnp.sum(down_grad, axis=0)
    down_low = down_grad.astype(jnp.bfloat16)
    down_weight_grad = jnp.einsum(
        "ti,td->id", inner_low, down_low, preferred_element_type=jnp.float32
    )
    inner_grad = jnp.einsum("td,id->ti", down_low, down_full, preferred_element_type=jnp.float32)
    up_grad, up_bias_grad = pull_sixth(inner_grad)
    up_low = up_grad.astype(jnp.bfloat16)
    up_weight_grad = jnp.einsum("td,tf->df", second_low, up_low, preferred_element_type=jnp.float32)
    second_grad = jnp.einsum("tf,df->td", up_low, up_full, preferred_element_type=jnp.float32)
    (
        hidden_mm_grad,
        hidden_x_grad,
        h_bias_grad,
        update_grad,
        row_grad_first,
        gain_two_grad,
        shift_two_grad,
    ) = pull_fifth((grad_out, second_grad))
    hidden_low = hidden_mm_grad.astype(jnp.bfloat16)
    h_weight_grad = jnp.einsum(
        "tv,td->vd", gated_low, hidden_low, preferred_element_type=jnp.float32
    )
    gated_grad = jnp.einsum("td,vd->tv", hidden_low, h_full, preferred_element_type=jnp.float32)
    attended_values_reduced = (
        (gated_grad * reset).astype(jnp.bfloat16).reshape(blocks, STRETCH, VALUE_WIDTH)
    )
    reset_grad = gated_grad * attended_values
    soft_grad = jnp.einsum(
        "uoz,ufz->uof", attended_values_reduced, values_reduced, preferred_element_type=jnp.float32
    )
    values_grad = jnp.einsum(
        "mul,mur->mlr",
        softmax_probs_reduced,
        attended_values_reduced,
        preferred_element_type=jnp.float32,
    ).reshape(sequence_length, VALUE_WIDTH)
    raw_grad, relative_grad = pull_third(soft_grad)
    raw_low = raw_grad.astype(jnp.bfloat16)
    query_grad = jnp.einsum(
        "nqk,nkz->nqz", raw_low, keys_low, preferred_element_type=jnp.float32
    ).reshape(sequence_length, Z)
    keys_grad = jnp.einsum(
        "nqk,nqz->nkz", raw_low, query_low, preferred_element_type=jnp.float32
    ).reshape(sequence_length, Z)
    values_mm_grad, v_bias_grad, base_mm_grad, mx_bias_grad, affine_grad = pull_second(
        (values_grad, update_grad, reset_grad, hidden_x_grad, query_grad, keys_grad)
    )
    base_low = base_mm_grad.astype(jnp.bfloat16)
    mx_weight_grad = jnp.einsum(
        "td,te->de", mixed_low, base_low, preferred_element_type=jnp.float32
    )
    mixed_grad = jnp.einsum("te,de->td", base_low, mx_full, preferred_element_type=jnp.float32)
    values_mm_low = values_mm_grad.astype(jnp.bfloat16)
    v_weight_grad = jnp.einsum(
        "td,tv->dv", normed_low, values_mm_low, preferred_element_type=jnp.float32
    )
    normed_grad = jnp.einsum("tv,dv->td", values_mm_low, v_full, preferred_element_type=jnp.float32)
    row_grad_second, gain_one_grad, shift_one_grad, omega_grad, ema_grad = pull_first(
        (normed_grad, mixed_grad)
    )
    grad_row = (row_grad_first + row_grad_second).astype(jnp.bfloat16)
    small_grad = jnp.concatenate(
        [
            gain_one_grad,
            gain_two_grad,
            shift_one_grad,
            shift_two_grad,
            omega_grad,
            affine_grad.reshape(-1),
            relative_grad,
            v_bias_grad,
            mx_bias_grad,
            h_bias_grad,
            up_bias_grad,
            down_bias_grad,
            ema_grad.reshape(-1),
        ]
    )
    return (
        (
            v_weight_grad,
            mx_weight_grad,
            h_weight_grad,
            up_weight_grad,
            down_weight_grad,
            small_grad,
        ),
        grad_row,
    )


def per_device(
    inputs, lengths, cotangent, v_weight, mx_weight, h_weight, up_weight, down_weight, small_params
):
    sequence_length = inputs.shape[2]
    positions = jnp.arange(sequence_length)
    totals = None
    results_all = []
    grads_all = []
    for micro in range(inputs.shape[0]):
        gathered = (
            lax.all_gather(v_weight, "fsdp", axis=0, tiled=True),
            lax.all_gather(mx_weight, "fsdp", axis=0, tiled=True),
            lax.all_gather(h_weight, "fsdp", axis=0, tiled=True),
            lax.all_gather(up_weight, "fsdp", axis=0, tiled=True),
            lax.all_gather(down_weight, "fsdp", axis=0, tiled=True),
            lax.all_gather(small_params, "fsdp", axis=0, tiled=True),
        )
        member = 0
        valid = (positions < lengths[micro, member]).astype(jnp.float32)[:, None]
        result, kept = forward_rows(inputs[micro, member], valid, gathered)
        results_micro = [result]
        saved = [kept]
        local_grads = None
        member = 0
        member_grads, grad_row = backward_rows(saved[member], cotangent[micro, member], gathered)
        grads_micro = [grad_row]
        local_grads = member_grads
        if totals is None:
            totals = local_grads
        else:
            totals = jax.tree.map(jnp.add, totals, local_grads)
        results_all.append(jnp.stack(results_micro))
        grads_all.append(jnp.stack(grads_micro))
    totals = (
        lax.psum_scatter(totals[0], "fsdp", scatter_dimension=0, tiled=True),
        lax.psum_scatter(totals[1], "fsdp", scatter_dimension=0, tiled=True),
        lax.psum_scatter(totals[2], "fsdp", scatter_dimension=0, tiled=True),
        lax.psum_scatter(totals[3], "fsdp", scatter_dimension=0, tiled=True),
        lax.psum_scatter(totals[4], "fsdp", scatter_dimension=0, tiled=True),
        lax.psum_scatter(totals[5], "fsdp", scatter_dimension=0, tiled=True),
    )
    return (
        jnp.stack(results_all),
        jnp.stack(grads_all),
        totals[0],
        totals[1],
        totals[2],
        totals[3],
        totals[4],
        totals[5],
    )


def solution(mesh):
    return jax.shard_map(
        per_device,
        mesh=mesh,
        in_specs=(
            P(None, "fsdp", None, None),
            P(None, "fsdp"),
            P(None, "fsdp", None, None),
            P("fsdp", None),
            P("fsdp", None),
            P("fsdp", None),
            P("fsdp", None),
            P("fsdp", None),
            P("fsdp"),
        ),
        out_specs=(
            P(None, "fsdp", None, None),
            P(None, "fsdp", None, None),
            P("fsdp", None),
            P("fsdp", None),
            P("fsdp", None),
            P("fsdp", None),
            P("fsdp", None),
            P("fsdp"),
        ),
        check_vma=False,
    )
```

profile of v0, /device:TPU:0, one launch (start us, length us, event | category | flops | bytes accessed | tf_op | source)
XLA Modules:
  0.0 2227.6 jit_solution(15572725691559503051)
XLA Ops:
  24.0 114.7 %all-reduce.39.cloned.1.call-done = bf16[83712]{0:T(1024)(128)(2,1)} async-done(((bf16[83712]{0:T(1024)(128)(2,1)}), bf16[83712]{0:T(1024)(128)(2,1)}) %all-reduce.39.cloned.1.call-update) | async-done | bytes 167440
  242.4 17.7 convolution_bitcast_fusion.3
  272.1 30.2 %fusion.237 = f32[1024,4,32]{2,1,0:T(4,128)S(1)} fusion(f32[1024,32,32]{2,1,0:T(8,128)} %copy.243, f32[4,32,1024]{1,0,2:T(4,128)S(1)} %copy.180, f32[4,32]{1,0:T(4,128)S(1)} %copy-done.129, f32[1024]{0:T(1024)S(1)} %get-tuple-element.757, f32[1024]{0:T(1024)S(1)} %get-tuple-element.716, f32[4,32]{1,0:T(4,128)S(1)} %rsqrt.49, f32[4,32]{1,0:T(4,128)S(1)} %div.191), kind=kOutput, calls=%fused_computation.451 | convolution fusion | flops 50987008 | bytes 5252608 | tf_op jit(solution)/shard_map/jvp(cts,nsc->ntc)/dot_general | solution.py:67
  353.6 74.2 %all-gather.12.cloned.1.call-done = bf16[1024,4096]{1,0:T(8,128)(2,1)} async-done(((bf16[32,4096]{1,0:T(8,128)(2,1)}), bf16[1024,4096]{1,0:T(8,128)(2,1)}) %all-gather.12.cloned.1.call-update) | async-done | bytes 8388624 | tf_op jit(solution)/shard_map/all_gather | solution.py:345
  433.8 72.7 %all-gather.14.cloned.1.call-done = bf16[4096,1024]{1,0:T(8,128)(2,1)} async-done(((bf16[128,1024]{1,0:T(8,128)(2,1)}), bf16[4096,1024]{1,0:T(8,128)(2,1)}) %all-gather.14.cloned.1.call-update) | async-done | bytes 8388624 | tf_op jit(solution)/shard_map/all_gather | solution.py:346
  531.4 22.7 %fusion.66 = (f32[1024,16]{1,0:T(8,128)}, f32[4,1024,16]{2,0,1:T(4,128)}) fusion(f32[4,1024,16]{2,0,1:T(4,128)} %copy.186, f32[1024,16]{1,0:T(8,128)} %copy-done.87, f32[1024,16]{1,0:T(8,128)} %get-tuple-element.700, f32[1024,16]{1,0:T(8,128)} %copy-done.91, f32[32]{0:T(128)} %iota_convert_fusion, f32[4,32,1024]{1,0,2:T(4,128)} %copy.196), kind=kOutput, calls=%fused_computation.101 | convolution fusion | flops 26394624 | bytes 1310848 | tf_op jit(solution)/shard_map/transpose(jvp(nch,tch->ntc))/dot_general | solution.py:75
  576.3 17.2 add_bitcast_fusion.1
  603.7 30.3 %fusion.238 = f32[1024,4,32]{2,1,0:T(4,128)} fusion(f32[1024,32,32]{2,1,0:T(8,128)} %copy.243, f32[4,32,1024]{1,0,2:T(4,128)} %copy.190, f32[4,32]{1,0:T(4,128)S(1)} %copy-done.132, f32[4,32]{1,0:T(4,128)S(1)} %rsqrt.52, f32[4,32]{1,0:T(4,128)S(1)} %copy-done.127, f32[1024]{0:T(1024)S(1)} %get-tuple-element.757, f32[1024]{0:T(1024)S(1)} %get-tuple-element.716), kind=kOutput, calls=%fused_computation.452 | convolution fusion | flops 50987008 | bytes 5252608 | tf_op jit(solution)/shard_map/jvp(cts,nsc->ntc)/dot_general | solution.py:67
  634.0 18.1 convolution_bitcast_fusion.2
  659.8 32.7 %fusion.62 = f32[1024,32,32]{2,1,0:T(8,128)} fusion(f32[4,32,1024]{1,0,2:T(4,128)S(1)} %copy-done.6, f32[4,32,1024]{1,0,2:T(4,128)S(1)} %copy.180, f32[4,32]{1,0:T(4,128)S(1)} %copy-done.130, f32[1024]{0:T(1024)S(1)} %get-tuple-element.757, f32[1024]{0:T(1024)S(1)} %get-tuple-element.716, f32[4,32]{1,0:T(4,128)S(1)} %copy-done.125, f32[4,32]{1,0:T(4,128)S(1)} %copy-done.122), kind=kOutput, calls=%fused_computation.95 | convolution fusion | flops 50987008 | bytes 5252608 | tf_op jit(solution)/shard_map/transpose(jvp(cts,nsc->ntc))/dot_general | solution.py:67
  761.9 22.8 %fusion.58 = (f32[1024,16]{1,0:T(8,128)}, f32[4,1024,16]{2,0,1:T(4,128)}) fusion(f32[4,1024,16]{2,0,1:T(4,128)} %copy.193, f32[1024,16]{1,0:T(8,128)} %copy-done.87, f32[1024,16]{1,0:T(8,128)} %get-tuple-element.700, f32[1024,16]{1,0:T(8,128)} %copy-done.91, f32[32]{0:T(128)S(1)} %copy-done.226, f32[4,32,1024]{1,0,2:T(4,128)} %copy.202), kind=kOutput, calls=%fused_computation.91 | convolution fusion | flops 26394624 | bytes 1310848 | tf_op jit(solution)/shard_map/transpose(jvp(nch,tch->ntc))/dot_general | solution.py:75
  784.8 32.5 %fusion.54 = f32[1024,32,32]{2,1,0:T(8,128)} fusion(f32[4,32,1024]{1,0,2:T(4,128)S(1)} %copy-done.8, f32[4,32,1024]{1,0,2:T(4,128)S(1)} %copy-done.2, f32[4,32]{1,0:T(4,128)S(1)} %copy-done.133, f32[4,32]{1,0:T(4,128)S(1)} %copy-done.135, f32[4,32]{1,0:T(4,128)S(1)} %copy-done.128, f32[1024]{0:T(1024)S(1)} %get-tuple-element.757, ...), kind=kOutput, calls=%fused_computation.85 | convolution fusion | flops 50987008 | bytes 5252608 | tf_op jit(solution)/shard_map/transpose(jvp(cts,nsc->ntc))/dot_general | solution.py:67
  841.0 19.0 convolution_bitcast_fusion
  876.0 19.1 convolution_bitcast_fusion.1
  897.4 17.1 add_bitcast_fusion
  941.2 16.5 reshape.751
  1002.8 16.5 reshape.752
  1139.1 43.5 %fusion.4 = (f32[1024,16]{1,0:T(8,128)S(1)}, f32[1024,16]{1,0:T(8,128)S(1)}, f32[1024,16]{1,0:T(8,128)S(1)}, f32[1024,16]{1,0:T(8,128)S(1)}) fusion(f32[32,1024,16]{0,2,1:T(8,128)} %rev.25, f32[1,1024,16]{0,2,1:T(8,128)} %copy.225, f32[1024,32]{1,0:T(8,128)S(1)} %copy-done.110, f32[1024,16]{1,0:T(8,128)S(1)} %copy-done.90, f32[1024,16]{1,0:T(8,128)S(1)} %copy-done.37, ...), kind=kOutput, calls=%fused_computation.18 | convolution fusion | flops 36175872 | bytes 7929984 | tf_op jit(solution)/shard_map/transpose(jvp(nch,tch->ntc))/dot_general | solution.py:75
  1307.9 41.4 %all-reduce.41.cloned.1.call-done = f32[83712]{0:T(1024)} async-done(((f32[83712]{0:T(1024)}), f32[83712]{0:T(1024)}) %all-reduce.41.cloned.1.call-update) | async-done | bytes 334864
  1350.7 151.1 %reduce-scatter.6.cloned.1.call-done = f32[32,2048]{1,0:T(8,128)} async-done(((f32[1024,2048]{1,0:T(8,128)}), f32[32,2048]{1,0:T(8,128)}) %reduce-scatter.6.cloned.1.call-update) | async-done | bytes 262160 | tf_op jit(solution)/shard_map/reduce_scatter | solution.py:366
  1501.8 147.5 %reduce-scatter.10.cloned.1.call-done = f32[64,1024]{1,0:T(8,128)} async-done(((f32[2048,1024]{1,0:T(8,128)}), f32[64,1024]{1,0:T(8,128)}) %reduce-scatter.10.cloned.1.call-update) | async-done | bytes 262160 | tf_op jit(solution)/shard_map/reduce_scatter | solution.py:368
  1649.3 199.1 %reduce-scatter.8.cloned.1.call-done = f32[32,4224]{1,0:T(8,128)} async-done(((f32[1024,4224]{1,0:T(8,128)}), f32[32,4224]{1,0:T(8,128)}) %reduce-scatter.8.cloned.1.call-update) | async-done | bytes 540688 | tf_op jit(solution)/shard_map/reduce_scatter | solution.py:367
  1848.4 184.8 %reduce-scatter.12.cloned.1.call-done = f32[32,4096]{1,0:T(8,128)} async-done(((f32[1024,4096]{1,0:T(8,128)}), f32[32,4096]{1,0:T(8,128)}) %reduce-scatter.12.cloned.1.call-update) | async-done | bytes 524304 | tf_op jit(solution)/shard_map/reduce_scatter | solution.py:369
  2033.2 187.3 %reduce-scatter.14.cloned.1.call-done = f32[128,1024]{1,0:T(8,128)} async-done(((f32[4096,1024]{1,0:T(8,128)}), f32[128,1024]{1,0:T(8,128)}) %reduce-scatter.14.cloned.1.call-update) | async-done | bytes 524304 | tf_op jit(solution)/shard_map/reduce_scatter | solution.py:370
  (792 shorter events, 706.6 us)
Async XLA Ops:
  7.2 131.5 %all-reduce.39.cloned.1.call-start = ((), (), s32[]{:S(2)}) async-start(), calls=%async_computation.15 | async-start | bytes 335872
  8.8 321.0 %all-gather.8.cloned.1.call-start = ((), (), s32[]{:S(2)}) async-start(), calls=%async_computation.6 | async-start | bytes 4325376 | tf_op jit(solution)/shard_map/all_gather | solution.py:342
  9.6 324.6 %all-gather.6.cloned.1.call-start = ((), (), s32[]{:S(2)}) async-start(), calls=%async_computation.5 | async-start | bytes 8921088 | tf_op jit(solution)/shard_map/all_gather | solution.py:343
  10.3 338.6 %all-gather.10.cloned.1.call-start = ((), (), s32[]{:S(2)}) async-start(), calls=%async_computation.7 | async-start | bytes 4325376 | tf_op jit(solution)/shard_map/all_gather | solution.py:344
  10.9 416.8 %all-gather.12.cloned.1.call-start = ((), (), s32[]{:S(2)}) async-start(), calls=%async_computation.8 | async-start | bytes 8650752 | tf_op jit(solution)/shard_map/all_gather | solution.py:345
  11.5 495.0 %all-gather.14.cloned.1.call-start = ((), (), s32[]{:S(2)}) async-start(), calls=%async_computation.9 | async-start | bytes 8650752 | tf_op jit(solution)/shard_map/all_gather | solution.py:346
  12.1 1337.3 %all-reduce.41.cloned.1.call-start = ((), (), s32[]{:S(2)}) async-start(), calls=%async_computation.16 | async-start | bytes 671744
  16.1 129.2 %copy-start.141 = (f32[128]{0:T(128)}, f32[128]{0:T(128)S(1)}, u32[]{:S(2)}) copy-start(f32[128]{0:T(128)S(1)} %get-tuple-element.760) | copy-start | bytes 1540
  16.2 255.8 %copy-start.121 = (f32[4,32]{1,0:T(4,128)}, f32[4,32]{1,0:T(4,128)S(1)}, u32[]{:S(2)}) copy-start(f32[4,32]{1,0:T(4,128)S(1)} %div.191) | copy-start | bytes 1540
  16.5 255.5 %copy-start.124 = (f32[4,32]{1,0:T(4,128)}, f32[4,32]{1,0:T(4,128)S(1)}, u32[]{:S(2)}) copy-start(f32[4,32]{1,0:T(4,128)S(1)} %rsqrt.49) | copy-start | bytes 1540
  242.4 492.6 %copy-start.99 = (f32[1024]{0:T(1024)}, f32[1024]{0:T(1024)S(1)}, u32[]{:S(2)}) copy-start(f32[1024]{0:T(1024)S(1)} %get-tuple-element.758) | copy-start | bytes 12292
  242.4 508.0 %copy-start.97 = (f32[1024]{0:T(1024)}, f32[1024]{0:T(1024)S(1)}, u32[]{:S(2)}) copy-start(f32[1024]{0:T(1024)S(1)} %get-tuple-element.715) | copy-start | bytes 12292
  341.0 181.6 %copy-start.166 = (f32[128]{0:T(128)}, f32[128]{0:T(128)S(1)}, u32[]{:S(2)}) copy-start(f32[128]{0:T(128)S(1)} %get-tuple-element.729) | copy-start | bytes 1540
  341.1 181.5 %copy-start.197 = (f32[128]{0:T(128)}, f32[128]{0:T(128)S(1)}, u32[]{:S(2)}) copy-start(f32[128]{0:T(128)S(1)} %fusion.196) | copy-start | bytes 1540
  353.3 164.8 %copy-start.18 = (f32[128,1024]{1,0:T(8,128)}, f32[128,1024]{1,0:T(8,128)S(1)}, u32[]{:S(2)}) copy-start(f32[128,1024]{1,0:T(8,128)S(1)} %get-tuple-element.660) | copy-start | bytes 1572868
  353.3 164.8 %copy-start.156 = (f32[128]{0:T(128)}, f32[128]{0:T(128)S(1)}, u32[]{:S(2)}) copy-start(f32[128]{0:T(128)S(1)} %broadcast_multiply_fusion.2) | copy-start | bytes 1540
  353.5 164.6 %copy-start.168 = (f32[128]{0:T(128)}, f32[128]{0:T(128)S(1)}, u32[]{:S(2)}) copy-start(f32[128]{0:T(128)S(1)} %fusion.207) | copy-start | bytes 1540
  519.7 137.7 %copy-start.23 = (f32[128,1024]{1,0:T(8,128)}, f32[128,1024]{1,0:T(8,128)S(1)}, u32[]{:S(2)}) copy-start(f32[128,1024]{1,0:T(8,128)S(1)} %get-tuple-element.694) | copy-start | bytes 1572868
  924.8 262.8 %copy-start.211 = (f32[128]{0:T(128)}, f32[128]{0:T(128)S(1)}, u32[]{:S(2)}) copy-start(f32[128]{0:T(128)S(1)} %multiply_multiply_fusion.3) | copy-start | bytes 1540
  1225.0 276.8 %reduce-scatter.6.cloned.1.call-start = ((), (), s32[]{:S(2)}) async-start(), calls=%async_computation.10 | async-start | bytes 8650752 | tf_op jit(solution)/shard_map/reduce_scatter | solution.py:366
  1233.1 416.2 %reduce-scatter.10.cloned.1.call-start = ((), (), s32[]{:S(2)}) async-start(), calls=%async_computation.12 | async-start | bytes 8650752 | tf_op jit(solution)/shard_map/reduce_scatter | solution.py:368
  1240.2 608.2 %reduce-scatter.8.cloned.1.call-start = ((), (), s32[]{:S(2)}) async-start(), calls=%async_computation.11 | async-start | bytes 17842176 | tf_op jit(solution)/shard_map/reduce_scatter | solution.py:367
  1265.6 767.7 %reduce-scatter.12.cloned.1.call-start = ((), (), s32[]{:S(2)}) async-start(), calls=%async_computation.13 | async-start | bytes 17301504 | tf_op jit(solution)/shard_map/reduce_scatter | solution.py:369
  1278.7 941.8 %reduce-scatter.14.cloned.1.call-start = ((), (), s32[]{:S(2)}) async-start(), calls=%async_computation.14 | async-start | bytes 17301504 | tf_op jit(solution)/shard_map/reduce_scatter | solution.py:370
  (232 other events, 2496.8 us)
Sparse Core Ops, SparseCore 0:
  14.1 124.5 all-reduce.38
  141.5 64.0 all-gather.7
  208.5 77.0 all-gather.5
  288.3 60.6 all-gather.9
  351.7 75.9 all-gather.11
  430.4 76.0 all-gather.13
  1225.1 124.1 all-reduce.40
  1352.3 149.4 reduce-scatter.5
  1504.8 144.5 reduce-scatter.9
  1657.3 191.0 reduce-scatter.7
  1851.4 181.7 reduce-scatter.11
  2036.0 184.4 reduce-scatter.13
where the time goes:
time: 2240 us; the launch traced here: 2230 us
  waiting for transfers between devices  1180 us (53%)
  matrix products  603 us (27%)
  local copies, waits for them, and re-layouts  337 us (15%)
  other arithmetic  87.4 us (4%)
    reduce_scatter x1, waiting for transfers between devices, per_device(): lax.psum_scatter(totals[1], 'fsdp', scatter_dimension=0, tiled=True)  199 us
    reduce_scatter x1, waiting for transfers between devices, per_device(): lax.psum_scatter(totals[4], 'fsdp', scatter_dimension=0, tiled=True)  187 us
    reduce_scatter x1, waiting for transfers between devices, per_device(): lax.psum_scatter(totals[3], 'fsdp', scatter_dimension=0, tiled=True)  185 us
    dot_general x6, matrix products, smooth_signal(): jnp.einsum('cts,nsc->ntc', toeplitz, blocks, precision=highest_precision)  160 us
    unnamed x14, waiting for transfers between devices  159 us
    reduce_scatter x1, waiting for transfers between devices, per_device(): lax.psum_scatter(totals[0], 'fsdp', scatter_dimension=0, tiled=True)  151 us
    reduce_scatter x1, waiting for transfers between devices, per_device(): lax.psum_scatter(totals[2], 'fsdp', scatter_dimension=0, tiled=True)  148 us
    dot_general x6, matrix products, smooth_signal(): jnp.einsum('nch,tch->ntc', starts * weight, powers * retain[None], precis...  134 us
  transfers between devices with their start and end apart: 12, of which 10 were waited for; matrix products, arithmetic and copies ran while one was open for 13% of the time, Pallas kernels for 0%

commit v1 on v0

--- a/solution.py
+++ b/solution.py
@@ -1,9 +1,12 @@
+import functools
 from functools import partial
 import math
 
 import jax
 import jax.numpy as jnp
 from jax import lax
+from jax.experimental import pallas as pl
+from jax.experimental.pallas import tpu as pltpu
 from jax.sharding import PartitionSpec as P
 
 D = 1024
@@ -16,6 +19,161 @@
 
 epsilon = 1e-05
 highest_precision = lax.Precision.HIGHEST
+
+
+MESH = pl.DeviceIdType.MESH
+
+class Place:
+    def __init__(self, dims):
+        self.Z, self.Y, self.X = dims
+        me = lax.axis_index("fsdp")
+        self.me = me
+        self.c = me % 2
+        self.x = (me // 2) % self.X
+        self.y = (me // (2 * self.X)) % self.Y
+        self.z = me // (2 * self.X * self.Y)
+        self.nx = self.dev(self.z, self.y, 1 - self.x, self.c)
+        self.ny = self.dev(self.z, 1 - self.y, self.x, self.c)
+        self.nc = self.dev(self.z, self.y, self.x, 1 - self.c)
+        self.has_down = self.z > 0
+        self.has_up = self.z < self.Z - 1
+        self.down = self.dev(jnp.maximum(self.z - 1, 0), self.y, self.x, self.c)
+        self.up = self.dev(jnp.minimum(self.z + 1, self.Z - 1), self.y, self.x, self.c)
+    def dev(self, z, y, x, c):
+        return ((z * self.Y + y) * self.X + x) * 2 + c
+    def barrier(self):
+        bar = pltpu.get_barrier_semaphore()
+        def tell(d):
+            pl.semaphore_signal(bar, inc=1, device_id=(d,), device_id_type=MESH)
+        for d in (self.nx, self.ny, self.nc):
+            tell(d)
+        pl.when(self.has_down)(lambda: tell(self.down))
+        pl.when(self.has_up)(lambda: tell(self.up))
+        pl.semaphore_wait(bar, 3 + jnp.where(self.has_down, 1, 0) + jnp.where(self.has_up, 1, 0))
+
+def when(cond, f):
+    if cond is None: f()
+    else: pl.when(cond)(f)
+
+class Gather:
+    def __init__(self, place, ins, outs, send_sem, recv_sem):
+        self.p, self.ins, self.outs = place, ins, outs
+        self.ss, self.rs = send_sem, recv_sem
+        self.ids, self.pend = {}, []
+    def rows(self, k, h):
+        n = self.ins[k].shape[0]
+        return (0, n) if h == 2 else (h * (n // 2), n // 2)
+    def copy(self, key, k, shard, h, to, own=False):
+        i = self.ids.setdefault((key, k), len(self.ids))
+        r, n = self.rows(k, h)
+        full = self.ins[k].shape[0]
+        dst = self.outs[k].at[pl.ds(shard * full + r, n)]
+        src = self.ins[k].at[pl.ds(r, n)] if own else dst
+        return pltpu.make_async_remote_copy(src_ref=src, dst_ref=dst, send_sem=self.ss.at[i], recv_sem=self.rs.at[i], device_id=(to,), device_id_type=MESH)
+    def send(self, cond, *a):
+        when(cond, lambda: self.copy(*a).start())
+        self.pend.append((cond, lambda: self.copy(*a).wait_send()))
+    def recv(self, cond, key, k, shard, h):
+        when(cond, lambda: self.copy(key, k, shard, h, self.p.me).wait_recv())
+    def col(self, o):
+        p = self.p
+        if o == 0: return None, p.z
+        if o > 0: return p.z - o >= 0, jnp.maximum(p.z - o, 0)
+        return p.z - o <= p.Z - 1, jnp.minimum(p.z - o, p.Z - 1)
+    def offs(self, s):
+        return (0,) if s == 0 else (s, -s)
+    def stage(self, k, s):
+        p = self.p
+        L = p.Z
+        if s < L:
+            for o in self.offs(s):
+                cond, zz = self.col(o)
+                sh = p.dev(zz, p.y, p.x, p.c)
+                own = o == 0
+                if not own:
+                    self.recv(cond, ("z", o), k, sh, 2)
+                if s + 1 < L:
+                    both = lambda c1: c1 if cond is None else jnp.logical_and(cond, c1)
+                    if o >= 0: self.send(both(p.has_up), ("z", s + 1), k, sh, 2, p.up, own)
+                    if o <= 0: self.send(both(p.has_down), ("z", -(s + 1)), k, sh, 2, p.down, own)
+                self.send(cond, ("x", o), k, sh, 2, p.nx, own)
+                self.send(cond, ("y", o), k, sh, 2, p.ny, own)
+                self.send(cond, ("c", o), k, sh, 2, p.nc, own)
+        if 1 <= s <= L:
+            for o in self.offs(s - 1):
+                cond, zz = self.col(o)
+                sx, sy = p.dev(zz, p.y, 1 - p.x, p.c), p.dev(zz, 1 - p.y, p.x, p.c)
+                self.recv(cond, ("x", o), k, sx, 2)
+                self.send(cond, ("xy", o), k, sx, 0, p.ny)
+                self.send(cond, ("cx", o), k, sx, 2, p.nc)
+                self.recv(cond, ("y", o), k, sy, 2)
+                self.send(cond, ("yx", o), k, sy, 1, p.nx)
+                self.send(cond, ("cy", o), k, sy, 2, p.nc)
+        if 2 <= s <= L + 1:
+            for o in self.offs(s - 2):
+                cond, zz = self.col(o)
+                sd = p.dev(zz, 1 - p.y, 1 - p.x, p.c)
+                self.recv(cond, ("xy", o), k, sd, 0)
+                self.recv(cond, ("yx", o), k, sd, 1)
+                self.send(cond, ("cd", o), k, sd, 2, p.nc)
+        if s == L + 2:
+            for t in range(L):
+                for o in self.offs(t):
+                    cond, zz = self.col(o)
+                    for key, yy, xx in (("c", p.y, p.x), ("cx", p.y, 1 - p.x), ("cy", 1 - p.y, p.x), ("cd", 1 - p.y, 1 - p.x)):
+                        self.recv(cond, (key, o), k, p.dev(zz, yy, xx, 1 - p.c), 2)
+    def stages(self):
+        return self.p.Z + 3
+    def finish(self):
+        for cond, f in self.pend:
+            when(cond, f)
+
+def sems_needed(dims, K):
+    Z = dims[0]
+    offs = 2 * Z - 1
+    return K * (2 * (Z - 1) + 8 * offs)
+
+def ag_kernel(dims, K, *refs):
+    ins, outs = refs[:K], refs[K:2 * K]
+    own, ss, rs = refs[2 * K:]
+    p = Place(dims)
+    p.barrier()
+    g = Gather(p, ins, outs, ss, rs)
+    cps = [pltpu.make_async_copy(ins[k], outs[k].at[pl.ds(p.me * ins[k].shape[0], ins[k].shape[0])], own.at[k]) for k in range(K)]
+    for cp in cps: cp.start()
+    S = g.stages()
+    for t in range(K + S - 1):
+        for k in range(K):
+            if 0 <= t - k < S: g.stage(k, t - k)
+    g.finish()
+    for cp in cps: cp.wait()
+
+def gather(dims, n, arrays, cid):
+    K = len(arrays)
+    ns = sems_needed(dims, K)
+    return pl.pallas_call(functools.partial(ag_kernel, dims, K),
+        out_shape=[jax.ShapeDtypeStruct((n * a.shape[0],) + a.shape[1:], a.dtype) for a in arrays],
+        in_specs=[pl.BlockSpec(memory_space=pl.ANY)] * K, out_specs=[pl.BlockSpec(memory_space=pl.ANY)] * K,
+        scratch_shapes=[pltpu.SemaphoreType.DMA((K,)), pltpu.SemaphoreType.DMA((ns,)), pltpu.SemaphoreType.DMA((ns,))],
+        compiler_params=pltpu.CompilerParams(collective_id=cid, has_side_effects=True))(*arrays)
+
+
+def grid_of(n):
+    chips = n // 2
+    return (chips // 4, 2, 2)
+
+
+def gather_all(n, weights, small):
+    if n != 32:
+        return tuple(lax.all_gather(w, "fsdp", axis=0, tiled=True) for w in weights + (small,))
+    dims = grid_of(n)
+    rows = -(-small.shape[0] // 128)
+    rows = -(-rows // 32) * 32
+    padded = jnp.pad(small, (0, rows * 128 - small.shape[0])).reshape(rows, 128)
+    (packed,) = gather(dims, n, (padded,), 0)
+    full = gather(dims, n, weights, 1)
+    flat = packed.reshape(n, rows * 128)[:, : small.shape[0]].reshape(-1)
+    return tuple(full) + (flat,)
 
 
 def split_vector(flat_vector):
@@ -330,22 +488,15 @@
 
 
 def per_device(
-    inputs, lengths, cotangent, v_weight, mx_weight, h_weight, up_weight, down_weight, small_params
+    n, inputs, lengths, cotangent, v_weight, mx_weight, h_weight, up_weight, down_weight, small_params
 ):
     sequence_length = inputs.shape[2]
     positions = jnp.arange(sequence_length)
+    gathered = gather_all(n, (v_weight, mx_weight, h_weight, up_weight, down_weight), small_params)
     totals = None
     results_all = []
     grads_all = []
     for micro in range(inputs.shape[0]):
-        gathered = (
-            lax.all_gather(v_weight, "fsdp", axis=0, tiled=True),
-            lax.all_gather(mx_weight, "fsdp", axis=0, tiled=True),
-            lax.all_gather(h_weight, "fsdp", axis=0, tiled=True),
-            lax.all_gather(up_weight, "fsdp", axis=0, tiled=True),
-            lax.all_gather(down_weight, "fsdp", axis=0, tiled=True),
-            lax.all_gather(small_params, "fsdp", axis=0, tiled=True),
-        )
         member = 0
         valid = (positions < lengths[micro, member]).astype(jnp.float32)[:, None]
         result, kept = forward_rows(inputs[micro, member], valid, gathered)
@@ -384,7 +535,7 @@
 
 def solution(mesh):
     return jax.shard_map(
-        per_device,
+        partial(per_device, mesh.shape["fsdp"]),
         mesh=mesh,
         in_specs=(
             P(None, "fsdp", None, None),

time: 2240 us -> 2100 us (0.938)
  waiting for transfers between devices: 1180 us -> 913 us
  Pallas kernels: 0 us -> 170 us
    pallas_call x0 -> x2, Pallas kernels: none -> 170 us  [gather(): pl.pallas_call(functools.partial(ag_kernel, dims, K), out_shape=[jax.Shap...]
    all_gather x5 -> x0, waiting for transfers between devices: 153 us -> none  [the longest x1 74.2 us: per_device(): lax.all_gather(up_weight, 'fsdp', axis=0, tiled=True)]
    unnamed x14 -> x7, waiting for transfers between devices: 159 us -> 43.5 us
    unnamed x519 -> x481, local copies, waits for them, and re-layouts: 67.1 us -> 63.1 us
  transfers between devices with their start and end apart: 12 -> 6, of which waited for: 10 -> 6; matrix products, arithmetic and copies ran while one was open for 13% -> 4% of each run, Pallas kernels for 0% -> 0%
where the time goes in v1:
time: 2100 us; the launch traced here: 2090 us
  waiting for transfers between devices  913 us (43%)
  matrix products  588 us (28%)
  local copies, waits for them, and re-layouts  325 us (15%)
  Pallas kernels  170 us (8%)
  other arithmetic  78.2 us (4%)
    reduce_scatter x1, waiting for transfers between devices, per_device(): lax.psum_scatter(totals[1], 'fsdp', scatter_dimension=0, tiled=True)  199 us
    reduce_scatter x1, waiting for transfers between devices, per_device(): lax.psum_scatter(totals[4], 'fsdp', scatter_dimension=0, tiled=True)  187 us
    reduce_scatter x1, waiting for transfers between devices, per_device(): lax.psum_scatter(totals[3], 'fsdp', scatter_dimension=0, tiled=True)  185 us
    pallas_call x2, Pallas kernels, gather(): pl.pallas_call(functools.partial(ag_kernel, dims, K), out_shape=[jax.Shap...  170 us
    dot_general x6, matrix products, smooth_signal(): jnp.einsum('cts,nsc->ntc', toeplitz, blocks, precision=highest_precision)  159 us
    reduce_scatter x1, waiting for transfers between devices, per_device(): lax.psum_scatter(totals[0], 'fsdp', scatter_dimension=0, tiled=True)  151 us
    reduce_scatter x1, waiting for transfers between devices, per_device(): lax.psum_scatter(totals[2], 'fsdp', scatter_dimension=0, tiled=True)  148 us
    dot_general x6, matrix products, smooth_signal(): jnp.einsum('nch,tch->ntc', starts * weight, powers * retain[None], precis...  129 us
  transfers between devices with their start and end apart: 6, of which 6 were waited for; matrix products, arithmetic and copies ran while one was open for 4% of the time, Pallas kernels for 0%

profile of v1, /device:TPU:0, one launch (start us, length us, event | category | flops | bytes accessed | tf_op | source)
XLA Modules:
  0.0 2091.9 jit_solution(5581829769187610855)
XLA Ops:
  8.5 21.7 %shard_map.152 = bf16[1024,128]{1,0:T(8,128)(2,1)} custom-call(bf16[32,128]{1,0:T(8,128)(2,1)} %pad_bitcast_fusion.refs_0_), custom_call_target="tpu_custom_call" | custom-call | tf_op jit(solution)/shard_map/pallas_call | solution.py:154
  139.9 17.7 convolution_bitcast_fusion.3
  169.6 30.3 %fusion.237 = f32[1024,4,32]{2,1,0:T(4,128)S(1)} fusion(f32[1024,32,32]{2,1,0:T(8,128)} %copy.243, f32[4,32,1024]{1,0,2:T(4,128)S(1)} %copy.180, f32[4,32]{1,0:T(4,128)S(1)} %copy-done.115, f32[1024]{0:T(1024)S(1)} %get-tuple-element.760, f32[1024]{0:T(1024)S(1)} %get-tuple-element.719, f32[4,32]{1,0:T(4,128)S(1)} %copy-done.120, f32[4,32]{1,0:T(4,128)S(1)} %copy-done.112), kind=kOutput, calls=%fused_computation.455 | convolution fusion | flops 50987008 | bytes 5252608 | tf_op jit(solution)/shard_map/jvp(cts,nsc->ntc)/dot_general | solution.py:225
  219.1 148.7 %shard_map.153 = (bf16[1024,2048]{1,0:T(8,128)(2,1)}, bf16[1024,4224]{1,0:T(8,128)(2,1)}, bf16[2048,1024]{1,0:T(8,128)(2,1)}, bf16[1024,4096]{1,0:T(8,128)(2,1)}, bf16[4096,1024]{1,0:T(8,128)(2,1)}) custom-call(bf16[32,2048]{1,0:T(8,128)(2,1)} %refs_0_.1, bf16[32,4224]{1,0:T(8,128)(2,1)} %refs_1_.1, bf16[64,1024]{1,0:T(8,128)(2,1)} %refs_2_.1, ...), custom_call_target="tpu_custom_call" | custom-call | tf_op jit(solution)/shard_map/pallas_call | solution.py:154
  416.9 22.7 %fusion.66 = (f32[1024,16]{1,0:T(8,128)}, f32[4,1024,16]{2,0,1:T(4,128)}) fusion(f32[4,1024,16]{2,0,1:T(4,128)} %copy.186, f32[1024,16]{1,0:T(8,128)} %copy-done.70, f32[1024,16]{1,0:T(8,128)} %copy-done.33, f32[1024,16]{1,0:T(8,128)} %copy-done.67, f32[32]{0:T(128)} %copy-done.200, f32[4,32,1024]{1,0,2:T(4,128)} %copy.196), kind=kOutput, calls=%fused_computation.101 | convolution fusion | flops 26394624 | bytes 1310848 | tf_op jit(solution)/shard_map/transpose(jvp(nch,tch->ntc))/dot_general | solution.py:233
  461.8 16.9 add_bitcast_fusion.1
  493.3 30.3 %fusion.238 = f32[1024,4,32]{2,1,0:T(4,128)} fusion(f32[1024,32,32]{2,1,0:T(8,128)} %copy.243, f32[4,32,1024]{1,0,2:T(4,128)} %copy.190, f32[4,32]{1,0:T(4,128)S(1)} %copy-done.118, f32[4,32]{1,0:T(4,128)S(1)} %rsqrt.52, f32[4,32]{1,0:T(4,128)S(1)} %div.206, f32[1024]{0:T(1024)S(1)} %get-tuple-element.760, f32[1024]{0:T(1024)S(1)} %get-tuple-element.719), kind=kOutput, calls=%fused_computation.456 | convolution fusion | flops 50987008 | bytes 5252608 | tf_op jit(solution)/shard_map/jvp(cts,nsc->ntc)/dot_general | solution.py:225
  523.6 18.0 convolution_bitcast_fusion.2
  546.7 32.5 %fusion.62 = f32[1024,32,32]{2,1,0:T(8,128)} fusion(f32[4,32,1024]{1,0,2:T(4,128)S(1)} %copy-done.5, f32[4,32,1024]{1,0,2:T(4,128)S(1)} %copy.180, f32[4,32]{1,0:T(4,128)S(1)} %copy-done.116, f32[1024]{0:T(1024)S(1)} %get-tuple-element.760, f32[1024]{0:T(1024)S(1)} %get-tuple-element.719, f32[4,32]{1,0:T(4,128)S(1)} %copy-done.121, f32[4,32]{1,0:T(4,128)S(1)} %copy-done.113), kind=kOutput, calls=%fused_computation.95 | convolution fusion | flops 50987008 | bytes 5252608 | tf_op jit(solution)/shard_map/transpose(jvp(cts,nsc->ntc))/dot_general | solution.py:225
  647.4 22.8 %fusion.58 = (f32[1024,16]{1,0:T(8,128)}, f32[4,1024,16]{2,0,1:T(4,128)}) fusion(f32[4,1024,16]{2,0,1:T(4,128)} %copy.193, f32[1024,16]{1,0:T(8,128)} %copy-done.70, f32[1024,16]{1,0:T(8,128)} %copy-done.33, f32[1024,16]{1,0:T(8,128)} %copy-done.67, f32[32]{0:T(128)S(1)} %copy-done.202, f32[4,32,1024]{1,0,2:T(4,128)} %copy.202), kind=kOutput, calls=%fused_computation.91 | convolution fusion | flops 26394624 | bytes 1310848 | tf_op jit(solution)/shard_map/transpose(jvp(nch,tch->ntc))/dot_general | solution.py:233
  670.1 32.5 %fusion.54 = f32[1024,32,32]{2,1,0:T(8,128)} fusion(f32[4,32,1024]{1,0,2:T(4,128)S(1)} %copy-done.9, f32[4,32,1024]{1,0,2:T(4,128)S(1)} %copy-done.1, f32[4,32]{1,0:T(4,128)S(1)} %copy-done.119, f32[4,32]{1,0:T(4,128)S(1)} %copy-done.126, f32[4,32]{1,0:T(4,128)S(1)} %copy-done.124, f32[1024]{0:T(1024)S(1)} %get-tuple-element.760, ...), kind=kOutput, calls=%fused_computation.85 | convolution fusion | flops 50987008 | bytes 5252608 | tf_op jit(solution)/shard_map/transpose(jvp(cts,nsc->ntc))/dot_general | solution.py:225
  726.0 18.9 convolution_bitcast_fusion
  745.0 16.2 fusion.67
  761.2 19.0 convolution_bitcast_fusion.1
  782.6 17.0 add_bitcast_fusion
  824.0 16.5 reshape.738
  881.7 16.5 reshape.739
  988.9 38.9 %fusion.4 = (f32[1024,16]{1,0:T(8,128)S(1)}, f32[1024,16]{1,0:T(8,128)S(1)}, f32[1024,16]{1,0:T(8,128)S(1)}, f32[1024,16]{1,0:T(8,128)S(1)}) fusion(f32[32,1024,16]{0,2,1:T(8,128)} %rev.25, f32[1,1024,16]{0,2,1:T(8,128)} %copy.225, f32[1024,32]{1,0:T(8,128)} %copy.227, f32[1024,16]{1,0:T(8,128)} %copy-done.70, f32[1024,16]{1,0:T(8,128)} %copy-done.33, ...), kind=kOutput, calls=%fused_computation.18 | convolution fusion | flops 36175872 | bytes 7929984 | tf_op jit(solution)/shard_map/transpose(jvp(nch,tch->ntc))/dot_general | solution.py:233
  1170.5 43.4 %all-reduce.38.cloned.1.call-done = f32[83712]{0:T(1024)} async-done(((f32[83712]{0:T(1024)}), f32[83712]{0:T(1024)}) %all-reduce.38.cloned.1.call-update) | async-done | bytes 334864
  1215.2 151.1 %reduce-scatter.6.cloned.1.call-done = f32[32,2048]{1,0:T(8,128)} async-done(((f32[1024,2048]{1,0:T(8,128)}), f32[32,2048]{1,0:T(8,128)}) %reduce-scatter.6.cloned.1.call-update) | async-done | bytes 262160 | tf_op jit(solution)/shard_map/reduce_scatter | solution.py:517
  1366.3 147.5 %reduce-scatter.10.cloned.1.call-done = f32[64,1024]{1,0:T(8,128)} async-done(((f32[2048,1024]{1,0:T(8,128)}), f32[64,1024]{1,0:T(8,128)}) %reduce-scatter.10.cloned.1.call-update) | async-done | bytes 262160 | tf_op jit(solution)/shard_map/reduce_scatter | solution.py:519
  1513.8 199.2 %reduce-scatter.8.cloned.1.call-done = f32[32,4224]{1,0:T(8,128)} async-done(((f32[1024,4224]{1,0:T(8,128)}), f32[32,4224]{1,0:T(8,128)}) %reduce-scatter.8.cloned.1.call-update) | async-done | bytes 540688 | tf_op jit(solution)/shard_map/reduce_scatter | solution.py:518
  1713.0 184.6 %reduce-scatter.12.cloned.1.call-done = f32[32,4096]{1,0:T(8,128)} async-done(((f32[1024,4096]{1,0:T(8,128)}), f32[32,4096]{1,0:T(8,128)}) %reduce-scatter.12.cloned.1.call-update) | async-done | bytes 524304 | tf_op jit(solution)/shard_map/reduce_scatter | solution.py:520
  1897.6 187.2 %reduce-scatter.14.cloned.1.call-done = f32[128,1024]{1,0:T(8,128)} async-done(((f32[4096,1024]{1,0:T(8,128)}), f32[128,1024]{1,0:T(8,128)}) %reduce-scatter.14.cloned.1.call-update) | async-done | bytes 524304 | tf_op jit(solution)/shard_map/reduce_scatter | solution.py:521
  (740 shorter events, 649.3 us)
Async XLA Ops:
  7.2 1206.6 %all-reduce.38.cloned.1.call-start = ((), (), s32[]{:S(2)}) async-start(), calls=%async_computation.10 | async-start | bytes 671744
  7.2 38.3 %copy-start.200 = (f32[32]{0:T(128)}, f32[32]{0:T(128)S(1)}, u32[]{:S(2)}) copy-start(f32[32]{0:T(128)S(1)} %iota_convert_fusion) | copy-start | bytes 388
  34.7 165.2 %copy-start.33 = (f32[1024,16]{1,0:T(8,128)}, f32[1024,16]{1,0:T(8,128)S(1)}, u32[]{:S(2)}) copy-start(f32[1024,16]{1,0:T(8,128)S(1)} %get-tuple-element.672) | copy-start | bytes 196612
  44.4 34.2 %copy-start.104 = (bf16[83712]{0:T(1024)(128)(2,1)}, bf16[83712]{0:T(1024)(128)(2,1)S(1)}, u32[]{:S(2)}) copy-start(bf16[83712]{0:T(1024)(128)(2,1)S(1)} %reshape.695) | copy-start | bytes 502276
  70.6 67.8 %copy-start.205 = (f32[128]{0:T(128)}, f32[128]{0:T(128)S(1)}, u32[]{:S(2)}) copy-start(f32[128]{0:T(128)S(1)} %multiply_reduce_fusion.13) | copy-start | bytes 1540
  139.9 480.5 %copy-start.90 = (f32[1024]{0:T(1024)}, f32[1024]{0:T(1024)S(1)}, u32[]{:S(2)}) copy-start(f32[1024]{0:T(1024)S(1)} %get-tuple-element.761) | copy-start | bytes 12292
  139.9 495.9 %copy-start.88 = (f32[1024]{0:T(1024)}, f32[1024]{0:T(1024)S(1)}, u32[]{:S(2)}) copy-start(f32[1024]{0:T(1024)S(1)} %get-tuple-element.718) | copy-start | bytes 12292
  169.5 30.4 %copy-start.37 = (f32[4,1024,16]{2,0,1:T(4,128)S(1)}, f32[4,1024,16]{2,0,1:T(4,128)}, u32[]{:S(2)}) copy-start(f32[4,1024,16]{2,0,1:T(4,128)} %copy.186) | copy-start | bytes 786436
  169.5 30.4 %copy-start.68 = (f32[1024,16]{1,0:T(8,128)S(1)}, f32[1024,16]{1,0:T(8,128)}, u32[]{:S(2)}) copy-start(f32[1024,16]{1,0:T(8,128)} %copy-done.67) | copy-start | bytes 196612
  214.3 153.5 %copy-start.105 = (f32[4224]{0:T(1024)S(1)}, f32[4224]{0:T(1024)}, u32[]{:S(2)}) copy-start(f32[4224]{0:T(1024)} %slice_convert_fusion.1) | copy-start | bytes 50692
  219.1 153.5 %copy-start.61 = (bf16[128,1024]{1,0:T(8,128)(2,1)}, bf16[128,1024]{1,0:T(8,128)(2,1)S(1)}, u32[]{:S(2)}) copy-start(bf16[128,1024]{1,0:T(8,128)(2,1)S(1)} %get-tuple-element.694) | copy-start | bytes 786436
  406.7 137.7 %copy-start.24 = (f32[128,1024]{1,0:T(8,128)}, f32[128,1024]{1,0:T(8,128)S(1)}, u32[]{:S(2)}) copy-start(f32[128,1024]{1,0:T(8,128)S(1)} %get-tuple-element.703) | copy-start | bytes 1572868
  487.4 36.2 %copy-start.123 = (f32[4,32]{1,0:T(4,128)}, f32[4,32]{1,0:T(4,128)S(1)}, u32[]{:S(2)}) copy-start(f32[4,32]{1,0:T(4,128)S(1)} %div.206) | copy-start | bytes 1540
  492.8 115.8 %copy-start.170 = (f32[128]{0:T(128)}, f32[128]{0:T(128)S(1)}, u32[]{:S(2)}) copy-start(f32[128]{0:T(128)S(1)} %fusion.208) | copy-start | bytes 1540
  988.9 39.0 %copy-start.8 = (f32[4096,16]{1,0:T(8,128)S(1)}, f32[4096,16]{1,0:T(8,128)}, u32[]{:S(2)}) copy-start(f32[4096,16]{1,0:T(8,128)} %copy-done.7) | copy-start | bytes 786436
  988.9 39.0 %copy-start.36 = (f32[1024,16]{1,0:T(8,128)S(1)}, f32[1024,16]{1,0:T(8,128)}, u32[]{:S(2)}) copy-start(f32[1024,16]{1,0:T(8,128)} %copy-done.33) | copy-start | bytes 196612
  988.9 39.0 %copy-start.43 = (f32[1,1024,16]{2,1,0:T(8,128)S(1)}, f32[1,1024,16]{2,1,0:T(8,128)}, u32[]{:S(2)}) copy-start(f32[1,1024,16]{2,1,0:T(8,128)} %copy-done.42) | copy-start | bytes 196612
  988.9 39.0 %copy-start.45 = (f32[1024,16]{1,0:T(8,128)S(1)}, f32[1024,16]{1,0:T(8,128)}, u32[]{:S(2)}) copy-start(f32[1024,16]{1,0:T(8,128)} %copy-done.44) | copy-start | bytes 196612
  988.9 39.0 %copy-start.47 = (f32[1024,16]{1,0:T(8,128)S(1)}, f32[1024,16]{1,0:T(8,128)}, u32[]{:S(2)}) copy-start(f32[1024,16]{1,0:T(8,128)} %copy-done.46) | copy-start | bytes 196612
  1089.5 276.8 %reduce-scatter.6.cloned.1.call-start = ((), (), s32[]{:S(2)}) async-start(), calls=%async_computation.5 | async-start | bytes 8650752 | tf_op jit(solution)/shard_map/reduce_scatter | solution.py:517
  1095.6 418.2 %reduce-scatter.10.cloned.1.call-start = ((), (), s32[]{:S(2)}) async-start(), calls=%async_computation.7 | async-start | bytes 8650752 | tf_op jit(solution)/shard_map/reduce_scatter | solution.py:519
  1102.7 610.3 %reduce-scatter.8.cloned.1.call-start = ((), (), s32[]{:S(2)}) async-start(), calls=%async_computation.6 | async-start | bytes 17842176 | tf_op jit(solution)/shard_map/reduce_scatter | solution.py:518
  1128.1 769.5 %reduce-scatter.12.cloned.1.call-start = ((), (), s32[]{:S(2)}) async-start(), calls=%async_computation.8 | async-start | bytes 17301504 | tf_op jit(solution)/shard_map/reduce_scatter | solution.py:520
  1141.2 943.6 %reduce-scatter.14.cloned.1.call-start = ((), (), s32[]{:S(2)}) async-start(), calls=%async_computation.9 | async-start | bytes 17301504 | tf_op jit(solution)/shard_map/reduce_scatter | solution.py:521
  (208 other events, 1668.1 us)
Sparse Core Ops, SparseCore 0:
  1089.6 124.1 all-reduce.37
  1216.8 149.4 reduce-scatter.5
  1369.3 144.5 reduce-scatter.9
  1521.8 191.1 reduce-scatter.7
  1715.8 181.7 reduce-scatter.11
  1900.4 184.3 reduce-scatter.13

commit v2 on v1

v2 whole, which is shorter than its diff:
```python
import functools
import math

import jax
import jax.numpy as jnp
from jax import lax
from jax.experimental import pallas as pl
from jax.experimental.pallas import tpu as pltpu
from jax.sharding import PartitionSpec as P

D = 1024
Z = 128
VALUE_WIDTH = 2048
H = 16
FF = 4096
STRETCH = 128


epsilon = 1e-05

MESH = pl.DeviceIdType.MESH

class Place:
    def __init__(self, dims):
        self.Z, self.Y, self.X = dims
        me = lax.axis_index("fsdp")
        self.me = me
        self.c = me % 2
        self.x = (me // 2) % self.X
        self.y = (me // (2 * self.X)) % self.Y
        self.z = me // (2 * self.X * self.Y)
        self.nx = self.dev(self.z, self.y, 1 - self.x, self.c)
        self.ny = self.dev(self.z, 1 - self.y, self.x, self.c)
        self.nc = self.dev(self.z, self.y, self.x, 1 - self.c)
        self.has_down = self.z > 0
        self.has_up = self.z < self.Z - 1
        self.down = self.dev(jnp.maximum(self.z - 1, 0), self.y, self.x, self.c)
        self.up = self.dev(jnp.minimum(self.z + 1, self.Z - 1), self.y, self.x, self.c)
    def dev(self, z, y, x, c):
        return ((z * self.Y + y) * self.X + x) * 2 + c
    def barrier(self):
        bar = pltpu.get_barrier_semaphore()
        def tell(d):
            pl.semaphore_signal(bar, inc=1, device_id=(d,), device_id_type=MESH)
        for d in (self.nx, self.ny, self.nc):
            tell(d)
        pl.when(self.has_down)(lambda: tell(self.down))
        pl.when(self.has_up)(lambda: tell(self.up))
        pl.semaphore_wait(bar, 3 + jnp.where(self.has_down, 1, 0) + jnp.where(self.has_up, 1, 0))

def when(cond, f):
    if cond is None: f()
    else: pl.when(cond)(f)

class Gather:
    def __init__(self, place, ins, outs, send_sem, recv_sem):
        self.p, self.ins, self.outs = place, ins, outs
        self.ss, self.rs = send_sem, recv_sem
        self.ids, self.pend = {}, []
    def rows(self, k, h):
        n = self.ins[k].shape[0]
        return (0, n) if h == 2 else (h * (n // 2), n // 2)
    def copy(self, key, k, shard, h, to, own=False):
        i = self.ids.setdefault((key, k), len(self.ids))
        r, n = self.rows(k, h)
        full = self.ins[k].shape[0]
        dst = self.outs[k].at[pl.ds(shard * full + r, n)]
        src = self.ins[k].at[pl.ds(r, n)] if own else dst
        return pltpu.make_async_remote_copy(src_ref=src, dst_ref=dst, send_sem=self.ss.at[i], recv_sem=self.rs.at[i], device_id=(to,), device_id_type=MESH)
    def send(self, cond, *a):
        when(cond, lambda: self.copy(*a).start())
        self.pend.append((cond, lambda: self.copy(*a).wait_send()))
    def recv(self, cond, key, k, shard, h):
        when(cond, lambda: self.copy(key, k, shard, h, self.p.me).wait_recv())
    def col(self, o):
        p = self.p
        if o == 0: return None, p.z
        if o > 0: return p.z - o >= 0, jnp.maximum(p.z - o, 0)
        return p.z - o <= p.Z - 1, jnp.minimum(p.z - o, p.Z - 1)
    def offs(self, s):
        return (0,) if s == 0 else (s, -s)
    def stage(self, k, s):
        p = self.p
        L = p.Z
        if s < L:
            for o in self.offs(s):
                cond, zz = self.col(o)
                sh = p.dev(zz, p.y, p.x, p.c)
                own = o == 0
                if not own:
                    self.recv(cond, ("z", o), k, sh, 2)
                if s + 1 < L:
                    both = lambda c1: c1 if cond is None else jnp.logical_and(cond, c1)
                    if o >= 0: self.send(both(p.has_up), ("z", s + 1), k, sh, 2, p.up, own)
                    if o <= 0: self.send(both(p.has_down), ("z", -(s + 1)), k, sh, 2, p.down, own)
                self.send(cond, ("x", o), k, sh, 2, p.nx, own)
                self.send(cond, ("y", o), k, sh, 2, p.ny, own)
                self.send(cond, ("c", o), k, sh, 2, p.nc, own)
        if 1 <= s <= L:
            for o in self.offs(s - 1):
                cond, zz = self.col(o)
                sx, sy = p.dev(zz, p.y, 1 - p.x, p.c), p.dev(zz, 1 - p.y, p.x, p.c)
                self.recv(cond, ("x", o), k, sx, 2)
                self.send(cond, ("xy", o), k, sx, 0, p.ny)
                self.send(cond, ("cx", o), k, sx, 2, p.nc)
                self.recv(cond, ("y", o), k, sy, 2)
                self.send(cond, ("yx", o), k, sy, 1, p.nx)
                self.send(cond, ("cy", o), k, sy, 2, p.nc)
        if 2 <= s <= L + 1:
            for o in self.offs(s - 2):
                cond, zz = self.col(o)
                sd = p.dev(zz, 1 - p.y, 1 - p.x, p.c)
                self.recv(cond, ("xy", o), k, sd, 0)
                self.recv(cond, ("yx", o), k, sd, 1)
                self.send(cond, ("cd", o), k, sd, 2, p.nc)
        if s == L + 2:
            for t in range(L):
                for o in self.offs(t):
                    cond, zz = self.col(o)
                    for key, yy, xx in (("c", p.y, p.x), ("cx", p.y, 1 - p.x), ("cy", 1 - p.y, p.x), ("cd", 1 - p.y, 1 - p.x)):
                        self.recv(cond, (key, o), k, p.dev(zz, yy, xx, 1 - p.c), 2)
    def stages(self):
        return self.p.Z + 3
    def finish(self):
        for cond, f in self.pend:
            when(cond, f)

def sems_needed(dims, K):
    Z = dims[0]
    offs = 2 * Z - 1
    return K * (2 * (Z - 1) + 8 * offs)

def ag_kernel(dims, K, *refs):
    ins, outs = refs[:K], refs[K:2 * K]
    own, ss, rs = refs[2 * K:]
    p = Place(dims)
    p.barrier()
    g = Gather(p, ins, outs, ss, rs)
    cps = [pltpu.make_async_copy(ins[k], outs[k].at[pl.ds(p.me * ins[k].shape[0], ins[k].shape[0])], own.at[k]) for k in range(K)]
    for cp in cps: cp.start()
    S = g.stages()
    for t in range(K + S - 1):
        for k in range(K):
            if 0 <= t - k < S: g.stage(k, t - k)
    g.finish()
    for cp in cps: cp.wait()

def gather(dims, n, arrays, cid):
    K = len(arrays)
    ns = sems_needed(dims, K)
    return pl.pallas_call(functools.partial(ag_kernel, dims, K),
        out_shape=[jax.ShapeDtypeStruct((n * a.shape[0],) + a.shape[1:], a.dtype) for a in arrays],
        in_specs=[pl.BlockSpec(memory_space=pl.ANY)] * K, out_specs=[pl.BlockSpec(memory_space=pl.ANY)] * K,
        scratch_shapes=[pltpu.SemaphoreType.DMA((K,)), pltpu.SemaphoreType.DMA((ns,)), pltpu.SemaphoreType.DMA((ns,))],
        compiler_params=pltpu.CompilerParams(collective_id=cid, has_side_effects=True))(*arrays)


F32, BF16 = jnp.float32, jnp.bfloat16
TILE = 256
O_GAIN, O_SHIFT, O_OMEGA, O_AFF, O_REL = 0, 2 * D, 4 * D, 5 * D, 5 * D + 4 * Z
O_VB = O_REL + STRETCH
O_MXB = O_VB + VALUE_WIDTH
MXW = 2 * D + Z + VALUE_WIDTH
O_HB = O_MXB + MXW
O_UPB = O_HB + D
O_DNB = O_UPB + FF
O_EMA = O_DNB + D
C_LAT, C_RES, C_HX = D, D + Z, D + Z + VALUE_WIDTH


def sigmoid(v):
    return 0.5 * jnp.tanh(0.5 * v) + 0.5


def silu_slope(v, s):
    return s * (1.0 + v * (1.0 - s))


def col_sum(v):
    return jnp.sum(v, axis=0, keepdims=True)


def dot(a, b, ca=1, cb=0):
    return lax.dot_general(a, b, (((ca,), (cb,)), ((), ())), preferred_element_type=F32)


def tiles(lo, hi, step, f):
    @pl.loop(0, (hi - lo) // step)
    def _(i):
        f(pl.multiple_of(lo + i * step, 128))


def lane_block(l):
    return pl.ds(pl.multiple_of(l * 128, 128), 128)


def center(xf):
    c = xf - jnp.mean(xf, axis=-1, keepdims=True)
    r = lax.rsqrt(jnp.mean(c * c, axis=-1, keepdims=True) + epsilon)
    return c * r, r


def ema_rates(ema):
    gate, a = sigmoid(ema[0]), sigmoid(ema[1])
    retain = 1.0 - gate * a
    weight = gate * ema[2] * ema[3] * (1.0 / math.sqrt(H))
    return gate, a, retain, weight


def rel_table(rel_row):
    wide = jnp.broadcast_to(rel_row, (STRETCH, STRETCH))
    return pltpu.roll(wide, 0, 1, stride=1, stride_axis=0)


def causal():
    i = lax.broadcasted_iota(jnp.int32, (STRETCH, STRETCH), 0)
    j = lax.broadcasted_iota(jnp.int32, (STRETCH, STRETCH), 1)
    return j <= i


class Forward:
    def __init__(self, x, valid, prow, ema, rel, w, s):
        self.x, self.valid, self.prow, self.ema, self.rel, self.w, self.s = x, valid, prow, ema, rel, w, s
        self.m = x.shape[0]
        self.seqs = self.m // STRETCH

    def p(self, lo, n):
        return self.prow[:, lo : lo + n]

    def pd(self, lo, col, n):
        return self.prow[:, pl.ds(pl.multiple_of(lo + col, 128), n)]

    def norm_one(self):
        s = self.s
        g, b = self.p(O_GAIN, D), self.p(O_SHIFT, D)
        for q in range(self.seqs):
            s.mpad[q, 0:8, :] = jnp.zeros((8, D), F32)

            @pl.loop(0, STRETCH // 32)
            def _(i):
                r = pl.ds(q * STRETCH + i * 32, 32)
                xhat, _ = center(self.x[r, :].astype(F32))
                n = xhat * g + b
                s.normed[r, :] = n.astype(BF16)
                s.mpad[q, pl.ds(8 + i * 32, 32), :] = n * self.valid[r, 0:1]

    def ema_kernel(self):
        _, _, retain, weight = ema_rates(self.ema)

        def step(j, p):
            self.s.kern[pl.ds(j, 1), :] = col_sum(p)
            return p * retain

        lax.fori_loop(0, STRETCH, step, weight)

    def smooth(self):
        s = self.s
        omega = self.p(O_OMEGA, D)
        for q in range(self.seqs):

            @pl.loop(0, D // 128)
            def _(l):
                lb = lane_block(l)
                om = self.prow[:, pl.ds(pl.multiple_of(O_OMEGA + l * 128, 128), 128)]
                nb = STRETCH // 8
                acc = [om * s.mpad[q, 8 + 8 * i : 16 + 8 * i, lb] for i in range(nb)]
                for b in range(8):
                    sh = [s.mpad[q, 8 - b + 8 * i : 16 - b + 8 * i, lb] for i in range(nb)]
                    for a in range(nb):
                        kb = jnp.broadcast_to(s.kern[8 * a + b : 8 * a + b + 1, lb], (8, 128))
                        for i in range(a, nb):
                            acc[i] = acc[i] + kb * sh[i - a]
                for i in range(nb):
                    r = slice(q * STRETCH + 8 * i, q * STRETCH + 8 * i + 8)
                    s.e[r, lb] = acc[i]

    def mix(self):
        s = self.s

        @pl.loop(0, self.m // 32)
        def _(i):
            r = pl.ds(i * 32, 32)
            e = s.e[r, :]
            s.mixed[r, :] = (e * sigmoid(e)).astype(BF16)

    def values(self):
        s = self.s

        def one(col):
            cols = pl.ds(col, TILE)
            v = dot(s.normed[...], self.w.v[:, cols]) + self.pd(O_VB, col, TILE)
            s.vpre[:, cols] = v
            s.val[:, cols] = (v * sigmoid(v)).astype(BF16)

        tiles(0, VALUE_WIDTH, TILE, one)

    def base(self):
        s = self.s

        def one(width):
            def f(col):
                cols = pl.ds(col, width)
                s.base[:, cols] = dot(s.mixed[...], self.w.mx[:, cols]) + self.pd(O_MXB, col, width)

            return f

        tiles(0, D, TILE, one(TILE))
        tiles(C_LAT, C_RES, Z, one(Z))
        tiles(C_RES, MXW, TILE, one(TILE))

    def attend(self):
        s = self.s
        table, mask = rel_table(self.rel[...]), causal()
        for q in range(self.seqs):
            r = slice(q * STRETCH, (q + 1) * STRETCH)
            b = s.base[r, C_LAT:C_RES]
            lat = b * sigmoid(b)
            query = (lat * (1.0 + self.p(O_AFF, Z)) + self.p(O_AFF + 2 * Z, Z)).astype(BF16)
            keys = (lat * (1.0 + self.p(O_AFF + Z, Z)) + self.p(O_AFF + 3 * Z, Z)).astype(BF16)
            sc = jnp.where(mask, dot(query, keys, 1, 1) * (1.0 / math.sqrt(Z)) + table, -1e30)
            ex = jnp.exp(sc - jnp.max(sc, axis=-1, keepdims=True))
            pr = ex / jnp.sum(ex, axis=-1, keepdims=True)
            s.probs[r, :] = pr
            s.query[r, :] = query
            s.keys[r, :] = keys
            low = pr.astype(BF16)

            def one(col):
                cols = pl.ds(col, TILE)
                at = dot(low, s.val[r, cols])
                s.att[r, cols] = at
                bb = s.base[r, pl.ds(pl.multiple_of(C_RES + col, 128), TILE)]
                s.gated[r, cols] = (at * (bb * sigmoid(bb))).astype(BF16)

            tiles(0, VALUE_WIDTH, TILE, one)

    def hidden(self):
        s = self.s

        def one(col):
            cols = pl.ds(col, TILE)
            h = dot(s.gated[...], self.w.h[:, cols]) + self.pd(O_HB, col, TILE)
            h = h + s.base[:, pl.ds(pl.multiple_of(C_HX + col, 128), TILE)]
            s.hpre[:, cols] = h
            xf = self.x[:, cols].astype(F32)
            u = sigmoid(s.base[:, cols])
            s.first[:, cols] = xf + self.valid[:, 0:1] * u * (h * sigmoid(h) - xf)

        tiles(0, D, TILE, one)

    def norm_two(self):
        s = self.s
        g, b = self.p(O_GAIN + D, D), self.p(O_SHIFT + D, D)

        @pl.loop(0, self.m // 32)
        def _(i):
            r = pl.ds(i * 32, 32)
            xhat, _ = center(s.first[r, :])
            s.second[r, :] = (xhat * g + b).astype(BF16)

    def up(self):
        s = self.s

        def one(col):
            cols = pl.ds(col, TILE)
            u = dot(s.second[...], self.w.up[:, cols]) + self.pd(O_UPB, col, TILE)
            s.upre[:, cols] = u
            s.inner[:, cols] = (u * sigmoid(u)).astype(BF16)

        tiles(0, FF, TILE, one)

    def down(self, out):
        s = self.s

        def one(col):
            cols = pl.ds(col, TILE)
            d = dot(s.inner[...], self.w.down[:, cols]) + self.pd(O_DNB, col, TILE)
            out[:, cols] = (s.first[:, cols] + self.valid[:, 0:1] * d).astype(BF16)

        tiles(0, D, TILE, one)


class Backward:
    def __init__(self, x, g, valid, prow, ema, rel, w, s, t, grow, gema):
        self.x, self.g, self.valid, self.prow, self.ema, self.rel = x, g, valid, prow, ema, rel
        self.w, self.s, self.t, self.grow, self.gema = w, s, t, grow, gema
        self.m = x.shape[0]
        self.seqs = self.m // STRETCH

    p, pd = Forward.p, Forward.pd

    def put(self, lo, col, n, v):
        self.grow[:, pl.ds(pl.multiple_of(lo + col, 128), n)] = v

    def cot(self):
        def one(col):
            cols = pl.ds(col, TILE)
            d = self.valid[:, 0:1] * self.g[:, cols].astype(F32)
            self.put(O_DNB, col, TILE, col_sum(d))
            self.t.dd[:, cols] = d.astype(BF16)

        tiles(0, D, TILE, one)

    def d_up(self):
        s, t = self.s, self.t

        def one(col):
            cols = pl.ds(col, TILE)
            di = dot(t.dd[...], self.w.down[cols, :], 1, 1)
            u = s.upre[:, cols]
            du = di * silu_slope(u, sigmoid(u))
            self.put(O_UPB, col, TILE, col_sum(du))
            t.dup[:, cols] = du.astype(BF16)

        tiles(0, FF, TILE, one)

    def d_second(self):
        t = self.t

        def one(col):
            cols = pl.ds(col, TILE)
            t.dsec[:, cols] = dot(t.dup[...], self.w.up[cols, :], 1, 1)

        tiles(0, D, TILE, one)

    def norm_two(self):
        s, t = self.s, self.t
        g = self.p(O_GAIN + D, D)
        t.acc[...] = jnp.zeros(t.acc.shape, F32)

        def add(k, v):
            t.acc[k] += jnp.sum(v.reshape(v.shape[0] // 8, 8, D), axis=0)

        @pl.loop(0, self.m // 32)
        def _(i):
            r = pl.ds(i * 32, 32)
            xhat, rstd = center(s.first[r, :])
            ds = t.dsec[r, :]
            add(0, ds * xhat)
            add(1, ds)
            dh = ds * g
            dn = rstd * (dh - jnp.mean(dh, axis=-1, keepdims=True) - xhat * jnp.mean(dh * xhat, axis=-1, keepdims=True))
            df = self.g[r, :].astype(F32) + dn
            v = self.valid[r, 0:1]
            u = sigmoid(s.base[r, 0:D])
            hp = s.hpre[r, :]
            sh = sigmoid(hp)
            xf = self.x[r, :].astype(F32)
            vu = v * u
            t.dx[r, :] = df - df * vu
            db = df * v * (hp * sh - xf) * u * (1.0 - u)
            add(2, db)
            t.dbase[r, 0:D] = db.astype(BF16)
            dhp = df * vu * silu_slope(hp, sh)
            add(3, dhp)
            t.dbase[r, C_HX:MXW] = dhp.astype(BF16)

        for k, lo in enumerate((O_GAIN + D, O_SHIFT + D, O_MXB, O_HB)):
            self.grow[:, lo : lo + D] = col_sum(t.acc[k])
        self.grow[:, O_MXB + C_HX : O_MXB + MXW] = col_sum(t.acc[3])

    def d_gated(self):
        s, t = self.s, self.t

        def one(col):
            cols = pl.ds(col, TILE)
            bcols = pl.ds(pl.multiple_of(C_RES + col, 128), TILE)
            dg = dot(t.dbase[:, C_HX:MXW], self.w.h[cols, :], 1, 1)
            b = s.base[:, bcols]
            sb = sigmoid(b)
            t.datt[:, cols] = (dg * (b * sb)).astype(BF16)
            db = dg * s.att[:, cols] * silu_slope(b, sb)
            self.put(O_MXB + C_RES, col, TILE, col_sum(db))
            t.dbase[:, bcols] = db.astype(BF16)

        tiles(0, VALUE_WIDTH, TILE, one)

    def attend(self):
        s, t = self.s, self.t
        mask = causal()
        lows, drel = [], None
        aff = [0.0, 0.0, 0.0, 0.0]
        lat_bias = 0.0
        for q in range(self.seqs):
            r = slice(q * STRETCH, (q + 1) * STRETCH)
            pr = s.probs[r, :]
            lows.append(pr.astype(BF16))
            dp = dot(t.datt[r, :], s.val[r, :], 1, 1)
            ds = pr * (dp - jnp.sum(pr * dp, axis=-1, keepdims=True))
            ds = jnp.where(mask, ds, 0.0)
            drel = ds if drel is None else drel + ds
            raw = (ds * (1.0 / math.sqrt(Z))).astype(BF16)
            dq = dot(raw, s.keys[r, :])
            dk = dot(raw, s.query[r, :], 0, 0)
            b = s.base[r, C_LAT:C_RES]
            sb = sigmoid(b)
            lat = b * sb
            for k, v in enumerate((dq * lat, dk * lat, dq, dk)):
                aff[k] = aff[k] + col_sum(v)
            dl = dq * (1.0 + self.p(O_AFF, Z)) + dk * (1.0 + self.p(O_AFF + Z, Z))
            db = dl * silu_slope(b, sb)
            lat_bias = lat_bias + col_sum(db)
            t.dbase[r, C_LAT:C_RES] = db.astype(BF16)
        for k in range(4):
            self.grow[:, O_AFF + k * Z : O_AFF + (k + 1) * Z] = aff[k]
        self.grow[:, O_MXB + C_LAT : O_MXB + C_RES] = lat_bias
        eight = 0.0
        for i in range(0, STRETCH, 8):
            eight = eight + pltpu.roll(drel[i : i + 8, :], (STRETCH - i) % STRETCH, 1)
        back = 0.0
        for i in range(8):
            back = back + pltpu.roll(eight[i : i + 1, :], (STRETCH - i) % STRETCH, 1)
        self.grow[:, O_REL : O_REL + STRETCH] = back

        def one(col):
            cols = pl.ds(col, TILE)
            bias = 0.0
            for q in range(self.seqs):
                r = slice(q * STRETCH, (q + 1) * STRETCH)
                dv = dot(lows[q], t.datt[r, cols], 0, 0)
                v = s.vpre[r, cols]
                dv = dv * silu_slope(v, sigmoid(v))
                bias = bias + col_sum(dv)
                t.dv[r, cols] = dv.astype(BF16)
            self.put(O_VB, col, TILE, bias)

        tiles(0, VALUE_WIDTH, TILE, one)

    def d_mixed(self):
        s, t = self.s, self.t
        for q in range(self.seqs):
            t.dpad[q, STRETCH : STRETCH + 8, :] = jnp.zeros((8, D), F32)

        def one(col):
            cols = pl.ds(col, TILE)
            dm = dot(t.dbase[...], self.w.mx[cols, :], 1, 1)
            e = s.e[:, cols]
            de = dm * silu_slope(e, sigmoid(e))
            om = 0.0
            for q in range(self.seqs):
                d = de[q * STRETCH : (q + 1) * STRETCH, :]
                t.dpad[q, 0:STRETCH, cols] = d
                om = om + col_sum(d * s.mpad[q, 8 : 8 + STRETCH, cols])
            self.put(O_OMEGA, col, TILE, om)

        tiles(0, D, TILE, one)

    def d_normed(self):
        t = self.t

        def one(col):
            cols = pl.ds(col, TILE)
            t.dn[:, cols] = dot(t.dv[...], self.w.v[cols, :], 1, 1)

        tiles(0, D, TILE, one)

    def smooth(self):
        s, t = self.s, self.t
        nb = STRETCH // 8

        @pl.loop(0, D // 128)
        def _(l):
            lb = lane_block(l)
            om = self.prow[:, pl.ds(pl.multiple_of(O_OMEGA + l * 128, 128), 128)]
            for q in range(self.seqs):
                acc = [om * t.dpad[q, 8 * i : 8 * i + 8, lb] for i in range(nb)]
                for b in range(8):
                    sh = [t.dpad[q, 8 * i + b : 8 * i + b + 8, lb] for i in range(nb)]
                    for a in range(nb):
                        kb = jnp.broadcast_to(s.kern[8 * a + b : 8 * a + b + 1, lb], (8, 128))
                        for i in range(nb - a):
                            acc[i] = acc[i] + kb * sh[i + a]
                for i in range(nb):
                    r = slice(q * STRETCH + 8 * i, q * STRETCH + 8 * i + 8)
                    t.dn[r, lb] = t.dn[r, lb] + self.valid[r, :] * acc[i]

        @pl.loop(0, D // 128)
        def _(l):
            lb = lane_block(l)
            for b in range(8):
                sums = [None] * nb
                for q in range(self.seqs):
                    de = [t.dpad[q, 8 * i : 8 * i + 8, lb] for i in range(nb)]
                    sh = [s.mpad[q, 8 - b + 8 * i : 16 - b + 8 * i, lb] for i in range(nb)]
                    for a in range(nb):
                        for i in range(a, nb):
                            v = de[i] * sh[i - a]
                            sums[a] = v if sums[a] is None else sums[a] + v
                for a in range(nb):
                    t.dkern[8 * a + b : 8 * a + b + 1, lb] = col_sum(sums[a])

    def norm_one(self, out):
        t = self.t
        g = self.p(O_GAIN, D)
        t.acc[...] = jnp.zeros(t.acc.shape, F32)

        def add(k, v):
            t.acc[k] += jnp.sum(v.reshape(v.shape[0] // 8, 8, D), axis=0)

        @pl.loop(0, self.m // 32)
        def _(i):
            r = pl.ds(i * 32, 32)
            xhat, rstd = center(self.x[r, :].astype(F32))
            dn = t.dn[r, :]
            add(0, dn * xhat)
            add(1, dn)
            dh = dn * g
            d = rstd * (dh - jnp.mean(dh, axis=-1, keepdims=True) - xhat * jnp.mean(dh * xhat, axis=-1, keepdims=True))
            out[r, :] = (t.dx[r, :] + d).astype(BF16)

        for k, lo in enumerate((O_GAIN, O_SHIFT)):
            self.grow[:, lo : lo + D] = col_sum(t.acc[k])


    def ema_grads(self):
        t = self.t
        gate, a, retain, weight = ema_rates(self.ema)
        zero = retain - retain

        def step(j, carry):
            power, before, dw, dr = carry
            row = t.dkern[pl.ds(j, 1), :]
            dw = dw + row * power
            dr = dr + (row * j.astype(F32)) * before
            return power * retain, power, dw, dr

        _, _, dw, dr = lax.fori_loop(0, STRETCH, step, (zero + 1.0, zero, zero, zero))
        drate = -dr * weight
        scale = 1.0 / math.sqrt(H)
        dgate = drate * a + dw * self.ema[2] * self.ema[3] * scale
        self.gema[0] = dgate * gate * (1.0 - gate)
        self.gema[1] = drate * gate * a * (1.0 - a)
        self.gema[2] = dw * gate * self.ema[3] * scale
        self.gema[3] = dw * gate * self.ema[2] * scale


class Scatter:
    def __init__(self, place, grads, bufs, outs, send_sem, recv_sem, local_sem):
        self.p, self.grads, self.bufs, self.outs = place, grads, bufs, outs
        self.ss, self.rs, self.ls = send_sem, recv_sem, local_sem
        self.ids, self.pend = {}, []

    def copy(self, key, k, src, dst, to):
        i = self.ids.setdefault((key, k), len(self.ids))
        return pltpu.make_async_remote_copy(src_ref=src, dst_ref=dst, send_sem=self.ss.at[i], recv_sem=self.rs.at[i], device_id=(to,), device_id_type=MESH)

    def send(self, cond, key, k, src, dst, to):
        when(cond, lambda: self.copy(key, k, src, dst, to).start())
        self.pend.append((cond, lambda: self.copy(key, k, src, dst, to).wait_send()))

    def recv(self, cond, key, k, dst):
        when(cond, lambda: self.copy(key, k, dst, dst, self.p.me).wait_recv())

    def own(self, k, z):
        p, b = self.p, self.bufs[k]
        layer = p.Y * p.X
        i = k * p.Z + z
        return pltpu.make_async_copy(self.grads[k].at[pl.ds(z * layer, layer), p.c], b.mine.at[pl.ds(z * layer, layer)], self.ls.at[i])

    def add(self, dst, a, b, r0=0, rows=None):
        n = rows

        @pl.loop(0, n // 16)
        def _(i):
            def at(v, r):
                ref, q, off = v
                return ref.at[q, pl.ds(pl.multiple_of(off + r, 16), 16)]

            r = i * 16
            at(dst, r)[...] = at(a, r)[...] + at(b, r)[...]

    def stage(self, k, s):
        p, b = self.p, self.bufs[k]
        layer = p.Y * p.X
        r = b.sum.shape[1]
        half = r // 2
        chip = lambda z, y, x: (z * p.Y + y) * p.X + x
        col = lambda z: (chip(z, p.y, p.x), chip(z, p.y, 1 - p.x), chip(z, 1 - p.y, p.x), chip(z, 1 - p.y, 1 - p.x))
        order = list(range(p.Z))
        if s == 0:
            for z in order:
                self.send(None, ("c", z), k, self.grads[k].at[pl.ds(z * layer, layer), 1 - p.c], b.sum.at[pl.ds(z * layer, layer)], p.nc)
                self.own(k, z).start()
        if s == 1:
            for z in order:
                self.recv(None, ("c", z), k, b.sum.at[pl.ds(z * layer, layer)])
                self.own(k, z).wait()
                me, nx, ny, nd = col(z)
                self.add((b.sum, nd, 0), (b.sum, nd, 0), (b.mine, nd, 0), rows=r)
                self.send(None, ("dx", z), k, b.sum.at[nd, pl.ds(0, half)], b.dx.at[z], p.nx)
                self.send(None, ("dy", z), k, b.sum.at[nd, pl.ds(half, half)], b.dy.at[z], p.ny)
                for q in (nx, ny, me):
                    self.add((b.sum, q, 0), (b.sum, q, 0), (b.mine, q, 0), rows=r)
        if s == 2:
            for z in order:
                me, nx, ny, nd = col(z)
                self.recv(None, ("dx", z), k, b.dx.at[z])
                self.add((b.sum, ny, 0), (b.sum, ny, 0), (b.dx, z, 0), rows=half)
                self.send(None, ("y", z), k, b.sum.at[ny], b.ry.at[z], p.ny)
                self.recv(None, ("dy", z), k, b.dy.at[z])
                self.add((b.sum, nx, half), (b.sum, nx, half), (b.dy, z, 0), rows=half)
                self.send(None, ("x", z), k, b.sum.at[nx], b.rx.at[z], p.nx)
        if s == 3:
            for z in order:
                me = col(z)[0]
                self.recv(None, ("y", z), k, b.ry.at[z])
                self.add((b.sum, me, 0), (b.sum, me, 0), (b.ry, z, 0), rows=r)
                self.recv(None, ("x", z), k, b.rx.at[z])
                self.add((b.sum, me, 0), (b.sum, me, 0), (b.rx, z, 0), rows=r)
        if s == 4:
            for d in range(1, p.Z):
                for up in (True, False):
                    t = p.Z - d if up else d - 1
                    buf, key = (b.ru, "u") if up else (b.rd, "d")
                    q = chip(t, p.y, p.x)
                    passing = p.z < t if up else p.z > t
                    fed = p.has_down if up else p.has_up

                    def relay(q=q, t=t, buf=buf, key=key):
                        self.copy((key, t), k, buf.at[t], buf.at[t], p.me).wait_recv()
                        self.add((b.sum, q, 0), (b.sum, q, 0), (buf, t, 0), rows=r)

                    pl.when(jnp.logical_and(passing, fed))(relay)
                    self.send(passing, (key, t), k, b.sum.at[q], buf.at[t], p.up if up else p.down)
        if s == 5:
            for cond, buf, key in ((None, None, None), (p.has_down, b.ru, "u"), (p.has_up, b.rd, "d")):
                me = chip(p.z, p.y, p.x)
                out = self.outs[k]
                if buf is None:
                    @pl.loop(0, r // 16)
                    def _(i):
                        rr = pl.ds(pl.multiple_of(i * 16, 16), 16)
                        out[rr, :] = b.sum[me, rr, :].astype(F32)
                    continue

                for t in range(p.Z):
                    def last(buf=buf, key=key, out=out, t=t):
                        self.copy((key, t), k, buf.at[t], buf.at[t], p.me).wait_recv()

                        @pl.loop(0, r // 16)
                        def _(i):
                            rr = pl.ds(pl.multiple_of(i * 16, 16), 16)
                            out[rr, :] += buf[t, rr, :].astype(F32)

                    if (key == "u" and t == 0) or (key == "d" and t == p.Z - 1):
                        continue
                    pl.when(jnp.logical_and(cond, p.z == t))(last)

    def stages(self):
        return 6

    def finish(self):
        for cond, f in self.pend:
            when(cond, f)


class Names:
    def __init__(self, **kw):
        self.__dict__.update(kw)


SCATTER_BUFS = ("mine", "sum", "dx", "dy", "rx", "ry", "ru", "rd")


def scatter_scratch(dims, r, w):
    Z, Y, X = dims
    chips = Z * Y * X
    shapes = ((chips, r, w), (chips, r, w), (Z, r // 2, w), (Z, r // 2, w), (Z, r, w), (Z, r, w), (Z, r, w), (Z, r, w))
    return [pltpu.VMEM(s, BF16) for s in shapes]


def scatter_sems(dims, K):
    Z = dims[0]
    return K * (5 * Z + 2 * (Z - 1))


def rs_kernel(dims, K, *refs):
    grads, outs = refs[:K], refs[K : 2 * K]
    nb = len(SCATTER_BUFS)
    bufs = [Names(**dict(zip(SCATTER_BUFS, refs[2 * K + nb * k : 2 * K + nb * (k + 1)]))) for k in range(K)]
    ss, rs, ls = refs[2 * K + nb * K :]
    p = Place(dims)
    p.barrier()
    sc = Scatter(p, grads, bufs, outs, ss, rs, ls)
    S = sc.stages()
    for t in range(K + S - 1):
        for k in range(K):
            if 0 <= t - k < S:
                sc.stage(k, t - k)
    sc.finish()


def scatter(dims, grads, cid):
    K = len(grads)
    n = 2 * dims[0] * dims[1] * dims[2]
    shaped = [g.reshape(n // 2, 2, g.shape[0] // n, g.shape[1]) for g in grads]
    scratch = []
    for g in shaped:
        scratch += scatter_scratch(dims, g.shape[2], g.shape[3])
    ns = scatter_sems(dims, K)
    return pl.pallas_call(
        functools.partial(rs_kernel, dims, K),
        out_shape=[jax.ShapeDtypeStruct(g.shape[2:], F32) for g in shaped],
        in_specs=[pl.BlockSpec(memory_space=pl.ANY)] * K,
        out_specs=[pl.BlockSpec(memory_space=pltpu.VMEM)] * K,
        scratch_shapes=scratch + [pltpu.SemaphoreType.DMA((ns,)), pltpu.SemaphoreType.DMA((ns,)), pltpu.SemaphoreType.DMA((K * dims[0],))],
        compiler_params=pltpu.CompilerParams(collective_id=cid, has_side_effects=True, vmem_limit_bytes=64 * 1024 * 1024),
    )(*shaped)


KEPT = ("normed", "mpad", "e", "mixed", "kern", "vpre", "val", "base", "probs", "query", "keys", "att", "gated", "hpre", "first", "second", "upre", "inner")


def kept_shapes(m):
    seqs = m // STRETCH
    f, b = (lambda *s: (s, F32)), (lambda *s: (s, BF16))
    return dict(
        normed=b(m, D), mpad=f(seqs, STRETCH + 8, D), e=f(m, D), mixed=b(m, D), kern=f(STRETCH, D),
        vpre=f(m, VALUE_WIDTH), val=b(m, VALUE_WIDTH), base=f(m, MXW), probs=f(m, STRETCH),
        query=b(m, Z), keys=b(m, Z), att=f(m, VALUE_WIDTH), gated=b(m, VALUE_WIDTH), hpre=f(m, D),
        first=f(m, D), second=b(m, D), upre=f(m, FF), inner=b(m, FF),
    )


VM = pltpu.VMEM
LIMIT = 64 * 1024 * 1024


def fwd_kernel(x, valid, prow, ema, rel, v, mx, h, up, down, *refs):
    nk = len(KEPT)
    out, kept = refs[0], refs[1 : 1 + nk]
    wv, wmx, wh, wup, wdown, sem = refs[1 + nk :]
    s = Names(**dict(zip(KEPT, kept)))
    loads = [pltpu.make_async_copy(a, b, sem.at[i]) for i, (a, b) in enumerate(((v, wv), (mx, wmx), (h, wh), (up, wup), (down, wdown)))]
    for c in loads:
        c.start()
    f = Forward(x, valid, prow, ema, rel, Names(v=wv, mx=wmx, h=wh, up=wup, down=wdown), s)
    f.norm_one()
    f.ema_kernel()
    f.smooth()
    f.mix()
    loads[0].wait()
    f.values()
    loads[1].wait()
    f.base()
    f.attend()
    loads[2].wait()
    f.hidden()
    f.norm_two()
    loads[3].wait()
    f.up()
    loads[4].wait()
    f.down(out)


def forward(x, valid, prow, ema, rel, weights):
    m = x.shape[0]
    ks = kept_shapes(m)
    outs = [jax.ShapeDtypeStruct((m, D), BF16)] + [jax.ShapeDtypeStruct(*ks[k]) for k in KEPT]
    vm, hbm = pl.BlockSpec(memory_space=VM), pl.BlockSpec(memory_space=pl.ANY)
    res = pl.pallas_call(
        fwd_kernel,
        out_shape=outs,
        in_specs=[vm] * 5 + [hbm] * 5,
        out_specs=[vm] * len(outs),
        scratch_shapes=[VM(w.shape, BF16) for w in weights] + [pltpu.SemaphoreType.DMA((5,))],
        compiler_params=pltpu.CompilerParams(vmem_limit_bytes=LIMIT),
    )(x, valid, prow, ema, rel, *weights)
    return res[0], res[1:]


def weight_grad(a, b, n, out, stage, sem, lo=0):
    count = out.shape[0] // TILE

    def copy(i, slot):
        return pltpu.make_async_copy(stage.at[slot, :, 0:n], out.at[pl.ds(pl.multiple_of(i * TILE, TILE), TILE)], sem.at[slot])

    @pl.loop(0, count // 2)
    def _(j):
        for slot in range(2):
            i = j * 2 + slot

            @pl.when(j > 0)
            def _():
                copy(i - 2, slot).wait()

            rows = a[:, pl.ds(pl.multiple_of(i * TILE, TILE), TILE)]
            for c in range(0, n, 1024):
                wd = min(1024, n - c)
                stage[slot, :, c : c + wd] = dot(rows, b[:, lo + c : lo + c + wd], 0, 0).astype(BF16)
            copy(i, slot).start()

    for slot in range(2):
        copy(count - 2 + slot, slot).wait()


def own_shapes(m):
    seqs = m // STRETCH
    return dict(
        dd=((m, D), BF16), dup=((m, FF), BF16), dsec=((m, D), F32), acc=((4, 8, D), F32), dx=((m, D), F32),
        dbase=((m, MXW), BF16), datt=((m, VALUE_WIDTH), BF16), dv=((m, VALUE_WIDTH), BF16),
        dpad=((seqs, STRETCH + 8, D), F32), dn=((m, D), F32), dkern=((STRETCH, D), F32),
    )


def bwd_kernel(x, g, valid, prow, ema, rel, *refs):
    nk = len(KEPT)
    s = Names(**dict(zip(KEPT, refs[:nk])))
    v, mx, h, up, down = refs[nk : nk + 5]
    refs = refs[nk + 5 :]
    dxo, grow, gema, gv, gmx, gh, gup, gdown = refs[:8]
    own = own_shapes(x.shape[0])
    t = Names(**dict(zip(own, refs[8 : 8 + len(own)])))
    wr, wc, wv, stage, wsem, ssem = refs[8 + len(own) :]
    cp = pltpu.make_async_copy
    l_down = cp(down, wr, wsem.at[0])
    l_up = cp(up, wc.at[:, 0:FF], wsem.at[1])
    l_v = cp(v, wv, wsem.at[2])
    l_h = cp(h, wr.at[0:VALUE_WIDTH], wsem.at[3])
    l_mx = cp(mx, wc, wsem.at[4])
    l_down.start()
    l_up.start()
    l_v.start()
    w = Names(v=wv, mx=wc, h=wr, up=wc.at[:, 0:FF], down=wr)
    b = Backward(x, g, valid, prow, ema, rel, w, s, t, grow, gema)
    b.cot()
    weight_grad(s.inner, t.dd, D, gdown, stage, ssem)
    l_down.wait()
    b.d_up()
    l_h.start()
    weight_grad(s.second, t.dup, FF, gup, stage, ssem)
    l_up.wait()
    b.d_second()
    l_mx.start()
    b.norm_two()
    weight_grad(s.gated, t.dbase, D, gh, stage, ssem, lo=C_HX)
    l_h.wait()
    b.d_gated()
    b.attend()
    weight_grad(s.mixed, t.dbase, MXW, gmx, stage, ssem)
    weight_grad(s.normed, t.dv, VALUE_WIDTH, gv, stage, ssem)
    l_mx.wait()
    b.d_mixed()
    l_v.wait()
    b.d_normed()
    b.smooth()
    b.norm_one(dxo)
    b.ema_grads()


def backward(x, g, valid, prow, ema, rel, kept, weights):
    m = x.shape[0]
    own = own_shapes(m)
    vm, hbm = pl.BlockSpec(memory_space=VM), pl.BlockSpec(memory_space=pl.ANY)
    outs = [jax.ShapeDtypeStruct((m, D), BF16), jax.ShapeDtypeStruct((1, O_EMA), F32), jax.ShapeDtypeStruct(ema.shape, F32)]
    outs += [jax.ShapeDtypeStruct(w.shape, BF16) for w in weights]
    scratch = [VM(*v) for v in own.values()]
    scratch += [VM((FF, D), BF16), VM((D, MXW), BF16), VM((D, VALUE_WIDTH), BF16), VM((2, TILE, MXW), BF16)]
    scratch += [pltpu.SemaphoreType.DMA((5,)), pltpu.SemaphoreType.DMA((2,))]
    res = pl.pallas_call(
        bwd_kernel,
        out_shape=outs,
        in_specs=[vm] * (6 + len(KEPT)) + [hbm] * 5,
        out_specs=[vm] * 3 + [hbm] * 5,
        scratch_shapes=scratch,
        compiler_params=pltpu.CompilerParams(vmem_limit_bytes=LIMIT),
    )(x, g, valid, prow, ema, rel, *kept, *weights)
    return res[0], res[1], res[2], res[3:]


def unpack_params(flat):
    f = flat.astype(F32)
    prow = f[:O_EMA].reshape(1, O_EMA)
    ema = f[O_EMA:].reshape(4, D, H).transpose(0, 2, 1)
    rel = jnp.roll(f[O_REL : O_REL + STRETCH][::-1], 1).reshape(1, STRETCH)
    return prow, ema, rel


def pack_grads(grow, gema):
    row = grow.reshape(-1)
    drel = jnp.roll(row[O_REL : O_REL + STRETCH][::-1], 1)
    return jnp.concatenate([row[:O_REL], drel, row[O_VB:], gema.transpose(0, 2, 1).reshape(-1)])


def layer(inputs, lengths, cotangent, weights, flat):
    shape = inputs.shape
    m = shape[0] * shape[1] * shape[2]
    x, g = inputs.reshape(m, D), cotangent.reshape(m, D)
    mask = (jnp.arange(shape[2]) < lengths[:, :, None]).astype(F32).reshape(m, 1)
    valid = jnp.broadcast_to(mask, (m, 128))
    prow, ema, rel = unpack_params(flat)
    out, kept = forward(x, valid, prow, ema, rel, weights)
    dx, grow, gema, grads = backward(x, g, valid, prow, ema, rel, kept, weights)
    return out.reshape(shape), dx.reshape(shape), grads, pack_grads(grow, gema)


def grid_of(n):
    return (n // 8, 2, 2)


def pack_rows(v, n):
    rows = -(-v.shape[-1] // (128 * 32)) * 32
    return jnp.pad(v, [(0, 0)] * (v.ndim - 1) + [(0, rows * 128 - v.shape[-1])]).reshape(v.shape[:-1] + (rows, 128))


def per_device(n, inputs, lengths, cotangent, v_weight, mx_weight, h_weight, up_weight, down_weight, small_params):
    weights = (v_weight, mx_weight, h_weight, up_weight, down_weight)
    count = small_params.shape[0]
    if n == 32:
        dims = grid_of(n)
        (packed,) = gather(dims, n, (pack_rows(small_params, n),), 0)
        flat = packed.reshape(n, -1)[:, :count].reshape(-1)
        full = gather(dims, n, weights, 1)
    else:
        flat = lax.all_gather(small_params, "fsdp", axis=0, tiled=True)
        full = [lax.all_gather(w, "fsdp", axis=0, tiled=True) for w in weights]
    out, dx, grads, small = layer(inputs, lengths, cotangent, full, flat)
    if n == 32:
        rows = pack_rows(small.astype(BF16).reshape(n, count), n)
        rows = rows.reshape(n * rows.shape[1], 128)
        gdown, gup, gh, gmx, gv, gs = scatter(dims, (grads[4], grads[3], grads[2], grads[1], grads[0], rows), 2)
        gs = gs.reshape(-1)[:count]
    else:
        gv, gmx, gh, gup, gdown = (lax.psum_scatter(a.astype(F32), "fsdp", scatter_dimension=0, tiled=True) for a in grads)
        gs = lax.psum_scatter(small, "fsdp", scatter_dimension=0, tiled=True)
    return out, dx, gv, gmx, gh, gup, gdown, gs


def solution(mesh):
    rows, cols = P("fsdp", None), P(None, "fsdp", None, None)
    return jax.shard_map(
        functools.partial(per_device, mesh.shape["fsdp"]),
        mesh=mesh,
        in_specs=(cols, P(None, "fsdp"), cols, rows, rows, rows, rows, rows, P("fsdp")),
        out_specs=(cols, cols, rows, rows, rows, rows, rows, P("fsdp")),
        check_vma=False,
    )
```

time: 2100 us -> 529 us (0.25)
  waiting for transfers between devices: 913 us -> 0 us
  matrix products: 588 us -> 0 us
  Pallas kernels: 170 us -> 501 us
  local copies, waits for them, and re-layouts: 325 us -> 22.1 us
  other arithmetic: 78.2 us -> 3.9 us
    reduce_scatter x5 -> x0, waiting for transfers between devices: 870 us -> none  [the longest x1 199 us: per_device(): lax.psum_scatter(totals[1], 'fsdp', scatter_dimension=0, tiled=True)]
    dot_general x66 -> x0, matrix products: 588 us -> none  [the longest x6 159 us: smooth_signal(): jnp.einsum('cts,nsc->ntc', toeplitz, blocks, precision=highest_precision)]
    pallas_call x0 -> x3, Pallas kernels: none -> 331 us  [the longest x1 190 us: scatter(): pl.pallas_call(functools.partial(rs_kernel, dims, K), out_shape=[jax.Shap...]
    reshape x15 -> x6, local copies, waits for them, and re-layouts: 86 us -> 5.6 us  [the longest x2 1.87 us: unpack_params(): ema = f[O_EMA:].reshape(4, D, H).transpose(0, 2, 1)]
    unnamed x481 -> x7, local copies, waits for them, and re-layouts: 63.1 us -> 9.73 us
    unnamed x7 -> x0, waiting for transfers between devices: 43.5 us -> none
    rev x6 -> x0, local copies, waits for them, and re-layouts: 40.1 us -> none  [the longest x3 39.4 us: smooth_signal(): powers[::-1]]
    pad x4 -> x0, local copies, waits for them, and re-layouts: 39.9 us -> none  [the longest x2 23.5 us: smooth_signal(): toeplitz = tiled.reshape(width_all, block, 2 * block - 2)[:, :, :block]]
  transfers between devices with their start and end apart: 6 -> 0, of which waited for: 6 -> 0; matrix products, arithmetic and copies ran while one was open for 4% -> 0% of each run, Pallas kernels for 0% -> 0%
where the time goes in v2:
time: 529 us; the launch traced here: 528 us
  Pallas kernels  501 us (95%)
  local copies, waits for them, and re-layouts  22.1 us (4%)
    pallas_call x1, Pallas kernels, scatter(): pl.pallas_call(functools.partial(rs_kernel, dims, K), out_shape=[jax.Shap...  190 us
    pallas_call x2, Pallas kernels, gather(): pl.pallas_call(functools.partial(ag_kernel, dims, K), out_shape=[jax.Shap...  170 us
    pallas_call x1, Pallas kernels, backward(): pl.pallas_call(bwd_kernel, out_shape=outs, in_specs=[vm] * (6 + len(KEPT)...  90.1 us
    pallas_call x1, Pallas kernels, forward(): pl.pallas_call(fwd_kernel, out_shape=outs, in_specs=[vm] * 5 + [hbm] * 5,...  50.7 us

profile of v2, /device:TPU:0, one launch (start us, length us, event | category | flops | bytes accessed | tf_op | source)
XLA Modules:
  0.0 527.9 jit_solution(6982467411660262563)
XLA Ops:
  0.6 0.7 compare_convert_fusion
  1.4 1.3 pad_bitcast_fusion.1.refs_0_
  2.7 0.7 broadcast_in_dim.2.valid
  3.4 21.7 %shard_map.155 = bf16[1024,128]{1,0:T(8,128)(2,1)} custom-call(bf16[32,128]{1,0:T(8,128)(2,1)} %pad_bitcast_fusion.1.refs_0_), custom_call_target="tpu_custom_call" | custom-call | tf_op jit(solution)/shard_map/pallas_call | solution.py:151
  25.1 1.1 reshape.108
  27.1 1.3 maximum_bitcast_fusion.rel
  28.4 0.7 reshape.109.prow
  29.7 1.3 copy.19
  31.0 148.7 %shard_map.156 = (bf16[1024,2048]{1,0:T(8,128)(2,1)}, bf16[1024,4224]{1,0:T(8,128)(2,1)}, bf16[2048,1024]{1,0:T(8,128)(2,1)}, bf16[1024,4096]{1,0:T(8,128)(2,1)}, bf16[4096,1024]{1,0:T(8,128)(2,1)}) custom-call(bf16[32,2048]{1,0:T(8,128)(2,1)} %refs_0_.1, bf16[32,4224]{1,0:T(8,128)(2,1)} %refs_1_.1, bf16[64,1024]{1,0:T(8,128)(2,1)} %refs_2_.1, ...), custom_call_target="tpu_custom_call" | custom-call | tf_op jit(solution)/shard_map/pallas_call | solution.py:151
  179.7 50.7 %shard_map.157 = (bf16[256,1024]{1,0:T(8,128)(2,1)}, bf16[256,1024]{1,0:T(8,128)(2,1)}, f32[2,136,1024]{2,1,0:T(8,128)}, f32[256,1024]{1,0:T(8,128)}, bf16[256,1...) custom-call(bf16[256,1024]{1,0:T(8,128)(2,1)} %bitcast.37, ...), custom_call_target="tpu_custom_call" | custom-call | tf_op jit(solution)/shard_map/pallas_call | solution.py:861
  230.4 90.1 %shard_map.158 = (bf16[256,1024]{1,0:T(8,128)(2,1)}, f32[1,18176]{1,0:T(1,128)}, f32[4,16,1024]{2,1,0:T(8,128)}, bf16[1024,2048]{1,0:T(8,128)(2,1)}, bf16[1024,4...) custom-call(bf16[256,1024]{1,0:T(8,128)(2,1)} %bitcast.38, ...), custom_call_target="tpu_custom_call" | custom-call | tf_op jit(solution)/shard_map/pallas_call | solution.py:960
  320.5 0.7 slice_bitcast_fusion
  321.2 0.9 convert.21
  323.0 1.0 convert_bitcast_fusion
  324.5 0.7 reshape.120
  325.1 1.5 concatenate.11
  327.0 0.7 copy.23
  327.7 189.9 %shard_map.159 = (f32[128,1024]{1,0:T(8,128)}, f32[32,4096]{1,0:T(8,128)}, f32[64,1024]{1,0:T(8,128)}, f32[32,4224]{1,0:T(8,128)}, f32[32,2048]{1,0:T(8,128)}, /*index=5*/f32[32,128]{1,0:T(8,128)}) custom-call(bf16[16,2,128,1024]{3,2,1,0:T(8,128)(2,1)} %bitcast.32, bf16[16,2,32,4096]{3,2,1,0:T(8,128)(2,1)} %bitcast.31, bf16[16,2,64,1024]{3,2,1,0:T(8,128)(2,1)} %bitcast.34, ...), custom_call_target="tpu_custom_call" | custom-call | tf_op jit(solution)/shard_map/pallas_call | solution.py:801
  517.6 1.3 slice.86
  519.0 1.7 copy.29
  520.6 1.9 copy.30
  522.5 1.7 copy.31
  524.2 1.9 copy.32
  526.0 1.9 copy.33
  (15 shorter events, 3.1 us)

commit v3 on v2

--- a/solution.py
+++ b/solution.py
@@ -93,25 +93,27 @@
                     both = lambda c1: c1 if cond is None else jnp.logical_and(cond, c1)
                     if o >= 0: self.send(both(p.has_up), ("z", s + 1), k, sh, 2, p.up, own)
                     if o <= 0: self.send(both(p.has_down), ("z", -(s + 1)), k, sh, 2, p.down, own)
-                self.send(cond, ("x", o), k, sh, 2, p.nx, own)
-                self.send(cond, ("y", o), k, sh, 2, p.ny, own)
+                if abs(o) != 1:
+                    self.send(cond, ("x", o), k, sh, 2, p.nx, own)
+                    self.send(cond, ("y", o), k, sh, 2, p.ny, own)
                 self.send(cond, ("c", o), k, sh, 2, p.nc, own)
         if 1 <= s <= L:
             for o in self.offs(s - 1):
                 cond, zz = self.col(o)
                 sx, sy = p.dev(zz, p.y, 1 - p.x, p.c), p.dev(zz, 1 - p.y, p.x, p.c)
-                self.recv(cond, ("x", o), k, sx, 2)
-                self.send(cond, ("xy", o), k, sx, 0, p.ny)
-                self.send(cond, ("cx", o), k, sx, 2, p.nc)
-                self.recv(cond, ("y", o), k, sy, 2)
-                self.send(cond, ("yx", o), k, sy, 1, p.nx)
-                self.send(cond, ("cy", o), k, sy, 2, p.nc)
+                for key, sh, half, to in (("x", sx, 0, p.ny), ("y", sy, 1, p.nx)):
+                    self.recv(cond, (key, o), k, sh, 2)
+                    if o == 0:
+                        self.send(p.has_up, (key, 1), k, sh, 2, p.up)
+                        self.send(p.has_down, (key, -1), k, sh, 2, p.down)
+                    self.send(cond, ("d" + key, o), k, sh, half, to)
+                    self.send(cond, ("c" + key, o), k, sh, 2, p.nc)
         if 2 <= s <= L + 1:
             for o in self.offs(s - 2):
                 cond, zz = self.col(o)
                 sd = p.dev(zz, 1 - p.y, 1 - p.x, p.c)
-                self.recv(cond, ("xy", o), k, sd, 0)
-                self.recv(cond, ("yx", o), k, sd, 1)
+                self.recv(cond, ("dx", o), k, sd, 0)
+                self.recv(cond, ("dy", o), k, sd, 1)
                 self.send(cond, ("cd", o), k, sd, 2, p.nc)
         if s == L + 2:
             for t in range(L):
@@ -127,32 +129,7 @@
 
 def sems_needed(dims, K):
     Z = dims[0]
-    offs = 2 * Z - 1
-    return K * (2 * (Z - 1) + 8 * offs)
-
-def ag_kernel(dims, K, *refs):
-    ins, outs = refs[:K], refs[K:2 * K]
-    own, ss, rs = refs[2 * K:]
-    p = Place(dims)
-    p.barrier()
-    g = Gather(p, ins, outs, ss, rs)
-    cps = [pltpu.make_async_copy(ins[k], outs[k].at[pl.ds(p.me * ins[k].shape[0], ins[k].shape[0])], own.at[k]) for k in range(K)]
-    for cp in cps: cp.start()
-    S = g.stages()
-    for t in range(K + S - 1):
-        for k in range(K):
-            if 0 <= t - k < S: g.stage(k, t - k)
-    g.finish()
-    for cp in cps: cp.wait()
-
-def gather(dims, n, arrays, cid):
-    K = len(arrays)
-    ns = sems_needed(dims, K)
-    return pl.pallas_call(functools.partial(ag_kernel, dims, K),
-        out_shape=[jax.ShapeDtypeStruct((n * a.shape[0],) + a.shape[1:], a.dtype) for a in arrays],
-        in_specs=[pl.BlockSpec(memory_space=pl.ANY)] * K, out_specs=[pl.BlockSpec(memory_space=pl.ANY)] * K,
-        scratch_shapes=[pltpu.SemaphoreType.DMA((K,)), pltpu.SemaphoreType.DMA((ns,)), pltpu.SemaphoreType.DMA((ns,))],
-        compiler_params=pltpu.CompilerParams(collective_id=cid, has_side_effects=True))(*arrays)
+    return K * (2 * (Z - 1) + 12 * (2 * Z - 1))
 
 
 F32, BF16 = jnp.float32, jnp.bfloat16
@@ -209,7 +186,7 @@
 
 def rel_table(rel_row):
     wide = jnp.broadcast_to(rel_row, (STRETCH, STRETCH))
-    return pltpu.roll(wide, 0, 1, stride=1, stride_axis=0)
+    return pltpu.roll(wide, 0, 1, stride=1, stride_axis=0).T
 
 
 def causal():
@@ -219,8 +196,8 @@
 
 
 class Forward:
-    def __init__(self, x, valid, prow, ema, rel, w, s):
-        self.x, self.valid, self.prow, self.ema, self.rel, self.w, self.s = x, valid, prow, ema, rel, w, s
+    def __init__(self, x, valid, prow, ema, w, s):
+        self.x, self.valid, self.prow, self.ema, self.w, self.s = x, valid, prow, ema, w, s
         self.m = x.shape[0]
         self.seqs = self.m // STRETCH
 
@@ -289,8 +266,9 @@
         def one(col):
             cols = pl.ds(col, TILE)
             v = dot(s.normed[...], self.w.v[:, cols]) + self.pd(O_VB, col, TILE)
-            s.vpre[:, cols] = v
-            s.val[:, cols] = (v * sigmoid(v)).astype(BF16)
+            sv = sigmoid(v)
+            s.vslope[:, cols] = silu_slope(v, sv).astype(BF16)
+            s.val[:, cols] = (v * sv).astype(BF16)
 
         tiles(0, VALUE_WIDTH, TILE, one)
 
@@ -310,7 +288,7 @@
 
     def attend(self):
         s = self.s
-        table, mask = rel_table(self.rel[...]), causal()
+        table, mask = rel_table(self.p(O_REL, STRETCH)), causal()
         for q in range(self.seqs):
             r = slice(q * STRETCH, (q + 1) * STRETCH)
             b = s.base[r, C_LAT:C_RES]
@@ -364,8 +342,9 @@
         def one(col):
             cols = pl.ds(col, TILE)
             u = dot(s.second[...], self.w.up[:, cols]) + self.pd(O_UPB, col, TILE)
-            s.upre[:, cols] = u
-            s.inner[:, cols] = (u * sigmoid(u)).astype(BF16)
+            su = sigmoid(u)
+            s.uslope[:, cols] = silu_slope(u, su).astype(BF16)
+            s.inner[:, cols] = (u * su).astype(BF16)
 
         tiles(0, FF, TILE, one)
 
@@ -381,8 +360,8 @@
 
 
 class Backward:
-    def __init__(self, x, g, valid, prow, ema, rel, w, s, t, grow, gema):
-        self.x, self.g, self.valid, self.prow, self.ema, self.rel = x, g, valid, prow, ema, rel
+    def __init__(self, x, g, valid, prow, ema, w, s, t, grow, gema):
+        self.x, self.g, self.valid, self.prow, self.ema = x, g, valid, prow, ema
         self.w, self.s, self.t, self.grow, self.gema = w, s, t, grow, gema
         self.m = x.shape[0]
         self.seqs = self.m // STRETCH
@@ -407,8 +386,7 @@
         def one(col):
             cols = pl.ds(col, TILE)
             di = dot(t.dd[...], self.w.down[cols, :], 1, 1)
-            u = s.upre[:, cols]
-            du = di * silu_slope(u, sigmoid(u))
+            du = di * s.uslope[:, cols].astype(F32)
             self.put(O_UPB, col, TILE, col_sum(du))
             t.dup[:, cols] = du.astype(BF16)
 
@@ -504,6 +482,7 @@
         for k in range(4):
             self.grow[:, O_AFF + k * Z : O_AFF + (k + 1) * Z] = aff[k]
         self.grow[:, O_MXB + C_LAT : O_MXB + C_RES] = lat_bias
+        drel = drel.T
         eight = 0.0
         for i in range(0, STRETCH, 8):
             eight = eight + pltpu.roll(drel[i : i + 8, :], (STRETCH - i) % STRETCH, 1)
@@ -518,8 +497,7 @@
             for q in range(self.seqs):
                 r = slice(q * STRETCH, (q + 1) * STRETCH)
                 dv = dot(lows[q], t.datt[r, cols], 0, 0)
-                v = s.vpre[r, cols]
-                dv = dv * silu_slope(v, sigmoid(v))
+                dv = dv * s.vslope[r, cols].astype(F32)
                 bias = bias + col_sum(dv)
                 t.dv[r, cols] = dv.astype(BF16)
             self.put(O_VB, col, TILE, bias)
@@ -808,7 +786,7 @@
     )(*shaped)
 
 
-KEPT = ("normed", "mpad", "e", "mixed", "kern", "vpre", "val", "base", "probs", "query", "keys", "att", "gated", "hpre", "first", "second", "upre", "inner")
+KEPT = ("normed", "mpad", "e", "mixed", "kern", "vslope", "val", "base", "probs", "query", "keys", "att", "gated", "hpre", "first", "second", "uslope", "inner")
 
 
 def kept_shapes(m):
@@ -816,57 +794,14 @@
     f, b = (lambda *s: (s, F32)), (lambda *s: (s, BF16))
     return dict(
         normed=b(m, D), mpad=f(seqs, STRETCH + 8, D), e=f(m, D), mixed=b(m, D), kern=f(STRETCH, D),
-        vpre=f(m, VALUE_WIDTH), val=b(m, VALUE_WIDTH), base=f(m, MXW), probs=f(m, STRETCH),
+        vslope=b(m, VALUE_WIDTH), val=b(m, VALUE_WIDTH), base=f(m, MXW), probs=f(m, STRETCH),
         query=b(m, Z), keys=b(m, Z), att=f(m, VALUE_WIDTH), gated=b(m, VALUE_WIDTH), hpre=f(m, D),
-        first=f(m, D), second=b(m, D), upre=f(m, FF), inner=b(m, FF),
+        first=f(m, D), second=b(m, D), uslope=b(m, FF), inner=b(m, FF),
     )
 
 
 VM = pltpu.VMEM
 LIMIT = 64 * 1024 * 1024
-
-
-def fwd_kernel(x, valid, prow, ema, rel, v, mx, h, up, down, *refs):
-    nk = len(KEPT)
-    out, kept = refs[0], refs[1 : 1 + nk]
-    wv, wmx, wh, wup, wdown, sem = refs[1 + nk :]
-    s = Names(**dict(zip(KEPT, kept)))
-    loads = [pltpu.make_async_copy(a, b, sem.at[i]) for i, (a, b) in enumerate(((v, wv), (mx, wmx), (h, wh), (up, wup), (down, wdown)))]
-    for c in loads:
-        c.start()
-    f = Forward(x, valid, prow, ema, rel, Names(v=wv, mx=wmx, h=wh, up=wup, down=wdown), s)
-    f.norm_one()
-    f.ema_kernel()
-    f.smooth()
-    f.mix()
-    loads[0].wait()
-    f.values()
-    loads[1].wait()
-    f.base()
-    f.attend()
-    loads[2].wait()
-    f.hidden()
-    f.norm_two()
-    loads[3].wait()
-    f.up()
-    loads[4].wait()
-    f.down(out)
-
-
-def forward(x, valid, prow, ema, rel, weights):
-    m = x.shape[0]
-    ks = kept_shapes(m)
-    outs = [jax.ShapeDtypeStruct((m, D), BF16)] + [jax.ShapeDtypeStruct(*ks[k]) for k in KEPT]
-    vm, hbm = pl.BlockSpec(memory_space=VM), pl.BlockSpec(memory_space=pl.ANY)
-    res = pl.pallas_call(
-        fwd_kernel,
-        out_shape=outs,
-        in_specs=[vm] * 5 + [hbm] * 5,
-        out_specs=[vm] * len(outs),
-        scratch_shapes=[VM(w.shape, BF16) for w in weights] + [pltpu.SemaphoreType.DMA((5,))],
-        compiler_params=pltpu.CompilerParams(vmem_limit_bytes=LIMIT),
-    )(x, valid, prow, ema, rel, *weights)
-    return res[0], res[1:]
 
 
 def weight_grad(a, b, n, out, stage, sem, lo=0):
@@ -897,39 +832,154 @@
 def own_shapes(m):
     seqs = m // STRETCH
     return dict(
-        dd=((m, D), BF16), dup=((m, FF), BF16), dsec=((m, D), F32), acc=((4, 8, D), F32), dx=((m, D), F32),
+        dd=((m, D), BF16), acc=((4, 8, D), F32), dx=((m, D), F32),
         dbase=((m, MXW), BF16), datt=((m, VALUE_WIDTH), BF16), dv=((m, VALUE_WIDTH), BF16),
         dpad=((seqs, STRETCH + 8, D), F32), dn=((m, D), F32), dkern=((STRETCH, D), F32),
     )
 
 
-def bwd_kernel(x, g, valid, prow, ema, rel, *refs):
-    nk = len(KEPT)
-    s = Names(**dict(zip(KEPT, refs[:nk])))
-    v, mx, h, up, down = refs[nk : nk + 5]
-    refs = refs[nk + 5 :]
-    dxo, grow, gema, gv, gmx, gh, gup, gdown = refs[:8]
-    own = own_shapes(x.shape[0])
-    t = Names(**dict(zip(own, refs[8 : 8 + len(own)])))
-    wr, wc, wv, stage, wsem, ssem = refs[8 + len(own) :]
-    cp = pltpu.make_async_copy
-    l_down = cp(down, wr, wsem.at[0])
-    l_up = cp(up, wc.at[:, 0:FF], wsem.at[1])
-    l_v = cp(v, wv, wsem.at[2])
-    l_h = cp(h, wr.at[0:VALUE_WIDTH], wsem.at[3])
-    l_mx = cp(mx, wc, wsem.at[4])
+SMALL_ROWS = 32
+FRAME = 24
+
+
+def frames(n, count):
+    return [(count * d) // 128 for d in range(n)]
+
+
+def spread(k):
+    p = lax.broadcasted_iota(jnp.int32, (D, TILE), 0)
+    c = lax.broadcasted_iota(jnp.int32, (D, TILE), 1) + k * TILE
+    return (c == 8 * (p % 128) + p // 128).astype(BF16)
+
+
+def unpack_params(n, count, packed, full, prow, ema):
+    full[...] = jnp.zeros(full.shape, F32)
+    for d, r in enumerate(frames(n, count)):
+        full[r : r + FRAME, :] += packed[d * SMALL_ROWS : d * SMALL_ROWS + FRAME, :].astype(F32)
+    for i in range(O_EMA // 128):
+        prow[:, i * 128 : (i + 1) * 128] = full[i : i + 1, :]
+    rows = []
+    for j in range(4):
+        lo = O_EMA // 128 + j * D * H // 128
+        t = full[lo : lo + 128, :].T
+        rows.append(jnp.concatenate([t[H * k : H * (k + 1), :] for k in range(8)], axis=1))
+    stack = jnp.concatenate(rows, axis=0).astype(BF16)
+    for k in range(D // TILE):
+        e = dot(stack, spread(k))
+        for j in range(4):
+            ema[j, :, k * TILE : (k + 1) * TILE] = e[j * H : (j + 1) * H, :]
+
+
+def pack_grads(n, count, grow, gema, full, out):
+    for i in range(O_EMA // 128):
+        full[i : i + 1, :] = grow[:, i * 128 : (i + 1) * 128]
+    stack = jnp.concatenate([gema[j] for j in range(4)], axis=0).astype(BF16)
+    back = 0.0
+    for k in range(D // TILE):
+        back = back + dot(stack[:, k * TILE : (k + 1) * TILE], spread(k), 1, 1)
+    for j in range(4):
+        e = back[j * H : (j + 1) * H, :]
+        lo = O_EMA // 128 + j * D * H // 128
+        full[lo : lo + 128, :] = jnp.concatenate([e[:, k * 128 : (k + 1) * 128] for k in range(8)], axis=0).T
+    for d, r in enumerate(frames(n, count)):
+        out[d * SMALL_ROWS : d * SMALL_ROWS + FRAME, :] = full[r : r + FRAME, :].astype(BF16)
+        out[d * SMALL_ROWS + FRAME : (d + 1) * SMALL_ROWS, :] = jnp.zeros((SMALL_ROWS - FRAME, 128), BF16)
+
+
+class Skip:
+    def step(self):
+        pass
+
+
+def mega_kernel(dims, n, count, K, *refs):
+    x, g, valid = refs[:3]
+    ins = refs[3 : 3 + K]
+    refs = refs[3 + K :]
+    out, dxo, gsmall = refs[:3]
+    grads = refs[3:8]
+    full_w = refs[8 : 8 + K] if dims else ins
+    refs = refs[8 + K :] if dims else refs[8:]
+    ks, own = KEPT, own_shapes(x.shape[0])
+    s = Names(**dict(zip(ks, refs[: len(ks)])))
+    refs = refs[len(ks) :]
+    t = Names(**dict(zip(own, refs[: len(own)])))
+    t.dup, t.dsec = s.inner, t.dn
+    refs = refs[len(own) :]
+    wr, wc, wv, stage, full, packed, prow, ema, grow, gema, lsem, ssem = refs[:12]
+    hsmall, hv, hmx, hh, hup, hdown = full_w
+
+    def loader(i, a, b):
+        return pltpu.make_async_copy(a, b, lsem.at[i])
+
+    if dims:
+        p = Place(dims)
+        p.barrier()
+        osem, send_sem, recv_sem = refs[12:]
+        gat = Gather(p, ins, full_w, send_sem, recv_sem)
+        cps = [pltpu.make_async_copy(ins[k], full_w[k].at[pl.ds(p.me * ins[k].shape[0], ins[k].shape[0])], osem.at[k]) for k in range(K)]
+        for cp in cps:
+            cp.start()
+        S = gat.stages()
+
+        def step(t):
+            for k in range(K):
+                if 0 <= t - k < S:
+                    gat.stage(k, t - k)
+                    if t - k == S - 1:
+                        cps[k].wait()
+    else:
+        S = 7
+
+        def step(t):
+            pass
+
+    w = Names(v=wv, mx=wc, h=wr.at[0:VALUE_WIDTH], up=wc.at[:, 0:FF], down=wr)
+    f = Forward(x, valid, prow, ema, w, s)
+    b = Backward(x, g, valid, prow, ema, w, s, t, grow, gema)
+    gv, gmx, gh, gup, gdown = grads
+    l_small = loader(0, hsmall, packed)
+    l_v = loader(1, hv, wv)
+    l_mx = loader(2, hmx, wc)
+    l_h = loader(3, hh, wr.at[0:VALUE_WIDTH])
+    l_up = loader(4, hup, wc.at[:, 0:FF])
+    l_down = loader(5, hdown, wr)
+
+    for i in range(S):
+        step(i)
+    l_small.start()
+    l_small.wait()
+    unpack_params(n, count, packed, full, prow, ema)
+    f.norm_one()
+    f.ema_kernel()
+    step(S)
+    l_v.start()
+    f.smooth()
+    f.mix()
+    l_v.wait()
+    step(S + 1)
+    l_mx.start()
+    f.values()
+    l_mx.wait()
+    f.base()
+    step(S + 2)
+    l_h.start()
+    f.attend()
+    l_h.wait()
+    f.hidden()
+    f.norm_two()
+    step(S + 3)
+    l_up.start()
+    b.cot()
+    l_up.wait()
+    f.up()
+    weight_grad(s.inner, t.dd, D, gdown, stage, ssem)
+    step(S + 4)
     l_down.start()
-    l_up.start()
-    l_v.start()
-    w = Names(v=wv, mx=wc, h=wr, up=wc.at[:, 0:FF], down=wr)
-    b = Backward(x, g, valid, prow, ema, rel, w, s, t, grow, gema)
-    b.cot()
-    weight_grad(s.inner, t.dd, D, gdown, stage, ssem)
     l_down.wait()
+    f.down(out)
     b.d_up()
     l_h.start()
     weight_grad(s.second, t.dup, FF, gup, stage, ssem)
-    l_up.wait()
     b.d_second()
     l_mx.start()
     b.norm_two()
@@ -941,89 +991,78 @@
     weight_grad(s.normed, t.dv, VALUE_WIDTH, gv, stage, ssem)
     l_mx.wait()
     b.d_mixed()
-    l_v.wait()
     b.d_normed()
     b.smooth()
     b.norm_one(dxo)
     b.ema_grads()
-
-
-def backward(x, g, valid, prow, ema, rel, kept, weights):
-    m = x.shape[0]
-    own = own_shapes(m)
+    pack_grads(n, count, grow, gema, full, gsmall)
+    if dims:
+        gat.finish()
+
+
+def mega(dims, n, count, x, g, valid, arrays, cid):
+    m, K = x.shape[0], len(arrays)
     vm, hbm = pl.BlockSpec(memory_space=VM), pl.BlockSpec(memory_space=pl.ANY)
-    outs = [jax.ShapeDtypeStruct((m, D), BF16), jax.ShapeDtypeStruct((1, O_EMA), F32), jax.ShapeDtypeStruct(ema.shape, F32)]
-    outs += [jax.ShapeDtypeStruct(w.shape, BF16) for w in weights]
-    scratch = [VM(*v) for v in own.values()]
+    whole = [(n * a.shape[0], a.shape[1]) if dims else a.shape for a in arrays]
+    outs = [((m, D), BF16), ((m, D), BF16), ((n * SMALL_ROWS, 128), BF16)] + [(s, BF16) for s in whole[1:]]
+    specs = [vm] * 3 + [hbm] * 5
+    sems = [pltpu.SemaphoreType.DMA((K,)), pltpu.SemaphoreType.DMA((2,))]
+    params = dict(vmem_limit_bytes=LIMIT)
+    if dims:
+        outs += [(s, BF16) for s in whole]
+        specs += [hbm] * K
+        ns = sems_needed(dims, K)
+        sems += [pltpu.SemaphoreType.DMA((K,)), pltpu.SemaphoreType.DMA((ns,)), pltpu.SemaphoreType.DMA((ns,))]
+        params.update(collective_id=cid, has_side_effects=True)
+    rows = -(-(n * count) // 128) + FRAME
+    scratch = [VM(*v) for v in kept_shapes(m).values()] + [VM(*v) for v in own_shapes(m).values()]
     scratch += [VM((FF, D), BF16), VM((D, MXW), BF16), VM((D, VALUE_WIDTH), BF16), VM((2, TILE, MXW), BF16)]
-    scratch += [pltpu.SemaphoreType.DMA((5,)), pltpu.SemaphoreType.DMA((2,))]
+    scratch += [VM((-(-rows // 8) * 8, 128), F32), VM((n * SMALL_ROWS, 128), BF16)]
+    scratch += [VM((1, O_EMA), F32), VM((4, H, D), F32), VM((1, O_EMA), F32), VM((4, H, D), F32)]
     res = pl.pallas_call(
-        bwd_kernel,
-        out_shape=outs,
-        in_specs=[vm] * (6 + len(KEPT)) + [hbm] * 5,
-        out_specs=[vm] * 3 + [hbm] * 5,
-        scratch_shapes=scratch,
-        compiler_params=pltpu.CompilerParams(vmem_limit_bytes=LIMIT),
-    )(x, g, valid, prow, ema, rel, *kept, *weights)
-    return res[0], res[1], res[2], res[3:]
-
-
-def unpack_params(flat):
-    f = flat.astype(F32)
-    prow = f[:O_EMA].reshape(1, O_EMA)
-    ema = f[O_EMA:].reshape(4, D, H).transpose(0, 2, 1)
-    rel = jnp.roll(f[O_REL : O_REL + STRETCH][::-1], 1).reshape(1, STRETCH)
-    return prow, ema, rel
-
-
-def pack_grads(grow, gema):
-    row = grow.reshape(-1)
-    drel = jnp.roll(row[O_REL : O_REL + STRETCH][::-1], 1)
-    return jnp.concatenate([row[:O_REL], drel, row[O_VB:], gema.transpose(0, 2, 1).reshape(-1)])
-
-
-def layer(inputs, lengths, cotangent, weights, flat):
+        functools.partial(mega_kernel, dims, n, count, K),
+        out_shape=[jax.ShapeDtypeStruct(*o) for o in outs],
+        in_specs=[vm] * 3 + [hbm] * K,
+        out_specs=specs,
+        scratch_shapes=scratch + sems,
+        compiler_params=pltpu.CompilerParams(**params),
+    )(x, g, valid, *arrays)
+    return res[0], res[1], res[2], res[3:8]
+
+
+def frame_in(small, me):
+    count = small.shape[0]
+    line = lax.dynamic_update_slice(jnp.zeros((FRAME * 128,), small.dtype), small, ((me * count) % 128,))
+    return jnp.pad(line.reshape(FRAME, 128), ((0, SMALL_ROWS - FRAME), (0, 0)))
+
+
+def frame_out(block, me, count):
+    return lax.dynamic_slice(block.reshape(-1), ((me * count) % 128,), (count,))
+
+
+def grid_of(n):
+    return (n // 8, 2, 2)
+
+
+def per_device(n, inputs, lengths, cotangent, v_weight, mx_weight, h_weight, up_weight, down_weight, small_params):
     shape = inputs.shape
-    m = shape[0] * shape[1] * shape[2]
+    m, count = shape[0] * shape[1] * shape[2], small_params.shape[0]
+    me = lax.axis_index("fsdp")
     x, g = inputs.reshape(m, D), cotangent.reshape(m, D)
     mask = (jnp.arange(shape[2]) < lengths[:, :, None]).astype(F32).reshape(m, 1)
     valid = jnp.broadcast_to(mask, (m, 128))
-    prow, ema, rel = unpack_params(flat)
-    out, kept = forward(x, valid, prow, ema, rel, weights)
-    dx, grow, gema, grads = backward(x, g, valid, prow, ema, rel, kept, weights)
-    return out.reshape(shape), dx.reshape(shape), grads, pack_grads(grow, gema)
-
-
-def grid_of(n):
-    return (n // 8, 2, 2)
-
-
-def pack_rows(v, n):
-    rows = -(-v.shape[-1] // (128 * 32)) * 32
-    return jnp.pad(v, [(0, 0)] * (v.ndim - 1) + [(0, rows * 128 - v.shape[-1])]).reshape(v.shape[:-1] + (rows, 128))
-
-
-def per_device(n, inputs, lengths, cotangent, v_weight, mx_weight, h_weight, up_weight, down_weight, small_params):
-    weights = (v_weight, mx_weight, h_weight, up_weight, down_weight)
-    count = small_params.shape[0]
-    if n == 32:
-        dims = grid_of(n)
-        (packed,) = gather(dims, n, (pack_rows(small_params, n),), 0)
-        flat = packed.reshape(n, -1)[:, :count].reshape(-1)
-        full = gather(dims, n, weights, 1)
+    arrays = (frame_in(small_params, me), v_weight, mx_weight, h_weight, up_weight, down_weight)
+    dims = grid_of(n) if n == 32 else None
+    if not dims:
+        arrays = [lax.all_gather(a, "fsdp", axis=0, tiled=True) for a in arrays]
+    out, dx, small, (gv, gmx, gh, gup, gdown) = mega(dims, n, count, x, g, valid, arrays, 0)
+    if dims:
+        gdown, gup, gh, gmx, gv, gs = scatter(dims, (gdown, gup, gh, gmx, gv, small), 1)
     else:
-        flat = lax.all_gather(small_params, "fsdp", axis=0, tiled=True)
-        full = [lax.all_gather(w, "fsdp", axis=0, tiled=True) for w in weights]
-    out, dx, grads, small = layer(inputs, lengths, cotangent, full, flat)
-    if n == 32:
-        rows = pack_rows(small.astype(BF16).reshape(n, count), n)
-        rows = rows.reshape(n * rows.shape[1], 128)
-        gdown, gup, gh, gmx, gv, gs = scatter(dims, (grads[4], grads[3], grads[2], grads[1], grads[0], rows), 2)
-        gs = gs.reshape(-1)[:count]
-    else:
-        gv, gmx, gh, gup, gdown = (lax.psum_scatter(a.astype(F32), "fsdp", scatter_dimension=0, tiled=True) for a in grads)
-        gs = lax.psum_scatter(small, "fsdp", scatter_dimension=0, tiled=True)
-    return out, dx, gv, gmx, gh, gup, gdown, gs
+        gv, gmx, gh, gup, gdown, gs = (
+            lax.psum_scatter(a.astype(F32), "fsdp", scatter_dimension=0, tiled=True) for a in (gv, gmx, gh, gup, gdown, small)
+        )
+    return out.reshape(shape), dx.reshape(shape), gv, gmx, gh, gup, gdown, frame_out(gs, me, count)
 
 
 def solution(mesh):

time: 529 us -> 474 us (0.90)
  Pallas kernels: 501 us -> 456 us
  local copies, waits for them, and re-layouts: 22.1 us -> 16.4 us
    pallas_call x4 -> x1, Pallas kernels: 311 us -> 262 us  [mega(): pl.pallas_call(functools.partial(mega_kernel, dims, n, count, K), out_sha...]
    reshape x6 -> x0, local copies, waits for them, and re-layouts: 5.6 us -> none  [the longest x2 1.87 us: unpack_params(): ema = f[O_EMA:].reshape(4, D, H).transpose(0, 2, 1)]
where the time goes in v3:
time: 474 us
  Pallas kernels  456 us (96%)
  local copies, waits for them, and re-layouts  16.4 us (3%)
    pallas_call x1, Pallas kernels, mega(): pl.pallas_call(functools.partial(mega_kernel, dims, n, count, K), out_sha...  262 us
    pallas_call x1, Pallas kernels, scatter(): pl.pallas_call(functools.partial(rs_kernel, dims, K), out_shape=[jax.Shap...  194 us
    unnamed x7, local copies, waits for them, and re-layouts  12.7 us

profile of v3, /device:TPU:0, one launch (start us, length us, event | category | flops | bytes accessed | tf_op | source)
XLA Modules:
  0.0 473.7 jit_solution(5843622518614570957)
XLA Ops:
  0.7 0.7 compare_convert_fusion
  1.4 0.9 dynamic_update_slice.3
  2.3 0.6 pad.4.refs_3_
  2.9 0.8 broadcast_in_dim.4.refs_2_
  3.6 261.9 %shard_map.155 = (bf16[256,1024]{1,0:T(8,128)(2,1)}, bf16[256,1024]{1,0:T(8,128)(2,1)}, bf16[1024,128]{1,0:T(8,128)(2,1)}, bf16[1024,2048]{1,0:T(8,128)(2,1)}, b...) custom-call(bf16[256,1024]{1,0:T(8,128)(2,1)} %bitcast.23, ...), custom_call_target="tpu_custom_call" | custom-call | tf_op jit(solution)/shard_map/pallas_call | solution.py:1022
  265.5 194.0 %shard_map.156 = (f32[128,1024]{1,0:T(8,128)}, f32[32,4096]{1,0:T(8,128)}, f32[64,1024]{1,0:T(8,128)}, f32[32,4224]{1,0:T(8,128)}, f32[32,2048]{1,0:T(8,128)}, /*index=5*/f32[32,128]{1,0:T(8,128)}) custom-call(bf16[16,2,128,1024]{3,2,1,0:T(8,128)(2,1)} %bitcast.20, bf16[16,2,32,4096]{3,2,1,0:T(8,128)(2,1)} %bitcast.19, bf16[16,2,64,1024]{3,2,1,0:T(8,128)(2,1)} %bitcast.22, ...), custom_call_target="tpu_custom_call" | custom-call | tf_op jit(solution)/shard_map/pallas_call | solution.py:779
  459.6 1.4 dynamic_slice.3
  461.0 1.9 copy.27
  462.9 1.9 copy.28
  464.7 1.7 copy.29
  466.4 1.9 copy.30
  468.3 1.7 copy.31
  470.0 1.9 copy.32
  471.8 1.9 copy.33
  (1 shorter events, 0.0 us)

commit v4 on v3

--- a/solution.py
+++ b/solution.py
@@ -47,6 +47,15 @@
         pl.when(self.has_down)(lambda: tell(self.down))
         pl.when(self.has_up)(lambda: tell(self.up))
         pl.semaphore_wait(bar, 3 + jnp.where(self.has_down, 1, 0) + jnp.where(self.has_up, 1, 0))
+
+    def barrier_all(self, n):
+        bar = pltpu.get_barrier_semaphore()
+
+        @pl.loop(1, n)
+        def _(i):
+            pl.semaphore_signal(bar, inc=1, device_id=((self.me + i) % n,), device_id_type=MESH)
+
+        pl.semaphore_wait(bar, n - 1)
 
 def when(cond, f):
     if cond is None: f()
@@ -230,10 +239,9 @@
 
         lax.fori_loop(0, STRETCH, step, weight)
 
-    def smooth(self):
+    def smooth(self, q):
         s = self.s
-        omega = self.p(O_OMEGA, D)
-        for q in range(self.seqs):
+        for q in (q,):
 
             @pl.loop(0, D // 128)
             def _(l):
@@ -292,6 +300,7 @@
         for q in range(self.seqs):
             r = slice(q * STRETCH, (q + 1) * STRETCH)
             b = s.base[r, C_LAT:C_RES]
+            s.lat[r, :] = b
             lat = b * sigmoid(b)
             query = (lat * (1.0 + self.p(O_AFF, Z)) + self.p(O_AFF + 2 * Z, Z)).astype(BF16)
             keys = (lat * (1.0 + self.p(O_AFF + Z, Z)) + self.p(O_AFF + 3 * Z, Z)).astype(BF16)
@@ -306,9 +315,12 @@
             def one(col):
                 cols = pl.ds(col, TILE)
                 at = dot(low, s.val[r, cols])
-                s.att[r, cols] = at
                 bb = s.base[r, pl.ds(pl.multiple_of(C_RES + col, 128), TILE)]
-                s.gated[r, cols] = (at * (bb * sigmoid(bb))).astype(BF16)
+                sb = sigmoid(bb)
+                res = bb * sb
+                s.res[r, cols] = res.astype(BF16)
+                s.ars[r, cols] = (at * silu_slope(bb, sb)).astype(BF16)
+                s.gated[r, cols] = (at * res).astype(BF16)
 
             tiles(0, VALUE_WIDTH, TILE, one)
 
@@ -322,6 +334,7 @@
             s.hpre[:, cols] = h
             xf = self.x[:, cols].astype(F32)
             u = sigmoid(s.base[:, cols])
+            s.upd[:, cols] = u
             s.first[:, cols] = xf + self.valid[:, 0:1] * u * (h * sigmoid(h) - xf)
 
         tiles(0, D, TILE, one)
@@ -420,7 +433,7 @@
             dn = rstd * (dh - jnp.mean(dh, axis=-1, keepdims=True) - xhat * jnp.mean(dh * xhat, axis=-1, keepdims=True))
             df = self.g[r, :].astype(F32) + dn
             v = self.valid[r, 0:1]
-            u = sigmoid(s.base[r, 0:D])
+            u = s.upd[r, :]
             hp = s.hpre[r, :]
             sh = sigmoid(hp)
             xf = self.x[r, :].astype(F32)
@@ -444,10 +457,8 @@
             cols = pl.ds(col, TILE)
             bcols = pl.ds(pl.multiple_of(C_RES + col, 128), TILE)
             dg = dot(t.dbase[:, C_HX:MXW], self.w.h[cols, :], 1, 1)
-            b = s.base[:, bcols]
-            sb = sigmoid(b)
-            t.datt[:, cols] = (dg * (b * sb)).astype(BF16)
-            db = dg * s.att[:, cols] * silu_slope(b, sb)
+            t.datt[:, cols] = (dg * s.res[:, cols].astype(F32)).astype(BF16)
+            db = dg * s.ars[:, cols].astype(F32)
             self.put(O_MXB + C_RES, col, TILE, col_sum(db))
             t.dbase[:, bcols] = db.astype(BF16)
 
@@ -470,7 +481,7 @@
             raw = (ds * (1.0 / math.sqrt(Z))).astype(BF16)
             dq = dot(raw, s.keys[r, :])
             dk = dot(raw, s.query[r, :], 0, 0)
-            b = s.base[r, C_LAT:C_RES]
+            b = s.lat[r, :]
             sb = sigmoid(b)
             lat = b * sb
             for k, v in enumerate((dq * lat, dk * lat, dq, dk)):
@@ -532,7 +543,7 @@
 
         tiles(0, D, TILE, one)
 
-    def smooth(self):
+    def smooth_signal(self, seq):
         s, t = self.s, self.t
         nb = STRETCH // 8
 
@@ -540,7 +551,7 @@
         def _(l):
             lb = lane_block(l)
             om = self.prow[:, pl.ds(pl.multiple_of(O_OMEGA + l * 128, 128), 128)]
-            for q in range(self.seqs):
+            for q in (seq,):
                 acc = [om * t.dpad[q, 8 * i : 8 * i + 8, lb] for i in range(nb)]
                 for b in range(8):
                     sh = [t.dpad[q, 8 * i + b : 8 * i + b + 8, lb] for i in range(nb)]
@@ -551,6 +562,10 @@
                 for i in range(nb):
                     r = slice(q * STRETCH + 8 * i, q * STRETCH + 8 * i + 8)
                     t.dn[r, lb] = t.dn[r, lb] + self.valid[r, :] * acc[i]
+
+    def smooth_filter(self):
+        s, t = self.s, self.t
+        nb = STRETCH // 8
 
         @pl.loop(0, D // 128)
         def _(l):
@@ -633,7 +648,7 @@
         p, b = self.p, self.bufs[k]
         layer = p.Y * p.X
         i = k * p.Z + z
-        return pltpu.make_async_copy(self.grads[k].at[pl.ds(z * layer, layer), p.c], b.mine.at[pl.ds(z * layer, layer)], self.ls.at[i])
+        return pltpu.make_async_copy(self.grads[k].at[pl.ds(z * layer, layer), p.c], b.mine.at[pl.ds((z % 2) * layer, layer)], self.ls.at[i])
 
     def add(self, dst, a, b, r0=0, rows=None):
         n = rows
@@ -654,65 +669,94 @@
         half = r // 2
         chip = lambda z, y, x: (z * p.Y + y) * p.X + x
         col = lambda z: (chip(z, p.y, p.x), chip(z, p.y, 1 - p.x), chip(z, 1 - p.y, p.x), chip(z, 1 - p.y, 1 - p.x))
-        order = list(range(p.Z))
+        L = p.Z
+        planes = range(L)
+        off = lambda z, d: p.z == z + d
+        far = lambda z: jnp.logical_and(p.z != z - 1, p.z != z + 1)
+        apart = lambda z: jnp.logical_and(far(z), p.z != z)
+        S, H0, H1 = b.sum, 0, half
         if s == 0:
-            for z in order:
-                self.send(None, ("c", z), k, self.grads[k].at[pl.ds(z * layer, layer), 1 - p.c], b.sum.at[pl.ds(z * layer, layer)], p.nc)
-                self.own(k, z).start()
+            for z in planes:
+                self.send(None, ("c", z), k, self.grads[k].at[pl.ds(z * layer, layer), 1 - p.c], S.at[pl.ds(z * layer, layer)], p.nc)
+                if z < 2:
+                    self.own(k, z).start()
         if s == 1:
-            for z in order:
-                self.recv(None, ("c", z), k, b.sum.at[pl.ds(z * layer, layer)])
+            for z in planes:
+                self.recv(None, ("c", z), k, S.at[pl.ds(z * layer, layer)])
                 self.own(k, z).wait()
                 me, nx, ny, nd = col(z)
-                self.add((b.sum, nd, 0), (b.sum, nd, 0), (b.mine, nd, 0), rows=r)
-                self.send(None, ("dx", z), k, b.sum.at[nd, pl.ds(0, half)], b.dx.at[z], p.nx)
-                self.send(None, ("dy", z), k, b.sum.at[nd, pl.ds(half, half)], b.dy.at[z], p.ny)
+                back = (z - z % 2) * layer
+                self.add((S, nd, 0), (S, nd, 0), (b.mine, nd - back, 0), rows=r)
+                self.send(None, ("dy", z), k, S.at[nd, pl.ds(0, half)], b.dy.at[z], p.ny)
+                self.send(None, ("dx", z), k, S.at[nd, pl.ds(half, half)], b.dx.at[z], p.nx)
                 for q in (nx, ny, me):
-                    self.add((b.sum, q, 0), (b.sum, q, 0), (b.mine, q, 0), rows=r)
+                    self.add((S, q, 0), (S, q, 0), (b.mine, q - back, 0), rows=r)
+                if z + 2 < L:
+                    self.own(k, z + 2).start()
         if s == 2:
-            for z in order:
+            for z in planes:
                 me, nx, ny, nd = col(z)
-                self.recv(None, ("dx", z), k, b.dx.at[z])
-                self.add((b.sum, ny, 0), (b.sum, ny, 0), (b.dx, z, 0), rows=half)
-                self.send(None, ("y", z), k, b.sum.at[ny], b.ry.at[z], p.ny)
-                self.recv(None, ("dy", z), k, b.dy.at[z])
-                self.add((b.sum, nx, half), (b.sum, nx, half), (b.dy, z, 0), rows=half)
-                self.send(None, ("x", z), k, b.sum.at[nx], b.rx.at[z], p.nx)
+                for key, q, h, buf, to, out in (("dy", nx, H0, b.dy, p.nx, b.rx), ("dx", ny, H1, b.dx, p.ny, b.ry)):
+                    self.recv(None, (key, z), k, buf.at[z])
+                    self.add((S, q, h), (S, q, h), (buf, z, 0), rows=half)
+                    tag = "x" if key == "dy" else "y"
+                    side = 0 if key == "dy" else 1
+                    self.send(apart(z), (tag, z), k, S.at[q], out.at[z], to)
+                    if z > 0:
+                        self.send(off(z, -1), ("z" + tag, 0), k, S.at[q], b.rz.at[side], p.up)
+                    if z < L - 1:
+                        self.send(off(z, 1), ("z" + tag, 1), k, S.at[q], b.rz.at[2 + side], p.down)
         if s == 3:
-            for z in order:
+            me, nx, ny, nd = col(p.z)
+            for tag, q, side, to, out in (("x", nx, 0, p.nx, b.rx), ("y", ny, 1, p.ny, b.ry)):
+                for cond, way in ((p.has_down, 0), (p.has_up, 1)):
+
+                    def take(q=q, side=side, way=way, tag=tag):
+                        self.copy(("z" + tag, way), k, b.rz.at[2 * way + side], b.rz.at[2 * way + side], p.me).wait_recv()
+                        self.add((S, q, 0), (S, q, 0), (b.rz, 2 * way + side, 0), rows=r)
+
+                    pl.when(cond)(take)
+                for z in planes:
+                    self.send(p.z == z, (tag, z), k, S.at[q], out.at[z], to)
+        if s == 4:
+            for z in planes:
                 me = col(z)[0]
-                self.recv(None, ("y", z), k, b.ry.at[z])
-                self.add((b.sum, me, 0), (b.sum, me, 0), (b.ry, z, 0), rows=r)
-                self.recv(None, ("x", z), k, b.rx.at[z])
-                self.add((b.sum, me, 0), (b.sum, me, 0), (b.rx, z, 0), rows=r)
-        if s == 4:
-            for d in range(1, p.Z):
-                for up in (True, False):
-                    t = p.Z - d if up else d - 1
-                    buf, key = (b.ru, "u") if up else (b.rd, "d")
+                for tag, buf in (("y", b.ry), ("x", b.rx)):
+
+                    def take(me=me, tag=tag, buf=buf, z=z):
+                        self.copy((tag, z), k, buf.at[z], buf.at[z], p.me).wait_recv()
+                        self.add((S, me, 0), (S, me, 0), (buf, z, 0), rows=r)
+
+                    pl.when(far(z))(take)
+        if 4 <= s < 4 + L - 1:
+            hop = s - 4
+            for up in (True, False):
+                zz = hop if up else L - 1 - hop
+                buf, key, to = (b.ru, "u", p.up) if up else (b.rd, "d", p.down)
+                here = p.z == zz
+                for t in range(L - 1, zz, -1) if up else range(0, zz):
                     q = chip(t, p.y, p.x)
-                    passing = p.z < t if up else p.z > t
-                    fed = p.has_down if up else p.has_up
 
                     def relay(q=q, t=t, buf=buf, key=key):
                         self.copy((key, t), k, buf.at[t], buf.at[t], p.me).wait_recv()
-                        self.add((b.sum, q, 0), (b.sum, q, 0), (buf, t, 0), rows=r)
-
-                    pl.when(jnp.logical_and(passing, fed))(relay)
-                    self.send(passing, (key, t), k, b.sum.at[q], buf.at[t], p.up if up else p.down)
-        if s == 5:
-            for cond, buf, key in ((None, None, None), (p.has_down, b.ru, "u"), (p.has_up, b.rd, "d")):
-                me = chip(p.z, p.y, p.x)
-                out = self.outs[k]
-                if buf is None:
-                    @pl.loop(0, r // 16)
-                    def _(i):
-                        rr = pl.ds(pl.multiple_of(i * 16, 16), 16)
-                        out[rr, :] = b.sum[me, rr, :].astype(F32)
-                    continue
-
-                for t in range(p.Z):
-                    def last(buf=buf, key=key, out=out, t=t):
+                        self.add((S, q, 0), (S, q, 0), (buf, t, 0), rows=r)
+
+                    if hop > 0:
+                        pl.when(here)(relay)
+                    self.send(here, (key, t), k, S.at[q], buf.at[t], to)
+        if s == 4 + L - 1:
+            me = chip(p.z, p.y, p.x)
+            out = self.outs[k]
+
+            @pl.loop(0, r // 16)
+            def _(i):
+                rr = pl.ds(pl.multiple_of(i * 16, 16), 16)
+                out[rr, :] = S[me, rr, :].astype(F32)
+
+            for buf, key in ((b.ru, "u"), (b.rd, "d")):
+                for t in range(1, L) if key == "u" else range(0, L - 1):
+
+                    def last(buf=buf, key=key, t=t):
                         self.copy((key, t), k, buf.at[t], buf.at[t], p.me).wait_recv()
 
                         @pl.loop(0, r // 16)
@@ -720,12 +764,10 @@
                             rr = pl.ds(pl.multiple_of(i * 16, 16), 16)
                             out[rr, :] += buf[t, rr, :].astype(F32)
 
-                    if (key == "u" and t == 0) or (key == "d" and t == p.Z - 1):
-                        continue
-                    pl.when(jnp.logical_and(cond, p.z == t))(last)
+                    pl.when(p.z == t)(last)
 
     def stages(self):
-        return 6
+        return 4 + self.p.Z
 
     def finish(self):
         for cond, f in self.pend:
@@ -737,19 +779,19 @@
         self.__dict__.update(kw)
 
 
-SCATTER_BUFS = ("mine", "sum", "dx", "dy", "rx", "ry", "ru", "rd")
+SCATTER_BUFS = ("mine", "sum", "dx", "dy", "rx", "ry", "ru", "rd", "rz")
 
 
 def scatter_scratch(dims, r, w):
     Z, Y, X = dims
     chips = Z * Y * X
-    shapes = ((chips, r, w), (chips, r, w), (Z, r // 2, w), (Z, r // 2, w), (Z, r, w), (Z, r, w), (Z, r, w), (Z, r, w))
+    shapes = ((2 * Y * X, r, w), (chips, r, w), (Z, r // 2, w), (Z, r // 2, w), (Z, r, w), (Z, r, w), (Z, r, w), (Z, r, w), (4, r, w))
     return [pltpu.VMEM(s, BF16) for s in shapes]
 
 
 def scatter_sems(dims, K):
     Z = dims[0]
-    return K * (5 * Z + 2 * (Z - 1))
+    return K * (7 * Z + 4)
 
 
 def rs_kernel(dims, K, *refs):
@@ -786,7 +828,7 @@
     )(*shaped)
 
 
-KEPT = ("normed", "mpad", "e", "mixed", "kern", "vslope", "val", "base", "probs", "query", "keys", "att", "gated", "hpre", "first", "second", "uslope", "inner")
+KEPT_OLD = ("normed", "mpad", "e", "mixed", "kern", "vslope", "val", "base", "probs", "query", "keys", "att", "gated", "hpre", "first", "second", "uslope", "inner")
 
 
 def kept_shapes(m):
@@ -795,7 +837,7 @@
     return dict(
         normed=b(m, D), mpad=f(seqs, STRETCH + 8, D), e=f(m, D), mixed=b(m, D), kern=f(STRETCH, D),
         vslope=b(m, VALUE_WIDTH), val=b(m, VALUE_WIDTH), base=f(m, MXW), probs=f(m, STRETCH),
-        query=b(m, Z), keys=b(m, Z), att=f(m, VALUE_WIDTH), gated=b(m, VALUE_WIDTH), hpre=f(m, D),
+        query=b(m, Z), keys=b(m, Z), upd=f(m, D), lat=f(m, Z), res=b(m, VALUE_WIDTH), ars=b(m, VALUE_WIDTH), gated=b(m, VALUE_WIDTH), hpre=f(m, D),
         first=f(m, D), second=b(m, D), uslope=b(m, FF), inner=b(m, FF),
     )
 
@@ -805,10 +847,22 @@
 
 
 def weight_grad(a, b, n, out, stage, sem, lo=0):
-    count = out.shape[0] // TILE
-
-    def copy(i, slot):
-        return pltpu.make_async_copy(stage.at[slot, :, 0:n], out.at[pl.ds(pl.multiple_of(i * TILE, TILE), TILE)], sem.at[slot])
+    flat = len(out.shape) == 2
+    r = out.shape[-2]
+    block = stage.shape[1]
+    count = (out.shape[0] if flat else out.shape[0] * 2 * r) // block
+    per = block // r
+
+    def start(i, slot):
+        if flat:
+            pltpu.make_async_copy(stage.at[slot, :, 0:n], out.at[pl.ds(pl.multiple_of(i * block, block), block)], sem.at[slot]).start()
+        for q in range(0 if flat else per):
+            d = i * per + q
+            pltpu.make_async_copy(stage.at[slot, pl.ds(q * r, r), 0:n], out.at[d // 2, d % 2], sem.at[slot]).start()
+
+    def wait(slot):
+        whole = stage.at[slot, :, 0:n]
+        pltpu.make_async_copy(whole, whole, sem.at[slot]).wait()
 
     @pl.loop(0, count // 2)
     def _(j):
@@ -817,16 +871,16 @@
 
             @pl.when(j > 0)
             def _():
-                copy(i - 2, slot).wait()
-
-            rows = a[:, pl.ds(pl.multiple_of(i * TILE, TILE), TILE)]
+                wait(slot)
+
+            rows = a[:, pl.ds(pl.multiple_of(i * block, block), block)]
             for c in range(0, n, 1024):
                 wd = min(1024, n - c)
                 stage[slot, :, c : c + wd] = dot(rows, b[:, lo + c : lo + c + wd], 0, 0).astype(BF16)
-            copy(i, slot).start()
+            start(i, slot)
 
     for slot in range(2):
-        copy(count - 2 + slot, slot).wait()
+        wait(slot)
 
 
 def own_shapes(m):
@@ -882,152 +936,456 @@
         lo = O_EMA // 128 + j * D * H // 128
         full[lo : lo + 128, :] = jnp.concatenate([e[:, k * 128 : (k + 1) * 128] for k in range(8)], axis=0).T
     for d, r in enumerate(frames(n, count)):
-        out[d * SMALL_ROWS : d * SMALL_ROWS + FRAME, :] = full[r : r + FRAME, :].astype(BF16)
-        out[d * SMALL_ROWS + FRAME : (d + 1) * SMALL_ROWS, :] = jnp.zeros((SMALL_ROWS - FRAME, 128), BF16)
-
-
-class Skip:
-    def step(self):
-        pass
-
-
-def mega_kernel(dims, n, count, K, *refs):
-    x, g, valid = refs[:3]
-    ins = refs[3 : 3 + K]
-    refs = refs[3 + K :]
-    out, dxo, gsmall = refs[:3]
-    grads = refs[3:8]
-    full_w = refs[8 : 8 + K] if dims else ins
-    refs = refs[8 + K :] if dims else refs[8:]
-    ks, own = KEPT, own_shapes(x.shape[0])
-    s = Names(**dict(zip(ks, refs[: len(ks)])))
-    refs = refs[len(ks) :]
-    t = Names(**dict(zip(own, refs[: len(own)])))
-    t.dup, t.dsec = s.inner, t.dn
-    refs = refs[len(own) :]
-    wr, wc, wv, stage, full, packed, prow, ema, grow, gema, lsem, ssem = refs[:12]
-    hsmall, hv, hmx, hh, hup, hdown = full_w
-
-    def loader(i, a, b):
-        return pltpu.make_async_copy(a, b, lsem.at[i])
-
+        out[d // 2, d % 2, 0:FRAME, :] = full[r : r + FRAME, :].astype(BF16)
+        out[d // 2, d % 2, FRAME:SMALL_ROWS, :] = jnp.zeros((SMALL_ROWS - FRAME, 128), BF16)
+
+
+def size_table(n, count, m):
+    rows = -(-(-(-(n * count) // 128) + FRAME) // 8) * 8
+    table = {k: v for k, v in list(kept_shapes(m).items()) + list(own_shapes(m).items())}
+    table.update(
+        out=((m, D), BF16), dxo=((m, D), BF16), grow=((1, O_EMA), F32), prow=((1, O_EMA), F32), ema=((4, H, D), F32),
+        gema=((4, H, D), F32), full=((rows, 128), F32), packed=((n * SMALL_ROWS, 128), BF16),
+        gsmall=((n // 2, 2, SMALL_ROWS, 128), BF16), wr=((FF, D), BF16), wc=((D, MXW), BF16), wv=((D, VALUE_WIDTH), BF16),
+        wup=((D, FF), BF16), stage=((2, TILE // 2, MXW), BF16),
+    )
+    return table
+
+
+class Parts:
+    def __init__(self, refs):
+        self.refs = list(refs)
+
+    def take(self, names):
+        got, self.refs = self.refs[: len(names)], self.refs[len(names) :]
+        return dict(zip(names, got))
+
+    def rest(self, k):
+        got, self.refs = self.refs[:k], self.refs[k:]
+        return got
+
+
+SAVED = dict(
+    front=("inner", "uslope", "first", "hpre", "second", "dd", "upd", "lat", "res", "ars", "gated", "val", "vslope", "probs", "query", "keys", "mixed", "normed", "e", "mpad", "kern", "grow", "prow", "ema"),
+    mid=("dbase", "dv", "dx", "grow"),
+    back=(),
+)
+LOADED = dict(
+    mid=("inner", "uslope", "first", "hpre", "second", "dd", "upd", "lat", "res", "ars", "gated", "val", "vslope", "probs", "query", "keys", "grow", "prow"),
+    back=("dbase", "dv", "dx", "grow", "mixed", "normed", "e", "mpad", "kern", "prow", "ema"),
+)
+HELD = dict(
+    front=SAVED["front"] + ("base", "full", "packed", "wr", "wc", "wv", "stage"),
+    mid=LOADED["mid"] + ("dbase", "dn", "acc", "wr", "wup", "stage"),
+    back=LOADED["back"] + ("dpad", "dn", "dkern", "acc", "gema", "full", "gsmall", "wc", "wv", "stage"),
+)
+
+
+class Store:
+    def __init__(self, kind, r, ins, outs):
+        held = r.take(HELD[kind])
+        self.s = Names(**held)
+        self.held = held
+        self.ins, self.outs = ins, outs
+        self.in_sem, self.out_sem = r.rest(2)
+        self.names_in, self.names_out = list(ins), list(outs)
+        self.seen, self.begun = set(), []
+
+    def fetch(self):
+        for k in self.names_in:
+            self.copy_in(k).start()
+
+    def copy_in(self, k):
+        return pltpu.make_async_copy(self.ins[k], self.held[k], self.in_sem.at[self.names_in.index(k)])
+
+    def need(self, *names):
+        for k in names:
+            if k not in self.seen:
+                self.copy_in(k).wait()
+                self.seen.add(k)
+
+    def copy_out(self, k):
+        return pltpu.make_async_copy(self.held[k], self.outs[k], self.out_sem.at[self.names_out.index(k)])
+
+    def save(self, *names):
+        for k in names:
+            self.copy_out(k).start()
+            self.begun.append(k)
+
+    def close(self):
+        self.need(*self.names_in)
+        self.save(*[k for k in self.names_out if k not in self.begun])
+        for k in self.begun:
+            self.copy_out(k).wait()
+
+
+def front_kernel(dims, n, count, *refs):
+    r = Parts(refs)
+    x, g, valid = r.rest(3)
+    ins = r.rest(6)
+    outs = r.take(SAVED["front"])
+    gdown = r.rest(1)[0]
+    whole = [None] + r.rest(5) if dims else ins
+    st = Store("front", r, {}, outs)
+    s = st.s
+    lsem, ssem = r.rest(2)
+    small = pltpu.make_async_copy(ins[0], s.packed, lsem.at[0])
     if dims:
+        osem, gsend, grecv, send_sem, recv_sem = r.rest(5)
         p = Place(dims)
-        p.barrier()
-        osem, send_sem, recv_sem = refs[12:]
-        gat = Gather(p, ins, full_w, send_sem, recv_sem)
-        cps = [pltpu.make_async_copy(ins[k], full_w[k].at[pl.ds(p.me * ins[k].shape[0], ins[k].shape[0])], osem.at[k]) for k in range(K)]
+        p.barrier_all(n)
+        mine = pl.ds(p.me * SMALL_ROWS, SMALL_ROWS)
+        own = pltpu.make_async_copy(ins[0], s.packed.at[mine], lsem.at[0])
+        own.start()
+
+        def tell(i, dev, block):
+            return pltpu.make_async_remote_copy(
+                src_ref=ins[0], dst_ref=s.packed.at[pl.ds(block * SMALL_ROWS, SMALL_ROWS)], send_sem=gsend.at[i], recv_sem=grecv.at[i],
+                device_id=(dev,), device_id_type=MESH,
+            )
+
+        @pl.loop(1, n)
+        def _(i):
+            tell(i, (p.me + i) % n, p.me).start()
+
+        gat = Gather(p, ins[1:], whole[1:], send_sem, recv_sem)
+        cps = [pltpu.make_async_copy(i, o.at[pl.ds(p.me * i.shape[0], i.shape[0])], osem.at[k]) for k, (i, o) in enumerate(zip(ins[1:], whole[1:]))]
         for cp in cps:
             cp.start()
-        S = gat.stages()
+        last = gat.stages() - 1
 
         def step(t):
-            for k in range(K):
-                if 0 <= t - k < S:
+            for k in range(5):
+                if 0 <= t - k <= last:
                     gat.stage(k, t - k)
-                    if t - k == S - 1:
+                    if t - k == last:
                         cps[k].wait()
+
+        def small_here():
+            own.wait()
+
+            @pl.loop(1, n)
+            def _(i):
+                tell(i, p.me, (p.me - i + n) % n).wait()
     else:
-        S = 7
-
-        def step(t):
-            pass
-
-    w = Names(v=wv, mx=wc, h=wr.at[0:VALUE_WIDTH], up=wc.at[:, 0:FF], down=wr)
-    f = Forward(x, valid, prow, ema, w, s)
-    b = Backward(x, g, valid, prow, ema, w, s, t, grow, gema)
-    gv, gmx, gh, gup, gdown = grads
-    l_small = loader(0, hsmall, packed)
-    l_v = loader(1, hv, wv)
-    l_mx = loader(2, hmx, wc)
-    l_h = loader(3, hh, wr.at[0:VALUE_WIDTH])
-    l_up = loader(4, hup, wc.at[:, 0:FF])
-    l_down = loader(5, hdown, wr)
-
-    for i in range(S):
-        step(i)
-    l_small.start()
-    l_small.wait()
-    unpack_params(n, count, packed, full, prow, ema)
+        step = lambda t: None
+
+        def small_here():
+            small.start()
+            small.wait()
+
+    S = dims[0] + 2 if dims else 6
+    w = Names(v=s.wv, mx=s.wc, h=s.wr.at[0:VALUE_WIDTH], up=s.wc.at[:, 0:FF])
+    into = (None, s.wv, s.wc, s.wr.at[0:VALUE_WIDTH], s.wc.at[:, 0:FF])
+    load = [None] + [pltpu.make_async_copy(whole[i], into[i], lsem.at[i]) for i in range(1, 5)]
+    f = Forward(x, valid, s.prow, s.ema, w, s)
+    b = Backward(x, g, valid, s.prow, s.ema, w, s, s, s.grow, None)
+    b.grow[...] = jnp.zeros(b.grow.shape, F32)
+    step(0)
+    b.cot()
+    step(1)
+    small_here()
+    unpack_params(n, count, s.packed, s.full, s.prow, s.ema)
     f.norm_one()
+    step(2)
     f.ema_kernel()
+    step(3)
+    f.smooth(0)
+    step(4)
+    f.smooth(1)
+    f.mix()
+    st.save("normed", "mixed", "e", "mpad", "kern", "prow", "ema", "dd", "grow")
+    for t in range(5, S):
+        step(t)
     step(S)
-    l_v.start()
-    f.smooth()
-    f.mix()
-    l_v.wait()
+    load[1].start()
+    load[1].wait()
+    f.values()
+    st.save("val", "vslope")
     step(S + 1)
-    l_mx.start()
-    f.values()
-    l_mx.wait()
+    load[2].start()
+    load[2].wait()
     f.base()
+    f.attend()
+    st.save("lat", "res", "ars", "gated", "probs", "query", "keys")
     step(S + 2)
-    l_h.start()
-    f.attend()
-    l_h.wait()
+    load[3].start()
+    load[3].wait()
     f.hidden()
+    st.save("first", "hpre", "upd")
     f.norm_two()
+    st.save("second")
     step(S + 3)
-    l_up.start()
-    b.cot()
-    l_up.wait()
+    load[4].start()
+    load[4].wait()
     f.up()
-    weight_grad(s.inner, t.dd, D, gdown, stage, ssem)
+    st.save("inner", "uslope")
+    weight_grad(s.inner, s.dd, D, gdown, s.stage, ssem)
     step(S + 4)
-    l_down.start()
-    l_down.wait()
-    f.down(out)
-    b.d_up()
-    l_h.start()
-    weight_grad(s.second, t.dup, FF, gup, stage, ssem)
-    b.d_second()
-    l_mx.start()
-    b.norm_two()
-    weight_grad(s.gated, t.dbase, D, gh, stage, ssem, lo=C_HX)
-    l_h.wait()
-    b.d_gated()
-    b.attend()
-    weight_grad(s.mixed, t.dbase, MXW, gmx, stage, ssem)
-    weight_grad(s.normed, t.dv, VALUE_WIDTH, gv, stage, ssem)
-    l_mx.wait()
-    b.d_mixed()
-    b.d_normed()
-    b.smooth()
-    b.norm_one(dxo)
-    b.ema_grads()
-    pack_grads(n, count, grow, gema, full, gsmall)
     if dims:
         gat.finish()
-
-
-def mega(dims, n, count, x, g, valid, arrays, cid):
-    m, K = x.shape[0], len(arrays)
+    st.close()
+
+
+def make_scatter(dims, parts, grads, outs):
+    nb = len(SCATTER_BUFS)
+    bufs = [Names(**dict(zip(SCATTER_BUFS, parts.rest(nb)))) for _ in grads]
+    p = Place(dims)
+    p.barrier()
+    return Scatter(p, grads, bufs, outs, *parts.rest(3))
+
+
+def columns(ref, w):
+    pieces, lo = [], 0
+    for q in w:
+        pieces.append(ref.at[(slice(None),) * (len(ref.shape) - 1) + (pl.ds(lo, q),)])
+        lo += q
+    return pieces
+
+
+def mid_kernel(dims, *refs):
+    r = Parts(refs)
+    x, g, valid, h, up, down = r.rest(6)
+    gdown = r.rest(1)[0]
+    ins = r.take(LOADED["mid"])
+    out = r.rest(1)[0]
+    outs = r.take(SAVED["mid"])
+    gup, gh = r.rest(2)
+    reduced = r.rest(2) if dims else []
+    st = Store("mid", r, ins, outs)
+    s = st.s
+    s.datt, s.dv, s.dx, s.dup, s.dsec = s.gated, s.vslope, s.first, s.inner, s.dn
+    st.held.update(dv=s.dv, dx=s.dx)
+    lsem, ssem = r.rest(2)
+    load_down = pltpu.make_async_copy(down, s.wr, lsem.at[0])
+    load_up = pltpu.make_async_copy(up, s.wup, lsem.at[1])
+    load_h = pltpu.make_async_copy(h, s.wr.at[0:VALUE_WIDTH], lsem.at[2])
+    load_down.start()
+    st.fetch()
+    load_up.start()
+    if dims:
+        cut = ((D // 2, D // 2), (FF // 2, FF // 2))
+        grads = columns(gdown, cut[0]) + columns(gup, cut[1])
+        sc = make_scatter(dims, r, grads, columns(reduced[0], cut[0]) + columns(reduced[1], cut[1]))
+        S = sc.stages()
+        late = 3
+        start = (0, 1, late, late + 1)
+
+        def step(t):
+            for k in range(4):
+                if 0 <= t - start[k] < S:
+                    sc.stage(k, t - start[k])
+    else:
+        S, late = 8, 3
+        step = lambda t: None
+    w = Names(h=s.wr.at[0:VALUE_WIDTH], up=s.wup, down=s.wr)
+    f = Forward(x, valid, s.prow, None, w, s)
+    b = Backward(x, g, valid, s.prow, None, w, s, s, s.grow, None)
+    step(0)
+    st.need("inner", "uslope", "first", "dd", "prow", "grow")
+    load_down.wait()
+    f.down(out)
+    step(1)
+    b.d_up()
+    load_h.start()
+    step(2)
+    st.need("second")
+    weight_grad(s.second, s.dup, FF, gup, s.stage, ssem)
+    step(3)
+    load_up.wait()
+    b.d_second()
+    step(4)
+    st.need("hpre", "upd")
+    b.norm_two()
+    st.save("dx")
+    step(5)
+    st.need("gated")
+    weight_grad(s.gated, s.dbase, D, gh, s.stage, ssem, lo=C_HX)
+    step(6)
+    load_h.wait()
+    st.need("res", "ars")
+    b.d_gated()
+    step(7)
+    st.need("lat", "val", "vslope", "probs", "query", "keys")
+    b.attend()
+    st.save("dbase", "dv", "grow")
+    for t in range(8, late + 1 + S):
+        step(t)
+    if dims:
+        sc.finish()
+    st.close()
+
+
+def back_kernel(dims, n, count, *refs):
+    r = Parts(refs)
+    x, valid, v, mx = r.rest(4)
+    gh = r.rest(1)[0]
+    ins = r.take(LOADED["back"])
+    dxo = r.rest(1)[0]
+    gmx, gv = r.rest(2)
+    reduced = r.rest(4) if dims else r.rest(1)
+    st = Store("back", r, ins, {})
+    s = st.s
+    lsem, ssem = r.rest(2)
+    l_mx = pltpu.make_async_copy(mx, s.wc, lsem.at[0])
+    l_v = pltpu.make_async_copy(v, s.wv, lsem.at[1])
+    st.fetch()
+    l_mx.start()
+    l_v.start()
+    start = (0, 2, 3, 2, 10)
+    if dims:
+        cut = (VALUE_WIDTH, MXW - VALUE_WIDTH)
+        split = (n // 2, 2, D // n)
+        gmx4, gv4 = gmx, gv
+        grads = [gh] + columns(gmx4, cut) + [gv4, s.gsmall]
+        sc = make_scatter(dims, r, grads, [reduced[0]] + columns(reduced[1], cut) + [reduced[2], reduced[3]])
+        S = sc.stages()
+
+        def step(t):
+            for k in range(5):
+                if 0 <= t - start[k] < S:
+                    sc.stage(k, t - start[k])
+    else:
+        S = 8
+        step = lambda t: None
+    b = Backward(x, None, valid, s.prow, s.ema, Names(mx=s.wc, v=s.wv), s, s, s.grow, s.gema)
+    step(0)
+    st.need("dv", "normed", "prow", "grow")
+    weight_grad(s.normed, s.dv, VALUE_WIDTH, gv, s.stage, ssem)
+    step(1)
+    st.need("dbase", "mixed")
+    weight_grad(s.mixed, s.dbase, MXW, gmx, s.stage, ssem)
+    step(2)
+    l_mx.wait()
+    st.need("e", "mpad")
+    b.d_mixed()
+    step(3)
+    l_v.wait()
+    b.d_normed()
+    step(4)
+    st.need("kern")
+    b.smooth_signal(0)
+    step(5)
+    b.smooth_signal(1)
+    step(6)
+    b.smooth_filter()
+    step(7)
+    st.need("ema")
+    b.ema_grads()
+    step(8)
+    st.need("dx")
+    b.norm_one(dxo)
+    step(9)
+    pack_grads(n, count, s.grow, s.gema, s.full, s.gsmall)
+    for t in range(10, start[4] + S):
+        step(t)
+    if dims:
+        sc.finish()
+    else:
+        reduced[0][...] = s.gsmall[...]
+    st.close()
+
+
+def scatter_parts(dims, shapes):
+    scratch = []
+    for q in shapes:
+        scratch += scatter_scratch(dims, q[0], q[1])
+    ns = scatter_sems(dims, len(shapes))
+    return scratch + [pltpu.SemaphoreType.DMA((ns,)), pltpu.SemaphoreType.DMA((ns,)), pltpu.SemaphoreType.DMA((len(shapes) * dims[0],))]
+
+
+def run_kernel(body, ins, outs, scratch, cid):
     vm, hbm = pl.BlockSpec(memory_space=VM), pl.BlockSpec(memory_space=pl.ANY)
+    params = dict(vmem_limit_bytes=LIMIT)
+    if cid is not None:
+        params.update(collective_id=cid, has_side_effects=True)
+    return pl.pallas_call(
+        body,
+        out_shape=[jax.ShapeDtypeStruct(o[0], o[1]) for o in outs],
+        in_specs=[vm if i[1] else hbm for i in ins],
+        out_specs=[vm if o[2] else hbm for o in outs],
+        scratch_shapes=scratch,
+        compiler_params=pltpu.CompilerParams(**params),
+    )(*[i[0] for i in ins])
+
+
+def copy_kernel(k, *refs):
+    ins, outs, bufs, sem = refs[:k], refs[k : 2 * k], refs[2 * k : 3 * k], refs[3 * k]
+    get = [pltpu.make_async_copy(a, b, sem.at[i]) for i, (a, b) in enumerate(zip(ins, bufs))]
+    put = [pltpu.make_async_copy(a, b, sem.at[k + i]) for i, (a, b) in enumerate(zip(bufs, outs))]
+    for c in get:
+        c.start()
+    for c, d in zip(get, put):
+        c.wait()
+        d.start()
+    for d in put:
+        d.wait()
+
+
+def settle(arrays):
+    return run_kernel(
+        functools.partial(copy_kernel, len(arrays)), [(a, False) for a in arrays], [(a.shape, a.dtype, False) for a in arrays],
+        [VM(a.shape, a.dtype) for a in arrays] + [pltpu.SemaphoreType.DMA((2 * len(arrays),))], None,
+    )
+
+
+def layer(dims, n, count, x, g, valid, arrays):
+    m = x.shape[0]
+    table = size_table(n, count, m)
+    dma = pltpu.SemaphoreType.DMA
+    tmp = lambda names: [VM(*table[k]) for k in names]
+    saved = lambda kind: [table[k] + (False,) for k in SAVED[kind]]
     whole = [(n * a.shape[0], a.shape[1]) if dims else a.shape for a in arrays]
-    outs = [((m, D), BF16), ((m, D), BF16), ((n * SMALL_ROWS, 128), BF16)] + [(s, BF16) for s in whole[1:]]
-    specs = [vm] * 3 + [hbm] * 5
-    sems = [pltpu.SemaphoreType.DMA((K,)), pltpu.SemaphoreType.DMA((2,))]
-    params = dict(vmem_limit_bytes=LIMIT)
+    parts = [(q[0] // n, q[1]) for q in whole]
+    split = lambda a: a.reshape(n // 2, 2, a.shape[0] // n, a.shape[1])
+    four = lambda i: (n // 2, 2) + parts[i]
+    held = lambda kind, k: tmp(HELD[kind]) + [dma((max(1, len(LOADED.get(kind, ()))),)), dma((max(1, len(SAVED[kind])),))] + [dma((k,)), dma((2,))]
+    a = {}
+
+    scratch = held("front", 6)
+    o = saved("front") + [(whole[5], BF16, False)]
     if dims:
-        outs += [(s, BF16) for s in whole]
-        specs += [hbm] * K
-        ns = sems_needed(dims, K)
-        sems += [pltpu.SemaphoreType.DMA((K,)), pltpu.SemaphoreType.DMA((ns,)), pltpu.SemaphoreType.DMA((ns,))]
-        params.update(collective_id=cid, has_side_effects=True)
-    rows = -(-(n * count) // 128) + FRAME
-    scratch = [VM(*v) for v in kept_shapes(m).values()] + [VM(*v) for v in own_shapes(m).values()]
-    scratch += [VM((FF, D), BF16), VM((D, MXW), BF16), VM((D, VALUE_WIDTH), BF16), VM((2, TILE, MXW), BF16)]
-    scratch += [VM((-(-rows // 8) * 8, 128), F32), VM((n * SMALL_ROWS, 128), BF16)]
-    scratch += [VM((1, O_EMA), F32), VM((4, H, D), F32), VM((1, O_EMA), F32), VM((4, H, D), F32)]
-    res = pl.pallas_call(
-        functools.partial(mega_kernel, dims, n, count, K),
-        out_shape=[jax.ShapeDtypeStruct(*o) for o in outs],
-        in_specs=[vm] * 3 + [hbm] * K,
-        out_specs=specs,
-        scratch_shapes=scratch + sems,
-        compiler_params=pltpu.CompilerParams(**params),
-    )(x, g, valid, *arrays)
-    return res[0], res[1], res[2], res[3:8]
+        ns = sems_needed(dims, 5)
+        scratch += [dma((5,)), dma((n,)), dma((n,)), dma((ns,)), dma((ns,))]
+        o += [(q, BF16, False) for q in whole[1:]]
+    ins = [(x, True), (g, True), (valid, True)] + [(q, False) for q in arrays]
+    res = run_kernel(functools.partial(front_kernel, dims, n, count), ins, o, scratch, 0 if dims else None)
+    a.update(zip(SAVED["front"], res))
+    res = res[len(SAVED["front"]) :]
+    gdown = res[0]
+    v, mx, h, up, down = res[1:] if dims else arrays[1:]
+
+    ins = [(x, True), (g, True), (valid, True), (h, False), (up, False), (down, False), (split(gdown), False)]
+    ins += [(a[k], False) for k in LOADED["mid"]]
+    o = [((m, D), BF16, True)] + saved("mid") + [(four(4), BF16, False), (four(3), BF16, False)]
+    scratch = held("mid", 3)
+    if dims:
+        o += [(parts[5], F32, True), (parts[4], F32, True)]
+        scratch += scatter_parts(dims, ((parts[5][0], D // 2),) * 2 + ((parts[4][0], FF // 2),) * 2)
+    res = run_kernel(functools.partial(mid_kernel, dims), ins, o, scratch, 1 if dims else None)
+    out = res[0]
+    a.update(zip(SAVED["mid"], res[1:]))
+    gup, gh = res[5:7]
+    if dims:
+        gdown, gup = res[7:]
+
+    ins = [(x, True), (valid, True), (v, False), (mx, False), (gh, False)] + [(a[k], False) for k in LOADED["back"]]
+    o = [((m, D), BF16, True), (four(2), BF16, False), (four(1), BF16, False)]
+    scratch = held("back", 2)
+    if dims:
+        o += [(parts[i], F32, True) for i in (3, 2, 1)] + [((SMALL_ROWS, 128), F32, True)]
+        rows = parts[2][0]
+        scratch += scatter_parts(dims, (parts[3], (rows, VALUE_WIDTH), (rows, MXW - VALUE_WIDTH), parts[1], (SMALL_ROWS, 128)))
+    else:
+        o += [table["gsmall"] + (True,)]
+    res = run_kernel(functools.partial(back_kernel, dims, n, count), ins, o, scratch, 2 if dims else None)
+    if dims:
+        gh, gmx, gv, gs = res[3:]
+    else:
+        gmx, gv = res[1:3]
+        gs = res[3]
+        gv, gmx, gh, gup, gs = (q.reshape(-1, q.shape[-1]) for q in (gv, gmx, gh, gup, gs))
+    return out, res[0], gv, gmx, gh, gup, gdown, gs
 
 
 def frame_in(small, me):
@@ -1055,12 +1413,12 @@
     dims = grid_of(n) if n == 32 else None
     if not dims:
         arrays = [lax.all_gather(a, "fsdp", axis=0, tiled=True) for a in arrays]
-    out, dx, small, (gv, gmx, gh, gup, gdown) = mega(dims, n, count, x, g, valid, arrays, 0)
+    out, dx, gv, gmx, gh, gup, gdown, gs = layer(dims, n, count, x, g, valid, arrays)
     if dims:
-        gdown, gup, gh, gmx, gv, gs = scatter(dims, (gdown, gup, gh, gmx, gv, small), 1)
+        out, dx, gv, gmx, gh, gup, gdown = settle((out, dx, gv, gmx, gh, gup, gdown))
     else:
         gv, gmx, gh, gup, gdown, gs = (
-            lax.psum_scatter(a.astype(F32), "fsdp", scatter_dimension=0, tiled=True) for a in (gv, gmx, gh, gup, gdown, small)
+            lax.psum_scatter(a.astype(F32), "fsdp", scatter_dimension=0, tiled=True) for a in (gv, gmx, gh, gup, gdown, gs)
         )
     return out.reshape(shape), dx.reshape(shape), gv, gmx, gh, gup, gdown, frame_out(gs, me, count)
 

time: 474 us -> 394 us (0.83)
  Pallas kernels: 456 us -> 388 us
  local copies, waits for them, and re-layouts: 16.4 us -> 3.65 us
    pallas_call x2 -> x4, Pallas kernels: 456 us -> 388 us  [run_kernel(): pl.pallas_call(body, out_shape=[jax.ShapeDtypeStruct(o[0], o[1]) for o in...]
    unnamed x7 -> x0, local copies, waits for them, and re-layouts: 12.7 us -> none
where the time goes in v4:
time: 394 us; the launch traced here: 393 us
  Pallas kernels  388 us (98%)
    pallas_call x4, Pallas kernels, run_kernel(): pl.pallas_call(body, out_shape=[jax.ShapeDtypeStruct(o[0], o[1]) for o in...  388 us

profile of v4, /device:TPU:0, one launch (start us, length us, event | category | flops | bytes accessed | tf_op | source)
XLA Modules:
  0.0 392.9 jit_solution(12529958829995441324)
XLA Ops:
  0.7 0.7 compare_convert_fusion
  1.4 0.9 dynamic_update_slice.3
  2.3 0.6 pad.4.refs_3_
  2.9 0.8 broadcast_in_dim.4.refs_2_.refs_1_
  3.6 186.6 %shard_map.155 = (bf16[256,4096]{1,0:T(8,128)(2,1)}, bf16[256,4096]{1,0:T(8,128)(2,1)}, f32[256,1024]{1,0:T(8,128)}, f32[256,1024]{1,0:T(8,128)}, bf16[256,1024]...) custom-call(bf16[256,1024]{1,0:T(8,128)(2,1)} %bitcast.14, ...), custom_call_target="tpu_custom_call" | custom-call | tf_op jit(solution)/shard_map/pallas_call | solution.py:1302
  190.2 90.1 %shard_map.156 = (bf16[256,1024]{1,0:T(8,128)(2,1)}, bf16[256,4224]{1,0:T(8,128)(2,1)}, bf16[256,2048]{1,0:T(8,128)(2,1)}, f32[256,1024]{1,0:T(8,128)}, f32[1,18...) custom-call(bf16[256,1024]{1,0:T(8,128)(2,1)} %bitcast.15, ...), custom_call_target="tpu_custom_call" | custom-call | tf_op jit(solution)/shard_map/pallas_call | solution.py:1302
  280.3 108.4 %shard_map.157 = (bf16[256,1024]{1,0:T(8,128)(2,1)}, bf16[16,2,32,4224]{3,2,1,0:T(8,128)(2,1)}, bf16[16,2,32,2048]{3,2,1,0:T(8,128)(2,1)}, f32[64,1024]{1,0:T(8,...) custom-call(bf16[256,1024]{1,0:T(8,128)(2,1)} %bitcast.16, ...), custom_call_target="tpu_custom_call" | custom-call | tf_op jit(solution)/shard_map/pallas_call | solution.py:1302
  388.7 2.8 shard_map.158
  391.5 1.4 dynamic_slice.3
  (1 shorter events, 0.0 us)

commit v5 on v4

--- a/solution.py
+++ b/solution.py
@@ -361,16 +361,6 @@
 
         tiles(0, FF, TILE, one)
 
-    def down(self, out):
-        s = self.s
-
-        def one(col):
-            cols = pl.ds(col, TILE)
-            d = dot(s.inner[...], self.w.down[:, cols]) + self.pd(O_DNB, col, TILE)
-            out[:, cols] = (s.first[:, cols] + self.valid[:, 0:1] * d).astype(BF16)
-
-        tiles(0, D, TILE, one)
-
 
 class Backward:
     def __init__(self, x, g, valid, prow, ema, w, s, t, grow, gema):
@@ -393,26 +383,27 @@
 
         tiles(0, D, TILE, one)
 
-    def d_up(self):
+    def down_tile(self, col, w):
+        s, t = self.s, self.t
+        cols = pl.ds(col, TILE)
+        t.dn[...] += dot(s.inner[:, cols], w[...])
+        di = dot(t.dd[...], w[...], 1, 1)
+        du = di * s.uslope[:, cols].astype(F32)
+        self.put(O_UPB, col, TILE, col_sum(du))
+        t.dup[:, cols] = du.astype(BF16)
+
+    def output(self, out):
         s, t = self.s, self.t
 
         def one(col):
             cols = pl.ds(col, TILE)
-            di = dot(t.dd[...], self.w.down[cols, :], 1, 1)
-            du = di * s.uslope[:, cols].astype(F32)
-            self.put(O_UPB, col, TILE, col_sum(du))
-            t.dup[:, cols] = du.astype(BF16)
-
-        tiles(0, FF, TILE, one)
-
-    def d_second(self):
-        t = self.t
-
-        def one(col):
-            cols = pl.ds(col, TILE)
-            t.dsec[:, cols] = dot(t.dup[...], self.w.up[cols, :], 1, 1)
+            d = t.dn[:, cols] + self.pd(O_DNB, col, TILE)
+            out[:, cols] = (s.first[:, cols] + self.valid[:, 0:1] * d).astype(BF16)
 
         tiles(0, D, TILE, one)
+
+    def second_tile(self, col, w):
+        self.t.dsec[:, pl.ds(col, TILE)] = dot(self.t.dup[...], w[...], 1, 1)
 
     def norm_two(self):
         s, t = self.s, self.t
@@ -450,19 +441,15 @@
             self.grow[:, lo : lo + D] = col_sum(t.acc[k])
         self.grow[:, O_MXB + C_HX : O_MXB + MXW] = col_sum(t.acc[3])
 
-    def d_gated(self):
+    def gated_tile(self, col, w):
         s, t = self.s, self.t
-
-        def one(col):
-            cols = pl.ds(col, TILE)
-            bcols = pl.ds(pl.multiple_of(C_RES + col, 128), TILE)
-            dg = dot(t.dbase[:, C_HX:MXW], self.w.h[cols, :], 1, 1)
-            t.datt[:, cols] = (dg * s.res[:, cols].astype(F32)).astype(BF16)
-            db = dg * s.ars[:, cols].astype(F32)
-            self.put(O_MXB + C_RES, col, TILE, col_sum(db))
-            t.dbase[:, bcols] = db.astype(BF16)
-
-        tiles(0, VALUE_WIDTH, TILE, one)
+        cols = pl.ds(col, TILE)
+        bcols = pl.ds(pl.multiple_of(C_RES + col, 128), TILE)
+        dg = dot(t.dbase[:, C_HX:MXW], w[...], 1, 1)
+        t.datt[:, cols] = (dg * s.res[:, cols].astype(F32)).astype(BF16)
+        db = dg * s.ars[:, cols].astype(F32)
+        self.put(O_MXB + C_RES, col, TILE, col_sum(db))
+        t.dbase[:, bcols] = db.astype(BF16)
 
     def attend(self):
         s, t = self.s, self.t
@@ -515,33 +502,25 @@
 
         tiles(0, VALUE_WIDTH, TILE, one)
 
-    def d_mixed(self):
+    def pad_tail(self):
+        for q in range(self.seqs):
+            self.t.dpad[q, STRETCH : STRETCH + 8, :] = jnp.zeros((8, D), F32)
+
+    def mixed_tile(self, col, w):
         s, t = self.s, self.t
+        cols = pl.ds(col, TILE)
+        dm = dot(t.dbase[...], w[...], 1, 1)
+        e = s.e[:, cols]
+        de = dm * silu_slope(e, sigmoid(e))
+        om = 0.0
         for q in range(self.seqs):
-            t.dpad[q, STRETCH : STRETCH + 8, :] = jnp.zeros((8, D), F32)
-
-        def one(col):
-            cols = pl.ds(col, TILE)
-            dm = dot(t.dbase[...], self.w.mx[cols, :], 1, 1)
-            e = s.e[:, cols]
-            de = dm * silu_slope(e, sigmoid(e))
-            om = 0.0
-            for q in range(self.seqs):
-                d = de[q * STRETCH : (q + 1) * STRETCH, :]
-                t.dpad[q, 0:STRETCH, cols] = d
-                om = om + col_sum(d * s.mpad[q, 8 : 8 + STRETCH, cols])
-            self.put(O_OMEGA, col, TILE, om)
-
-        tiles(0, D, TILE, one)
-
-    def d_normed(self):
-        t = self.t
-
-        def one(col):
-            cols = pl.ds(col, TILE)
-            t.dn[:, cols] = dot(t.dv[...], self.w.v[cols, :], 1, 1)
-
-        tiles(0, D, TILE, one)
+            d = de[q * STRETCH : (q + 1) * STRETCH, :]
+            t.dpad[q, 0:STRETCH, cols] = d
+            om = om + col_sum(d * s.mpad[q, 8 : 8 + STRETCH, cols])
+        self.put(O_OMEGA, col, TILE, om)
+
+    def normed_tile(self, col, w):
+        self.t.dn[:, pl.ds(col, TILE)] = dot(self.t.dv[...], w[...], 1, 1)
 
     def smooth_signal(self, seq):
         s, t = self.s, self.t
@@ -628,10 +607,30 @@
 
 
 class Scatter:
-    def __init__(self, place, grads, bufs, outs, send_sem, recv_sem, local_sem):
-        self.p, self.grads, self.bufs, self.outs = place, grads, bufs, outs
+    def __init__(self, place, grads, rings, depth, outs, send_sem, recv_sem, local_sem, credit):
+        self.p, self.grads, self.outs, self.depth, self.credit = place, grads, outs, depth, credit
+        self.bufs = []
+        for k, g in enumerate(grads):
+            e, w = k % depth, pl.ds(0, g.shape[-1])
+            self.bufs.append(Names(**{name: ref.at[e, :, :, w] for name, ref in rings.items()}))
         self.ss, self.rs, self.ls = send_sem, recv_sem, local_sem
-        self.ids, self.pend = {}, []
+        self.ids, self.pend = {}, [[] for _ in grads]
+
+    def around(self):
+        p = self.p
+        return ((None, p.nc), (None, p.nx), (None, p.ny), (p.has_up, p.up), (p.has_down, p.down))
+
+    def release(self, k):
+        self.finish(k)
+        if k + self.depth < len(self.grads):
+            for i, (cond, to) in enumerate(self.around()):
+                slot = (0, 1, 2, 4, 3)[i]
+                when(cond, lambda slot=slot, to=to: pl.semaphore_signal(self.credit.at[k, slot], inc=1, device_id=(to,), device_id_type=MESH))
+
+    def admit(self, k):
+        if k >= self.depth:
+            for i, (cond, to) in enumerate(self.around()):
+                when(cond, lambda i=i: pl.semaphore_wait(self.credit.at[k - self.depth, i], 1))
 
     def copy(self, key, k, src, dst, to):
         i = self.ids.setdefault((key, k), len(self.ids))
@@ -639,7 +638,7 @@
 
     def send(self, cond, key, k, src, dst, to):
         when(cond, lambda: self.copy(key, k, src, dst, to).start())
-        self.pend.append((cond, lambda: self.copy(key, k, src, dst, to).wait_send()))
+        self.pend[k].append((cond, lambda: self.copy(key, k, src, dst, to).wait_send()))
 
     def recv(self, cond, key, k, dst):
         when(cond, lambda: self.copy(key, k, dst, dst, self.p.me).wait_recv())
@@ -676,6 +675,7 @@
         apart = lambda z: jnp.logical_and(far(z), p.z != z)
         S, H0, H1 = b.sum, 0, half
         if s == 0:
+            self.admit(k)
             for z in planes:
                 self.send(None, ("c", z), k, self.grads[k].at[pl.ds(z * layer, layer), 1 - p.c], S.at[pl.ds(z * layer, layer)], p.nc)
                 if z < 2:
@@ -746,32 +746,34 @@
                     self.send(here, (key, t), k, S.at[q], buf.at[t], to)
         if s == 4 + L - 1:
             me = chip(p.z, p.y, p.x)
-            out = self.outs[k]
-
-            @pl.loop(0, r // 16)
-            def _(i):
-                rr = pl.ds(pl.multiple_of(i * 16, 16), 16)
-                out[rr, :] = S[me, rr, :].astype(F32)
-
-            for buf, key in ((b.ru, "u"), (b.rd, "d")):
-                for t in range(1, L) if key == "u" else range(0, L - 1):
-
-                    def last(buf=buf, key=key, t=t):
-                        self.copy((key, t), k, buf.at[t], buf.at[t], p.me).wait_recv()
+            for key, buf, ts in (("", None, (0,)), ("u", b.ru, range(1, L)), ("d", b.rd, range(0, L - 1))):
+                for t in ts:
+
+                    def last(key=key, buf=buf, t=t):
+                        if buf is not None:
+                            self.copy((key, t), k, buf.at[t], buf.at[t], p.me).wait_recv()
 
                         @pl.loop(0, r // 16)
                         def _(i):
                             rr = pl.ds(pl.multiple_of(i * 16, 16), 16)
-                            out[rr, :] += buf[t, rr, :].astype(F32)
-
-                    pl.when(p.z == t)(last)
+                            v = (S[me, rr, :] if buf is None else buf[t, rr, :]).astype(F32)
+                            for out, row, col, lo, w in self.outs[k]:
+                                o = out.at[pl.ds(pl.multiple_of(row + i * 16, 16), 16), col : col + w]
+                                if buf is None:
+                                    o[...] = v[:, lo : lo + w]
+                                else:
+                                    o[...] += v[:, lo : lo + w]
+
+                    when(None if buf is None else p.z == t, last)
+            self.release(k)
 
     def stages(self):
         return 4 + self.p.Z
 
-    def finish(self):
-        for cond, f in self.pend:
+    def finish(self, k):
+        for cond, f in self.pend[k]:
             when(cond, f)
+        self.pend[k] = []
 
 
 class Names:
@@ -782,50 +784,13 @@
 SCATTER_BUFS = ("mine", "sum", "dx", "dy", "rx", "ry", "ru", "rd", "rz")
 
 
-def scatter_scratch(dims, r, w):
+def scatter_scratch(dims, r, w, depth, K):
     Z, Y, X = dims
-    chips = Z * Y * X
-    shapes = ((2 * Y * X, r, w), (chips, r, w), (Z, r // 2, w), (Z, r // 2, w), (Z, r, w), (Z, r, w), (Z, r, w), (Z, r, w), (4, r, w))
-    return [pltpu.VMEM(s, BF16) for s in shapes]
-
-
-def scatter_sems(dims, K):
-    Z = dims[0]
-    return K * (7 * Z + 4)
-
-
-def rs_kernel(dims, K, *refs):
-    grads, outs = refs[:K], refs[K : 2 * K]
-    nb = len(SCATTER_BUFS)
-    bufs = [Names(**dict(zip(SCATTER_BUFS, refs[2 * K + nb * k : 2 * K + nb * (k + 1)]))) for k in range(K)]
-    ss, rs, ls = refs[2 * K + nb * K :]
-    p = Place(dims)
-    p.barrier()
-    sc = Scatter(p, grads, bufs, outs, ss, rs, ls)
-    S = sc.stages()
-    for t in range(K + S - 1):
-        for k in range(K):
-            if 0 <= t - k < S:
-                sc.stage(k, t - k)
-    sc.finish()
-
-
-def scatter(dims, grads, cid):
-    K = len(grads)
-    n = 2 * dims[0] * dims[1] * dims[2]
-    shaped = [g.reshape(n // 2, 2, g.shape[0] // n, g.shape[1]) for g in grads]
-    scratch = []
-    for g in shaped:
-        scratch += scatter_scratch(dims, g.shape[2], g.shape[3])
-    ns = scatter_sems(dims, K)
-    return pl.pallas_call(
-        functools.partial(rs_kernel, dims, K),
-        out_shape=[jax.ShapeDtypeStruct(g.shape[2:], F32) for g in shaped],
-        in_specs=[pl.BlockSpec(memory_space=pl.ANY)] * K,
-        out_specs=[pl.BlockSpec(memory_space=pltpu.VMEM)] * K,
-        scratch_shapes=scratch + [pltpu.SemaphoreType.DMA((ns,)), pltpu.SemaphoreType.DMA((ns,)), pltpu.SemaphoreType.DMA((K * dims[0],))],
-        compiler_params=pltpu.CompilerParams(collective_id=cid, has_side_effects=True, vmem_limit_bytes=64 * 1024 * 1024),
-    )(*shaped)
+    sizes = dict(mine=(2 * Y * X, r), sum=(Z * Y * X, r), dx=(Z, r // 2), dy=(Z, r // 2), rx=(Z, r), ry=(Z, r), ru=(Z, r), rd=(Z, r), rz=(4, r))
+    ns = K * (7 * Z + 4)
+    dma = pltpu.SemaphoreType.DMA
+    scratch = [pltpu.VMEM((depth,) + sizes[k] + (w,), BF16) for k in SCATTER_BUFS]
+    return scratch + [dma((ns,)), dma((ns,)), dma((K * Z,)), pltpu.SemaphoreType.REGULAR((K, 5))]
 
 
 KEPT_OLD = ("normed", "mpad", "e", "mixed", "kern", "vslope", "val", "base", "probs", "query", "keys", "att", "gated", "hpre", "first", "second", "uslope", "inner")
@@ -846,41 +811,78 @@
 LIMIT = 64 * 1024 * 1024
 
 
-def weight_grad(a, b, n, out, stage, sem, lo=0):
-    flat = len(out.shape) == 2
-    r = out.shape[-2]
-    block = stage.shape[1]
-    count = (out.shape[0] if flat else out.shape[0] * 2 * r) // block
-    per = block // r
-
-    def start(i, slot):
-        if flat:
-            pltpu.make_async_copy(stage.at[slot, :, 0:n], out.at[pl.ds(pl.multiple_of(i * block, block), block)], sem.at[slot]).start()
-        for q in range(0 if flat else per):
-            d = i * per + q
-            pltpu.make_async_copy(stage.at[slot, pl.ds(q * r, r), 0:n], out.at[d // 2, d % 2], sem.at[slot]).start()
-
-    def wait(slot):
-        whole = stage.at[slot, :, 0:n]
+def weight_grad(a, b, out, turned, stage, sem, lo=0, start=0, stop=None, place=None):
+    stop = stop or b.shape[1] - lo
+
+    def begin(slot, i, col, w):
+        if place is None:
+            cols = pl.ds(pl.multiple_of(col, 128), w)
+            pltpu.make_async_copy(stage.at[slot, :, 0:w], out.at[pl.ds(i * D, D), cols], sem.at[slot]).start()
+            return
+        chips, pieces = place
+        src = stage.at[slot, :, 0:w].reshape(chips, 2, pieces, D // (2 * chips * pieces), w)
+        for q in range(pieces):
+            cols = pl.ds(pl.multiple_of((q % 2) * D + col, 128), w)
+            pltpu.make_async_copy(src.at[:, :, q], out.at[q // 2, pl.ds(i * chips, chips), :, :, cols], sem.at[slot]).start()
+
+    def wait(slot, w):
+        whole = stage.at[slot, :, 0:w]
         pltpu.make_async_copy(whole, whole, sem.at[slot]).wait()
 
-    @pl.loop(0, count // 2)
-    def _(j):
-        for slot in range(2):
-            i = j * 2 + slot
-
-            @pl.when(j > 0)
-            def _():
-                wait(slot)
-
-            rows = a[:, pl.ds(pl.multiple_of(i * block, block), block)]
-            for c in range(0, n, 1024):
-                wd = min(1024, n - c)
-                stage[slot, :, c : c + wd] = dot(rows, b[:, lo + c : lo + c + wd], 0, 0).astype(BF16)
-            start(i, slot)
-
-    for slot in range(2):
-        wait(slot)
+    def block(slot, i, col, w):
+        stage[slot, :, 0:w] = dot(turned[...], b[:, pl.ds(pl.multiple_of(lo + col, 128), w)]).astype(BF16)
+        begin(slot, i, col, w)
+
+    pairs = (stop - start) // (2 * TILE)
+    for i in range(a.shape[1] // D):
+        turned[...] = a[:, i * D : (i + 1) * D].T
+
+        @pl.loop(0, pairs)
+        def _(j):
+            for slot in range(2):
+
+                @pl.when(jnp.logical_or(j > 0, i > 0))
+                def _():
+                    wait(slot, TILE)
+
+                block(slot, i, start + (j * 2 + slot) * TILE, TILE)
+
+    rest = stop - start - pairs * 2 * TILE
+    wait(0, TILE)
+    if rest:
+        block(0, 0, stop - rest, rest)
+    wait(1, TILE)
+    if rest:
+        wait(0, rest)
+
+
+class Stream:
+    def __init__(self, w, ring, sem):
+        self.w, self.ring, self.sem = w, ring, sem
+        self.width = w.shape[1]
+
+    def copy(self, i, slot):
+        rows = pl.ds(pl.multiple_of(i * TILE, TILE), TILE)
+        return pltpu.make_async_copy(self.w.at[rows], self.ring.at[slot, :, 0 : self.width], self.sem.at[slot])
+
+    def prefetch(self):
+        self.copy(0, 0).start()
+        self.copy(1, 1).start()
+
+    def run(self, body, lo=0, hi=None):
+        count = self.w.shape[0] // TILE
+        hi = hi or count
+
+        @pl.loop(lo // 2, hi // 2)
+        def _(j):
+            for slot in range(2):
+                i = j * 2 + slot
+                self.copy(i, slot).wait()
+                body(pl.multiple_of(i * TILE, TILE), self.ring.at[slot, :, 0 : self.width])
+
+                @pl.when(i + 2 < count)
+                def _():
+                    self.copy(i + 2, slot).start()
 
 
 def own_shapes(m):
@@ -947,7 +949,7 @@
         out=((m, D), BF16), dxo=((m, D), BF16), grow=((1, O_EMA), F32), prow=((1, O_EMA), F32), ema=((4, H, D), F32),
         gema=((4, H, D), F32), full=((rows, 128), F32), packed=((n * SMALL_ROWS, 128), BF16),
         gsmall=((n // 2, 2, SMALL_ROWS, 128), BF16), wr=((FF, D), BF16), wc=((D, MXW), BF16), wv=((D, VALUE_WIDTH), BF16),
-        wup=((D, FF), BF16), stage=((2, TILE // 2, MXW), BF16),
+        wup=((D, FF), BF16), ring=((2, TILE, MXW), BF16), stage=((2, D, TILE), BF16), turned=((D, m), BF16), wh=((VALUE_WIDTH, D), BF16),
     )
     return table
 
@@ -965,20 +967,21 @@
         return got
 
 
+GATHER_STARTS = (0, 1, 2, 3, 4)
+LAG = GATHER_STARTS[-1]
+
 SAVED = dict(
     front=("inner", "uslope", "first", "hpre", "second", "dd", "upd", "lat", "res", "ars", "gated", "val", "vslope", "probs", "query", "keys", "mixed", "normed", "e", "mpad", "kern", "grow", "prow", "ema"),
-    mid=("dbase", "dv", "dx", "grow"),
     back=(),
 )
-LOADED = dict(
-    mid=("inner", "uslope", "first", "hpre", "second", "dd", "upd", "lat", "res", "ars", "gated", "val", "vslope", "probs", "query", "keys", "grow", "prow"),
-    back=("dbase", "dv", "dx", "grow", "mixed", "normed", "e", "mpad", "kern", "prow", "ema"),
+LOADED = dict(back=SAVED["front"])
+HELD = dict(
+    front=SAVED["front"] + ("base", "full", "packed", "wh", "wup", "wc", "wv", "stage", "turned"),
+    back=SAVED["front"] + ("dbase", "dn", "acc", "dpad", "dkern", "gema", "full", "gsmall", "ring", "stage", "turned"),
 )
-HELD = dict(
-    front=SAVED["front"] + ("base", "full", "packed", "wr", "wc", "wv", "stage"),
-    mid=LOADED["mid"] + ("dbase", "dn", "acc", "wr", "wup", "stage"),
-    back=LOADED["back"] + ("dpad", "dn", "dkern", "acc", "gema", "full", "gsmall", "wc", "wv", "stage"),
-)
+DEPTH = 4
+UNIT = 2 * D
+WIDE = MXW - UNIT
 
 
 class Store:
@@ -1029,7 +1032,7 @@
     st = Store("front", r, {}, outs)
     s = st.s
     lsem, ssem = r.rest(2)
-    small = pltpu.make_async_copy(ins[0], s.packed, lsem.at[0])
+
     if dims:
         osem, gsend, grecv, send_sem, recv_sem = r.rest(5)
         p = Place(dims)
@@ -1055,10 +1058,10 @@
         last = gat.stages() - 1
 
         def step(t):
-            for k in range(5):
-                if 0 <= t - k <= last:
-                    gat.stage(k, t - k)
-                    if t - k == last:
+            for k, q in enumerate(GATHER_STARTS):
+                if 0 <= t - q <= last:
+                    gat.stage(k, t - q)
+                    if t - q == last:
                         cps[k].wait()
 
         def small_here():
@@ -1071,12 +1074,13 @@
         step = lambda t: None
 
         def small_here():
+            small = pltpu.make_async_copy(ins[0], s.packed, lsem.at[0])
             small.start()
             small.wait()
 
     S = dims[0] + 2 if dims else 6
-    w = Names(v=s.wv, mx=s.wc, h=s.wr.at[0:VALUE_WIDTH], up=s.wc.at[:, 0:FF])
-    into = (None, s.wv, s.wc, s.wr.at[0:VALUE_WIDTH], s.wc.at[:, 0:FF])
+    w = Names(v=s.wv, mx=s.wc, h=s.wh, up=s.wup)
+    into = (None, s.wv, s.wc, s.wh, s.wup)
     load = [None] + [pltpu.make_async_copy(whole[i], into[i], lsem.at[i]) for i in range(1, 5)]
     f = Forward(x, valid, s.prow, s.ema, w, s)
     b = Backward(x, g, valid, s.prow, s.ema, w, s, s, s.grow, None)
@@ -1095,203 +1099,173 @@
     f.smooth(1)
     f.mix()
     st.save("normed", "mixed", "e", "mpad", "kern", "prow", "ema", "dd", "grow")
-    for t in range(5, S):
+    for t in range(5, S + 1):
         step(t)
-    step(S)
     load[1].start()
+    step(S + 1)
+    load[2].start()
     load[1].wait()
     f.values()
     st.save("val", "vslope")
-    step(S + 1)
-    load[2].start()
+    step(S + 2)
+    load[3].start()
     load[2].wait()
     f.base()
     f.attend()
     st.save("lat", "res", "ars", "gated", "probs", "query", "keys")
-    step(S + 2)
-    load[3].start()
+    step(S + 3)
+    load[4].start()
     load[3].wait()
     f.hidden()
     st.save("first", "hpre", "upd")
     f.norm_two()
     st.save("second")
-    step(S + 3)
-    load[4].start()
+    for t in range(S + 4, S + LAG):
+        step(t)
     load[4].wait()
     f.up()
     st.save("inner", "uslope")
-    weight_grad(s.inner, s.dd, D, gdown, s.stage, ssem)
-    step(S + 4)
+    weight_grad(s.inner, s.dd, gdown, s.turned, s.stage, ssem, place=unit_place(n, FF) if dims else None)
+    step(S + LAG)
     if dims:
         gat.finish()
     st.close()
 
 
-def make_scatter(dims, parts, grads, outs):
-    nb = len(SCATTER_BUFS)
-    bufs = [Names(**dict(zip(SCATTER_BUFS, parts.rest(nb)))) for _ in grads]
-    p = Place(dims)
-    p.barrier()
-    return Scatter(p, grads, bufs, outs, *parts.rest(3))
-
-
-def columns(ref, w):
-    pieces, lo = [], 0
-    for q in w:
-        pieces.append(ref.at[(slice(None),) * (len(ref.shape) - 1) + (pl.ds(lo, q),)])
-        lo += q
-    return pieces
-
-
-def mid_kernel(dims, *refs):
+def unit_place(n, rows):
+    return D * n // (2 * rows), rows // (32 * n)
+
+
+def blocks_of(ref, n):
+    return ref.reshape(n // 2, 2, ref.shape[0] // n, ref.shape[1])
+
+
+def back_kernel(dims, n, count, *refs):
     r = Parts(refs)
-    x, g, valid, h, up, down = r.rest(6)
-    gdown = r.rest(1)[0]
-    ins = r.take(LOADED["mid"])
-    out = r.rest(1)[0]
-    outs = r.take(SAVED["mid"])
-    gup, gh = r.rest(2)
-    reduced = r.rest(2) if dims else []
-    st = Store("mid", r, ins, outs)
+    x, g, valid, v, mx, h, up, down, gdown = r.rest(9)
+    ins = r.take(LOADED["back"])
+    out, dxo = r.rest(2)
+    gup, gh, gmx, gv = r.rest(4)
+    reduced = r.rest(6) if dims else r.rest(1)
+    st = Store("back", r, ins, {})
     s = st.s
     s.datt, s.dv, s.dx, s.dup, s.dsec = s.gated, s.vslope, s.first, s.inner, s.dn
-    st.held.update(dv=s.dv, dx=s.dx)
-    lsem, ssem = r.rest(2)
-    load_down = pltpu.make_async_copy(down, s.wr, lsem.at[0])
-    load_up = pltpu.make_async_copy(up, s.wup, lsem.at[1])
-    load_h = pltpu.make_async_copy(h, s.wr.at[0:VALUE_WIDTH], lsem.at[2])
-    load_down.start()
-    st.fetch()
-    load_up.start()
+    wsem, ssem = r.rest(2)
+    ws = {k: Stream(w, s.ring, wsem) for k, w in (("down", down), ("up", up), ("h", h), ("mx", mx), ("v", v))}
     if dims:
-        cut = ((D // 2, D // 2), (FF // 2, FF // 2))
-        grads = columns(gdown, cut[0]) + columns(gup, cut[1])
-        sc = make_scatter(dims, r, grads, columns(reduced[0], cut[0]) + columns(reduced[1], cut[1]))
+        arrive, gsend, grecv = r.rest(3)
+        rings = dict(zip(SCATTER_BUFS, r.rest(len(SCATTER_BUFS))))
+        p = Place(dims)
+        p.barrier_all(n)
+        cols = lambda ref, lo, w: ref.at[:, :, :, pl.ds(lo, w)]
+        up4, mx4 = blocks_of(gup, n), blocks_of(gmx, n)
+        rv, rmx, rh, rup, rdown, rsmall = reduced
+        halves = lambda o, row: [(o, row, 0, 0, D), (o, row + 32, 0, D, D)]
+        units = [
+            (gdown.at[0], halves(rdown, 0)),
+            (gdown.at[1], halves(rdown, 64)),
+            (cols(up4, 0, UNIT), [(rup, 0, 0, 0, UNIT)]),
+            (cols(up4, UNIT, UNIT), [(rup, 0, UNIT, 0, UNIT)]),
+            (gh.at[0], halves(rh, 0)),
+            (blocks_of(gv, n), [(rv, 0, 0, 0, UNIT)]),
+            (cols(mx4, 0, UNIT), [(rmx, 0, 0, 0, UNIT)]),
+            (cols(mx4, UNIT, WIDE), [(rmx, 0, UNIT, 0, WIDE)]),
+        ]
+        sc = Scatter(p, [u[0] for u in units], rings, DEPTH, [u[1] for u in units], *r.rest(4))
         S = sc.stages()
-        late = 3
-        start = (0, 1, late, late + 1)
 
         def step(t):
-            for k in range(4):
-                if 0 <= t - start[k] < S:
-                    sc.stage(k, t - start[k])
-    else:
-        S, late = 8, 3
-        step = lambda t: None
-    w = Names(h=s.wr.at[0:VALUE_WIDTH], up=s.wup, down=s.wr)
-    f = Forward(x, valid, s.prow, None, w, s)
-    b = Backward(x, g, valid, s.prow, None, w, s, s, s.grow, None)
-    step(0)
-    st.need("inner", "uslope", "first", "dd", "prow", "grow")
-    load_down.wait()
-    f.down(out)
-    step(1)
-    b.d_up()
-    load_h.start()
-    step(2)
-    st.need("second")
-    weight_grad(s.second, s.dup, FF, gup, s.stage, ssem)
-    step(3)
-    load_up.wait()
-    b.d_second()
-    step(4)
-    st.need("hpre", "upd")
-    b.norm_two()
-    st.save("dx")
-    step(5)
-    st.need("gated")
-    weight_grad(s.gated, s.dbase, D, gh, s.stage, ssem, lo=C_HX)
-    step(6)
-    load_h.wait()
-    st.need("res", "ars")
-    b.d_gated()
-    step(7)
-    st.need("lat", "val", "vslope", "probs", "query", "keys")
-    b.attend()
-    st.save("dbase", "dv", "grow")
-    for t in range(8, late + 1 + S):
-        step(t)
-    if dims:
-        sc.finish()
-    st.close()
-
-
-def back_kernel(dims, n, count, *refs):
-    r = Parts(refs)
-    x, valid, v, mx = r.rest(4)
-    gh = r.rest(1)[0]
-    ins = r.take(LOADED["back"])
-    dxo = r.rest(1)[0]
-    gmx, gv = r.rest(2)
-    reduced = r.rest(4) if dims else r.rest(1)
-    st = Store("back", r, ins, {})
-    s = st.s
-    lsem, ssem = r.rest(2)
-    l_mx = pltpu.make_async_copy(mx, s.wc, lsem.at[0])
-    l_v = pltpu.make_async_copy(v, s.wv, lsem.at[1])
-    st.fetch()
-    l_mx.start()
-    l_v.start()
-    start = (0, 2, 3, 2, 10)
-    if dims:
-        cut = (VALUE_WIDTH, MXW - VALUE_WIDTH)
-        split = (n // 2, 2, D // n)
-        gmx4, gv4 = gmx, gv
-        grads = [gh] + columns(gmx4, cut) + [gv4, s.gsmall]
-        sc = make_scatter(dims, r, grads, [reduced[0]] + columns(reduced[1], cut) + [reduced[2], reduced[3]])
-        S = sc.stages()
-
-        def step(t):
-            for k in range(5):
-                if 0 <= t - start[k] < S:
-                    sc.stage(k, t - start[k])
+            for k, q in enumerate(UNIT_STARTS):
+                if 0 <= t - q < S:
+                    sc.stage(k, t - q)
+
+        def give(i, dev, slot):
+            return pltpu.make_async_remote_copy(
+                src_ref=s.gsmall.at[dev // 2, dev % 2], dst_ref=arrive.at[slot], send_sem=gsend.at[i], recv_sem=grecv.at[i],
+                device_id=(dev,), device_id_type=MESH,
+            )
     else:
         S = 8
         step = lambda t: None
-    b = Backward(x, None, valid, s.prow, s.ema, Names(mx=s.wc, v=s.wv), s, s, s.grow, s.gema)
+    st.fetch()
+    ws["down"].prefetch()
+    b = Backward(x, g, valid, s.prow, s.ema, None, s, s, s.grow, s.gema)
+    grad = lambda *q, **kw: weight_grad(*q[:3], s.turned, s.stage, ssem, **kw)
     step(0)
-    st.need("dv", "normed", "prow", "grow")
-    weight_grad(s.normed, s.dv, VALUE_WIDTH, gv, s.stage, ssem)
+    s.dn[...] = jnp.zeros(s.dn.shape, F32)
+    b.pad_tail()
+    st.need("inner", "uslope", "first", "dd", "prow", "grow")
     step(1)
-    st.need("dbase", "mixed")
-    weight_grad(s.mixed, s.dbase, MXW, gmx, s.stage, ssem)
+    ws["down"].run(b.down_tile)
+    ws["up"].prefetch()
     step(2)
-    l_mx.wait()
+    st.need("second")
+    grad(s.second, s.dup, gup, start=0, stop=UNIT)
+    step(3)
+    grad(s.second, s.dup, gup, start=UNIT, stop=FF)
+    step(4)
+    b.output(out)
+    ws["up"].run(b.second_tile)
+    ws["h"].prefetch()
+    step(5)
+    st.need("hpre", "upd")
+    b.norm_two()
+    step(6)
+    st.need("gated")
+    grad(s.gated, s.dbase, gh, lo=C_HX, place=unit_place(n, VALUE_WIDTH) if dims else None)
+    step(7)
+    st.need("res", "ars")
+    ws["h"].run(b.gated_tile)
+    ws["mx"].prefetch()
+    step(8)
+    st.need("lat", "val", "vslope", "probs", "query", "keys")
+    b.attend()
+    st.need("normed")
+    grad(s.normed, s.dv, gv)
+    step(9)
+    st.need("mixed")
+    grad(s.mixed, s.dbase, gmx, start=0, stop=UNIT)
+    step(10)
+    grad(s.mixed, s.dbase, gmx, start=UNIT)
+    step(11)
     st.need("e", "mpad")
-    b.d_mixed()
-    step(3)
-    l_v.wait()
-    b.d_normed()
-    step(4)
+    ws["mx"].run(b.mixed_tile)
+    ws["v"].prefetch()
+    step(12)
+    ws["v"].run(b.normed_tile)
     st.need("kern")
     b.smooth_signal(0)
-    step(5)
+    step(13)
     b.smooth_signal(1)
-    step(6)
+    step(14)
     b.smooth_filter()
-    step(7)
+    step(15)
     st.need("ema")
     b.ema_grads()
-    step(8)
-    st.need("dx")
     b.norm_one(dxo)
-    step(9)
+    step(16)
     pack_grads(n, count, s.grow, s.gema, s.full, s.gsmall)
-    for t in range(10, start[4] + S):
-        step(t)
     if dims:
-        sc.finish()
+        me = p.me
+
+        @pl.loop(1, n)
+        def _(i):
+            give(i, (me + i) % n, i).start()
+
+        for t in range(17, UNIT_STARTS[-1] + S):
+            step(t)
+        rsmall[...] = s.gsmall[me // 2, me % 2].astype(F32)
+
+        @pl.loop(1, n)
+        def _(i):
+            give(i, me, i).wait()
+            rsmall[...] += arrive[i].astype(F32)
     else:
         reduced[0][...] = s.gsmall[...]
     st.close()
 
 
-def scatter_parts(dims, shapes):
-    scratch = []
-    for q in shapes:
-        scratch += scatter_scratch(dims, q[0], q[1])
-    ns = scatter_sems(dims, len(shapes))
-    return scratch + [pltpu.SemaphoreType.DMA((ns,)), pltpu.SemaphoreType.DMA((ns,)), pltpu.SemaphoreType.DMA((len(shapes) * dims[0],))]
+UNIT_STARTS = (0, 1, 3, 4, 8, 9, 11, 12)
 
 
 def run_kernel(body, ins, outs, scratch, cid):
@@ -1338,12 +1312,12 @@
     whole = [(n * a.shape[0], a.shape[1]) if dims else a.shape for a in arrays]
     parts = [(q[0] // n, q[1]) for q in whole]
     split = lambda a: a.reshape(n // 2, 2, a.shape[0] // n, a.shape[1])
-    four = lambda i: (n // 2, 2) + parts[i]
     held = lambda kind, k: tmp(HELD[kind]) + [dma((max(1, len(LOADED.get(kind, ()))),)), dma((max(1, len(SAVED[kind])),))] + [dma((k,)), dma((2,))]
     a = {}
+    unit = lambda k: (k, n // 2, 2, 32, UNIT)
 
     scratch = held("front", 6)
-    o = saved("front") + [(whole[5], BF16, False)]
+    o = saved("front") + [(unit(2) if dims else whole[5], BF16, False)]
     if dims:
         ns = sems_needed(dims, 5)
         scratch += [dma((5,)), dma((n,)), dma((n,)), dma((ns,)), dma((ns,))]
@@ -1355,37 +1329,23 @@
     gdown = res[0]
     v, mx, h, up, down = res[1:] if dims else arrays[1:]
 
-    ins = [(x, True), (g, True), (valid, True), (h, False), (up, False), (down, False), (split(gdown), False)]
-    ins += [(a[k], False) for k in LOADED["mid"]]
-    o = [((m, D), BF16, True)] + saved("mid") + [(four(4), BF16, False), (four(3), BF16, False)]
-    scratch = held("mid", 3)
-    if dims:
-        o += [(parts[5], F32, True), (parts[4], F32, True)]
-        scratch += scatter_parts(dims, ((parts[5][0], D // 2),) * 2 + ((parts[4][0], FF // 2),) * 2)
-    res = run_kernel(functools.partial(mid_kernel, dims), ins, o, scratch, 1 if dims else None)
-    out = res[0]
-    a.update(zip(SAVED["mid"], res[1:]))
-    gup, gh = res[5:7]
-    if dims:
-        gdown, gup = res[7:]
-
-    ins = [(x, True), (valid, True), (v, False), (mx, False), (gh, False)] + [(a[k], False) for k in LOADED["back"]]
-    o = [((m, D), BF16, True), (four(2), BF16, False), (four(1), BF16, False)]
+    ins = [(x, True), (g, True), (valid, True)] + [(q, False) for q in (v, mx, h, up, down, gdown)] + [(a[k], False) for k in LOADED["back"]]
+    o = [((m, D), BF16, True)] * 2 + [(whole[4], BF16, False), (unit(1) if dims else whole[3], BF16, False), (whole[2], BF16, False), (whole[1], BF16, False)]
     scratch = held("back", 2)
     if dims:
-        o += [(parts[i], F32, True) for i in (3, 2, 1)] + [((SMALL_ROWS, 128), F32, True)]
-        rows = parts[2][0]
-        scratch += scatter_parts(dims, (parts[3], (rows, VALUE_WIDTH), (rows, MXW - VALUE_WIDTH), parts[1], (SMALL_ROWS, 128)))
+        o += [(parts[i], F32, True) for i in (1, 2, 3, 4, 5)] + [((SMALL_ROWS, 128), F32, True)]
+        scratch += [VM((n, SMALL_ROWS, 128), BF16), dma((n,)), dma((n,))]
+        scratch += scatter_scratch(dims, 32, WIDE, DEPTH, len(UNIT_STARTS))
     else:
         o += [table["gsmall"] + (True,)]
-    res = run_kernel(functools.partial(back_kernel, dims, n, count), ins, o, scratch, 2 if dims else None)
+    res = run_kernel(functools.partial(back_kernel, dims, n, count), ins, o, scratch, 1 if dims else None)
+    out, dx = res[:2]
     if dims:
-        gh, gmx, gv, gs = res[3:]
+        gv, gmx, gh, gup, gdown, gs = res[6:]
     else:
-        gmx, gv = res[1:3]
-        gs = res[3]
-        gv, gmx, gh, gup, gs = (q.reshape(-1, q.shape[-1]) for q in (gv, gmx, gh, gup, gs))
-    return out, res[0], gv, gmx, gh, gup, gdown, gs
+        gup, gh, gmx, gv = res[2:6]
+        gs = res[6].reshape(n * SMALL_ROWS, 128)
+    return out, dx, gv, gmx, gh, gup, gdown, gs
 
 
 def frame_in(small, me):

time: 394 us -> 374 us (0.949)
  Pallas kernels: 388 us -> 368 us
    pallas_call x4 -> x3, Pallas kernels: 388 us -> 368 us  [run_kernel(): pl.pallas_call(body, out_shape=[jax.ShapeDtypeStruct(o[0], o[1]) for o in...]
where the time goes in v5:
time: 374 us; the launch traced here: 373 us
  Pallas kernels  368 us (98%)
    pallas_call x3, Pallas kernels, run_kernel(): pl.pallas_call(body, out_shape=[jax.ShapeDtypeStruct(o[0], o[1]) for o in...  368 us

profile of v5, /device:TPU:0, one launch (start us, length us, event | category | flops | bytes accessed | tf_op | source)
XLA Modules:
  0.0 373.0 jit_solution(10473490755352619228)
XLA Ops:
  0.7 0.7 compare_convert_fusion
  1.4 0.9 dynamic_update_slice.3
  2.3 0.6 pad.4.refs_3_
  2.9 0.8 broadcast_in_dim.4.refs_2_
  3.6 183.3 %shard_map.155 = (bf16[256,4096]{1,0:T(8,128)(2,1)}, bf16[256,4096]{1,0:T(8,128)(2,1)}, f32[256,1024]{1,0:T(8,128)}, f32[256,1024]{1,0:T(8,128)}, bf16[256,1024]...) custom-call(bf16[256,1024]{1,0:T(8,128)(2,1)} %bitcast.12, ...), custom_call_target="tpu_custom_call" | custom-call | tf_op jit(solution)/shard_map/pallas_call | solution.py:1276
  187.0 181.8 %shard_map.156 = (bf16[256,1024]{1,0:T(8,128)(2,1)}, bf16[256,1024]{1,0:T(8,128)(2,1)}, bf16[1024,4096]{1,0:T(8,128)(2,1)}, bf16[1,16,2,32,2048]{4,3,2,1,0:T(8,1...) custom-call(bf16[256,1024]{1,0:T(8,128)(2,1)} %bitcast.13, ...), custom_call_target="tpu_custom_call" | custom-call | tf_op jit(solution)/shard_map/pallas_call | solution.py:1276
  368.7 2.8 shard_map.157
  371.6 1.4 dynamic_slice.3
  (1 shorter events, 0.0 us)

commit v6 on v5

--- a/solution.py
+++ b/solution.py
@@ -138,7 +138,7 @@
 
 def sems_needed(dims, K):
     Z = dims[0]
-    return K * (2 * (Z - 1) + 12 * (2 * Z - 1))
+    return K * (2 * (Z - 1) + 8 * (2 * Z - 1) + 4)
 
 
 F32, BF16 = jnp.float32, jnp.bfloat16
@@ -280,27 +280,43 @@
 
         tiles(0, VALUE_WIDTH, TILE, one)
 
-    def base(self):
+    def base_one(self):
         s = self.s
 
-        def one(width):
-            def f(col):
-                cols = pl.ds(col, width)
-                s.base[:, cols] = dot(s.mixed[...], self.w.mx[:, cols]) + self.pd(O_MXB, col, width)
-
-            return f
-
-        tiles(0, D, TILE, one(TILE))
-        tiles(C_LAT, C_RES, Z, one(Z))
-        tiles(C_RES, MXW, TILE, one(TILE))
+        def f(dst, lo, width):
+            def one(col):
+                dst[:, pl.ds(pl.multiple_of(col - lo, 128), width)] = dot(s.mixed[...], self.w.mx1[:, pl.ds(col, width)]) + self.pd(O_MXB, col, width)
+
+            return one
+
+        def gate(col):
+            cols = pl.ds(col, TILE)
+            s.upd[:, cols] = sigmoid(dot(s.mixed[...], self.w.mx1[:, cols]) + self.pd(O_MXB, col, TILE))
+
+        tiles(0, D, TILE, gate)
+        s.lat[...] = dot(s.mixed[...], self.w.mx1[:, C_LAT:C_RES]) + self.p(O_MXB + C_LAT, Z)
+        tiles(C_RES, C_RES + D, TILE, f(s.first, C_RES, TILE))
+
+    def base_two(self):
+        s = self.s
+
+        def f(dst, lo):
+            def one(col):
+                here = pl.multiple_of(lo + col, 128)
+                v = dot(s.mixed[...], self.w.mx2[:, pl.ds(here, TILE)]) + self.pd(O_MXB + C_RES + D, here, TILE)
+                dst[:, pl.ds(col, TILE)] = v
+
+            return one
+
+        tiles(0, D, TILE, f(s.dn, 0))
+        tiles(0, D, TILE, f(s.hpre, D))
 
     def attend(self):
         s = self.s
         table, mask = rel_table(self.p(O_REL, STRETCH)), causal()
         for q in range(self.seqs):
             r = slice(q * STRETCH, (q + 1) * STRETCH)
-            b = s.base[r, C_LAT:C_RES]
-            s.lat[r, :] = b
+            b = s.lat[r, :]
             lat = b * sigmoid(b)
             query = (lat * (1.0 + self.p(O_AFF, Z)) + self.p(O_AFF + 2 * Z, Z)).astype(BF16)
             keys = (lat * (1.0 + self.p(O_AFF + Z, Z)) + self.p(O_AFF + 3 * Z, Z)).astype(BF16)
@@ -312,30 +328,29 @@
             s.keys[r, :] = keys
             low = pr.astype(BF16)
 
-            def one(col):
-                cols = pl.ds(col, TILE)
+            def one(half, pre, col):
+                cols = pl.ds(pl.multiple_of(half + col, 128), TILE)
                 at = dot(low, s.val[r, cols])
-                bb = s.base[r, pl.ds(pl.multiple_of(C_RES + col, 128), TILE)]
+                bb = pre[r, pl.ds(col, TILE)]
                 sb = sigmoid(bb)
                 res = bb * sb
                 s.res[r, cols] = res.astype(BF16)
                 s.ars[r, cols] = (at * silu_slope(bb, sb)).astype(BF16)
                 s.gated[r, cols] = (at * res).astype(BF16)
 
-            tiles(0, VALUE_WIDTH, TILE, one)
+            tiles(0, D, TILE, functools.partial(one, 0, s.first))
+            tiles(0, D, TILE, functools.partial(one, D, s.dn))
 
     def hidden(self):
         s = self.s
 
         def one(col):
             cols = pl.ds(col, TILE)
-            h = dot(s.gated[...], self.w.h[:, cols]) + self.pd(O_HB, col, TILE)
-            h = h + s.base[:, pl.ds(pl.multiple_of(C_HX + col, 128), TILE)]
+            h = dot(s.gated[:, 0:D], self.w.h1[:, cols]) + dot(s.gated[:, D : 2 * D], self.w.h2[:, cols])
+            h = s.hpre[:, cols] + h + self.pd(O_HB, col, TILE)
             s.hpre[:, cols] = h
             xf = self.x[:, cols].astype(F32)
-            u = sigmoid(s.base[:, cols])
-            s.upd[:, cols] = u
-            s.first[:, cols] = xf + self.valid[:, 0:1] * u * (h * sigmoid(h) - xf)
+            s.first[:, cols] = xf + self.valid[:, 0:1] * s.upd[:, cols] * (h * sigmoid(h) - xf)
 
         tiles(0, D, TILE, one)
 
@@ -349,17 +364,18 @@
             xhat, _ = center(s.first[r, :])
             s.second[r, :] = (xhat * g + b).astype(BF16)
 
-    def up(self):
+    def up(self, half):
         s = self.s
+        w, lo = (self.w.up1, 0) if half == 0 else (self.w.up2, FF // 2)
 
         def one(col):
-            cols = pl.ds(col, TILE)
-            u = dot(s.second[...], self.w.up[:, cols]) + self.pd(O_UPB, col, TILE)
+            cols = pl.ds(pl.multiple_of(lo + col, 128), TILE)
+            u = dot(s.second[...], w[:, pl.ds(col, TILE)]) + self.pd(O_UPB + lo, col, TILE)
             su = sigmoid(u)
             s.uslope[:, cols] = silu_slope(u, su).astype(BF16)
             s.inner[:, cols] = (u * su).astype(BF16)
 
-        tiles(0, FF, TILE, one)
+        tiles(0, FF // 2, TILE, one)
 
 
 class Backward:
@@ -586,33 +602,47 @@
 
     def ema_grads(self):
         t = self.t
-        gate, a, retain, weight = ema_rates(self.ema)
-        zero = retain - retain
-
-        def step(j, carry):
-            power, before, dw, dr = carry
-            row = t.dkern[pl.ds(j, 1), :]
-            dw = dw + row * power
-            dr = dr + (row * j.astype(F32)) * before
-            return power * retain, power, dw, dr
-
-        _, _, dw, dr = lax.fori_loop(0, STRETCH, step, (zero + 1.0, zero, zero, zero))
-        drate = -dr * weight
         scale = 1.0 / math.sqrt(H)
-        dgate = drate * a + dw * self.ema[2] * self.ema[3] * scale
-        self.gema[0] = dgate * gate * (1.0 - gate)
-        self.gema[1] = drate * gate * a * (1.0 - a)
-        self.gema[2] = dw * gate * self.ema[3] * scale
-        self.gema[3] = dw * gate * self.ema[2] * scale
+
+        @pl.loop(0, D // 128)
+        def _(l):
+            lb = lane_block(l)
+            par = self.ema[:, :, lb]
+            gate, a, retain, weight = ema_rates(par)
+            zero = retain - retain
+
+            def eight(k, carry):
+                power, before, dw, dr = carry
+                rows = t.dkern[pl.ds(pl.multiple_of(8 * k, 8), 8), lb]
+                for i in range(8):
+                    row = rows[i : i + 1, :]
+                    dw = dw + row * power
+                    dr = dr + (row * (8 * k + i).astype(F32)) * before
+                    power, before = power * retain, power
+                return power, before, dw, dr
+
+            _, _, dw, dr = lax.fori_loop(0, STRETCH // 8, eight, (zero + 1.0, zero, zero, zero))
+            drate = -dr * weight
+            dgate = drate * a + dw * par[2] * par[3] * scale
+            self.gema[0, :, lb] = dgate * gate * (1.0 - gate)
+            self.gema[1, :, lb] = drate * gate * a * (1.0 - a)
+            self.gema[2, :, lb] = dw * gate * par[3] * scale
+            self.gema[3, :, lb] = dw * gate * par[2] * scale
 
 
 class Scatter:
-    def __init__(self, place, grads, rings, depth, outs, send_sem, recv_sem, local_sem, credit):
+    def __init__(self, place, grads, pool, depth, outs, send_sem, recv_sem, local_sem, credit, first):
+        self.ready = first
         self.p, self.grads, self.outs, self.depth, self.credit = place, grads, outs, depth, credit
         self.bufs = []
         for k, g in enumerate(grads):
-            e, w = k % depth, pl.ds(0, g.shape[-1])
-            self.bufs.append(Names(**{name: ref.at[e, :, :, w] for name, ref in rings.items()}))
+            wide, w = pool.shape[1], pl.ds(0, g.shape[-1])
+            lo = (k % depth) * (pool.shape[0] // depth)
+            views = {}
+            for name, (q, r) in unit_buffers((place.Z, place.Y, place.X), g.shape[-2]).items():
+                views[name] = pool.at[pl.ds(lo, q * r)].reshape(q, r, wide).at[:, :, w]
+                lo += q * r
+            self.bufs.append(Names(**views))
         self.ss, self.rs, self.ls = send_sem, recv_sem, local_sem
         self.ids, self.pend = {}, [[] for _ in grads]
 
@@ -627,7 +657,18 @@
                 slot = (0, 1, 2, 4, 3)[i]
                 when(cond, lambda slot=slot, to=to: pl.semaphore_signal(self.credit.at[k, slot], inc=1, device_id=(to,), device_id_type=MESH))
 
+    def open(self):
+        for i, (cond, to) in enumerate(self.around()):
+            slot = (0, 1, 2, 4, 3)[i]
+            when(cond, lambda slot=slot, to=to: pl.semaphore_signal(self.ready.at[slot], inc=1, device_id=(to,), device_id_type=MESH))
+
+    def entered(self):
+        for i, (cond, to) in enumerate(self.around()):
+            when(cond, lambda i=i: pl.semaphore_wait(self.ready.at[i], 1))
+
     def admit(self, k):
+        if k == 0:
+            self.entered()
         if k >= self.depth:
             for i, (cond, to) in enumerate(self.around()):
                 when(cond, lambda i=i: pl.semaphore_wait(self.credit.at[k - self.depth, i], 1))
@@ -784,13 +825,17 @@
 SCATTER_BUFS = ("mine", "sum", "dx", "dy", "rx", "ry", "ru", "rd", "rz")
 
 
-def scatter_scratch(dims, r, w, depth, K):
+def unit_buffers(dims, r):
     Z, Y, X = dims
-    sizes = dict(mine=(2 * Y * X, r), sum=(Z * Y * X, r), dx=(Z, r // 2), dy=(Z, r // 2), rx=(Z, r), ry=(Z, r), ru=(Z, r), rd=(Z, r), rz=(4, r))
-    ns = K * (7 * Z + 4)
-    dma = pltpu.SemaphoreType.DMA
-    scratch = [pltpu.VMEM((depth,) + sizes[k] + (w,), BF16) for k in SCATTER_BUFS]
-    return scratch + [dma((ns,)), dma((ns,)), dma((K * Z,)), pltpu.SemaphoreType.REGULAR((K, 5))]
+    return dict(
+        mine=(2 * Y * X, r), sum=(Z * Y * X, r), dx=(Z, r // 2), dy=(Z, r // 2), rx=(Z, r), ry=(Z, r), ru=(Z, r), rd=(Z, r), rz=(4, r)
+    )
+
+
+def scatter_sems(dims, K):
+    ns = K * (7 * dims[0] + 4)
+    dma, plain = pltpu.SemaphoreType.DMA, pltpu.SemaphoreType.REGULAR
+    return [dma((ns,)), dma((ns,)), dma((K * dims[0],)), plain((K, 5)), plain((5,))]
 
 
 KEPT_OLD = ("normed", "mpad", "e", "mixed", "kern", "vslope", "val", "base", "probs", "query", "keys", "att", "gated", "hpre", "first", "second", "uslope", "inner")
@@ -833,25 +878,27 @@
         stage[slot, :, 0:w] = dot(turned[...], b[:, pl.ds(pl.multiple_of(lo + col, 128), w)]).astype(BF16)
         begin(slot, i, col, w)
 
-    pairs = (stop - start) // (2 * TILE)
+    slots = stage.shape[0]
+    rounds = (stop - start) // (slots * TILE)
     for i in range(a.shape[1] // D):
         turned[...] = a[:, i * D : (i + 1) * D].T
 
-        @pl.loop(0, pairs)
+        @pl.loop(0, rounds)
         def _(j):
-            for slot in range(2):
+            for slot in range(slots):
 
                 @pl.when(jnp.logical_or(j > 0, i > 0))
                 def _():
                     wait(slot, TILE)
 
-                block(slot, i, start + (j * 2 + slot) * TILE, TILE)
-
-    rest = stop - start - pairs * 2 * TILE
+                block(slot, i, start + (j * slots + slot) * TILE, TILE)
+
+    rest = stop - start - rounds * slots * TILE
     wait(0, TILE)
     if rest:
         block(0, 0, stop - rest, rest)
-    wait(1, TILE)
+    for slot in range(1, slots):
+        wait(slot, TILE)
     if rest:
         wait(0, rest)
 
@@ -894,8 +941,12 @@
     )
 
 
-SMALL_ROWS = 32
-FRAME = 24
+def frame(count):
+    return -(-(-(-count // 128) + 1) // 8) * 8
+
+
+def slot_rows(count):
+    return -(-frame(count) // 16) * 16
 
 
 def frames(n, count):
@@ -911,7 +962,7 @@
 def unpack_params(n, count, packed, full, prow, ema):
     full[...] = jnp.zeros(full.shape, F32)
     for d, r in enumerate(frames(n, count)):
-        full[r : r + FRAME, :] += packed[d * SMALL_ROWS : d * SMALL_ROWS + FRAME, :].astype(F32)
+        full[r : r + frame(count), :] += packed[d * slot_rows(count) : d * slot_rows(count) + frame(count), :].astype(F32)
     for i in range(O_EMA // 128):
         prow[:, i * 128 : (i + 1) * 128] = full[i : i + 1, :]
     rows = []
@@ -938,18 +989,18 @@
         lo = O_EMA // 128 + j * D * H // 128
         full[lo : lo + 128, :] = jnp.concatenate([e[:, k * 128 : (k + 1) * 128] for k in range(8)], axis=0).T
     for d, r in enumerate(frames(n, count)):
-        out[d // 2, d % 2, 0:FRAME, :] = full[r : r + FRAME, :].astype(BF16)
-        out[d // 2, d % 2, FRAME:SMALL_ROWS, :] = jnp.zeros((SMALL_ROWS - FRAME, 128), BF16)
+        out[d // 2, d % 2, 0:frame(count), :] = full[r : r + frame(count), :].astype(BF16)
+        out[d // 2, d % 2, frame(count):slot_rows(count), :] = jnp.zeros((slot_rows(count) - frame(count), 128), BF16)
 
 
 def size_table(n, count, m):
-    rows = -(-(-(-(n * count) // 128) + FRAME) // 8) * 8
+    rows = -(-(-(-(n * count) // 128) + frame(count)) // 8) * 8
     table = {k: v for k, v in list(kept_shapes(m).items()) + list(own_shapes(m).items())}
     table.update(
         out=((m, D), BF16), dxo=((m, D), BF16), grow=((1, O_EMA), F32), prow=((1, O_EMA), F32), ema=((4, H, D), F32),
-        gema=((4, H, D), F32), full=((rows, 128), F32), packed=((n * SMALL_ROWS, 128), BF16),
-        gsmall=((n // 2, 2, SMALL_ROWS, 128), BF16), wr=((FF, D), BF16), wc=((D, MXW), BF16), wv=((D, VALUE_WIDTH), BF16),
-        wup=((D, FF), BF16), ring=((2, TILE, MXW), BF16), stage=((2, D, TILE), BF16), turned=((D, m), BF16), wh=((VALUE_WIDTH, D), BF16),
+        gema=((4, H, D), F32), full=((rows, 128), F32), packed=((n * slot_rows(count), 128), BF16),
+        gsmall=((n // 2, 2, slot_rows(count), 128), BF16), wr=((FF, D), BF16), wc=((D, MXW), BF16), wv=((D, VALUE_WIDTH), BF16),
+        wup=((D, FF), BF16), ring=((2, TILE, MXW), BF16), pool=((6 * D, WIDE), BF16), stage=((4, D, TILE), BF16), turned=((D, m), BF16), wh=((VALUE_WIDTH, D), BF16),
     )
     return table
 
@@ -970,80 +1021,45 @@
 GATHER_STARTS = (0, 1, 2, 3, 4)
 LAG = GATHER_STARTS[-1]
 
-SAVED = dict(
-    front=("inner", "uslope", "first", "hpre", "second", "dd", "upd", "lat", "res", "ars", "gated", "val", "vslope", "probs", "query", "keys", "mixed", "normed", "e", "mpad", "kern", "grow", "prow", "ema"),
-    back=(),
-)
-LOADED = dict(back=SAVED["front"])
-HELD = dict(
-    front=SAVED["front"] + ("base", "full", "packed", "wh", "wup", "wc", "wv", "stage", "turned"),
-    back=SAVED["front"] + ("dbase", "dn", "acc", "dpad", "dkern", "gema", "full", "gsmall", "ring", "stage", "turned"),
-)
+KEPT = ("inner", "uslope", "first", "hpre", "second", "dd", "upd", "lat", "res", "ars", "gated", "val", "vslope", "probs", "query", "keys", "mixed", "normed", "e", "mpad", "kern", "grow", "prow", "ema")
+HELD = KEPT + ("packed", "dbase", "dn", "acc", "dpad", "dkern", "gema", "full", "gsmall", "ring", "stage", "turned", "pool")
 DEPTH = 4
 UNIT = 2 * D
 WIDE = MXW - UNIT
 
 
-class Store:
-    def __init__(self, kind, r, ins, outs):
-        held = r.take(HELD[kind])
-        self.s = Names(**held)
-        self.held = held
-        self.ins, self.outs = ins, outs
-        self.in_sem, self.out_sem = r.rest(2)
-        self.names_in, self.names_out = list(ins), list(outs)
-        self.seen, self.begun = set(), []
-
-    def fetch(self):
-        for k in self.names_in:
-            self.copy_in(k).start()
-
-    def copy_in(self, k):
-        return pltpu.make_async_copy(self.ins[k], self.held[k], self.in_sem.at[self.names_in.index(k)])
-
-    def need(self, *names):
-        for k in names:
-            if k not in self.seen:
-                self.copy_in(k).wait()
-                self.seen.add(k)
-
-    def copy_out(self, k):
-        return pltpu.make_async_copy(self.held[k], self.outs[k], self.out_sem.at[self.names_out.index(k)])
-
-    def save(self, *names):
-        for k in names:
-            self.copy_out(k).start()
-            self.begun.append(k)
-
-    def close(self):
-        self.need(*self.names_in)
-        self.save(*[k for k in self.names_out if k not in self.begun])
-        for k in self.begun:
-            self.copy_out(k).wait()
-
-
-def front_kernel(dims, n, count, *refs):
+def unit_place(n, rows):
+    return D * n // (2 * rows), rows // (32 * n)
+
+
+def blocks_of(ref, n):
+    return ref.reshape(n // 2, 2, ref.shape[0] // n, ref.shape[1])
+
+
+def layer_kernel(dims, n, count, *refs):
     r = Parts(refs)
     x, g, valid = r.rest(3)
     ins = r.rest(6)
-    outs = r.take(SAVED["front"])
-    gdown = r.rest(1)[0]
+    out, dxo = r.rest(2)
+    gup, gh, gmx, gv, gdown = r.rest(5)
+    reduced = r.rest(6) if dims else r.rest(1)
     whole = [None] + r.rest(5) if dims else ins
-    st = Store("front", r, {}, outs)
-    s = st.s
-    lsem, ssem = r.rest(2)
-
+    s = Names(**r.take(HELD))
+    s.datt, s.dv, s.dx, s.dup, s.dsec = s.gated, s.vslope, s.first, s.inner, s.dn
+    lsem, wsem, ssem = r.rest(3)
+    _, v, mx, h, up, down = whole
+    ws = {k: Stream(w, s.ring, wsem) for k, w in (("down", down), ("up", up), ("h", h), ("mx", mx), ("v", v))}
     if dims:
-        osem, gsend, grecv, send_sem, recv_sem = r.rest(5)
+        osem, gsend, grecv, hsend, hrecv, send_sem, recv_sem, arrive = r.rest(8)
         p = Place(dims)
         p.barrier_all(n)
-        mine = pl.ds(p.me * SMALL_ROWS, SMALL_ROWS)
+        mine = pl.ds(p.me * slot_rows(count), slot_rows(count))
         own = pltpu.make_async_copy(ins[0], s.packed.at[mine], lsem.at[0])
         own.start()
 
         def tell(i, dev, block):
             return pltpu.make_async_remote_copy(
-                src_ref=ins[0], dst_ref=s.packed.at[pl.ds(block * SMALL_ROWS, SMALL_ROWS)], send_sem=gsend.at[i], recv_sem=grecv.at[i],
+                src_ref=ins[0], dst_ref=s.packed.at[pl.ds(block * slot_rows(count), slot_rows(count))], send_sem=gsend.at[i], recv_sem=grecv.at[i],
                 device_id=(dev,), device_id_type=MESH,
             )
 
@@ -1057,7 +1073,7 @@
             cp.start()
         last = gat.stages() - 1
 
-        def step(t):
+        def get(t):
             for k, q in enumerate(GATHER_STARTS):
                 if 0 <= t - q <= last:
                     gat.stage(k, t - q)
@@ -1070,93 +1086,7 @@
             @pl.loop(1, n)
             def _(i):
                 tell(i, p.me, (p.me - i + n) % n).wait()
-    else:
-        step = lambda t: None
-
-        def small_here():
-            small = pltpu.make_async_copy(ins[0], s.packed, lsem.at[0])
-            small.start()
-            small.wait()
-
-    S = dims[0] + 2 if dims else 6
-    w = Names(v=s.wv, mx=s.wc, h=s.wh, up=s.wup)
-    into = (None, s.wv, s.wc, s.wh, s.wup)
-    load = [None] + [pltpu.make_async_copy(whole[i], into[i], lsem.at[i]) for i in range(1, 5)]
-    f = Forward(x, valid, s.prow, s.ema, w, s)
-    b = Backward(x, g, valid, s.prow, s.ema, w, s, s, s.grow, None)
-    b.grow[...] = jnp.zeros(b.grow.shape, F32)
-    step(0)
-    b.cot()
-    step(1)
-    small_here()
-    unpack_params(n, count, s.packed, s.full, s.prow, s.ema)
-    f.norm_one()
-    step(2)
-    f.ema_kernel()
-    step(3)
-    f.smooth(0)
-    step(4)
-    f.smooth(1)
-    f.mix()
-    st.save("normed", "mixed", "e", "mpad", "kern", "prow", "ema", "dd", "grow")
-    for t in range(5, S + 1):
-        step(t)
-    load[1].start()
-    step(S + 1)
-    load[2].start()
-    load[1].wait()
-    f.values()
-    st.save("val", "vslope")
-    step(S + 2)
-    load[3].start()
-    load[2].wait()
-    f.base()
-    f.attend()
-    st.save("lat", "res", "ars", "gated", "probs", "query", "keys")
-    step(S + 3)
-    load[4].start()
-    load[3].wait()
-    f.hidden()
-    st.save("first", "hpre", "upd")
-    f.norm_two()
-    st.save("second")
-    for t in range(S + 4, S + LAG):
-        step(t)
-    load[4].wait()
-    f.up()
-    st.save("inner", "uslope")
-    weight_grad(s.inner, s.dd, gdown, s.turned, s.stage, ssem, place=unit_place(n, FF) if dims else None)
-    step(S + LAG)
-    if dims:
-        gat.finish()
-    st.close()
-
-
-def unit_place(n, rows):
-    return D * n // (2 * rows), rows // (32 * n)
-
-
-def blocks_of(ref, n):
-    return ref.reshape(n // 2, 2, ref.shape[0] // n, ref.shape[1])
-
-
-def back_kernel(dims, n, count, *refs):
-    r = Parts(refs)
-    x, g, valid, v, mx, h, up, down, gdown = r.rest(9)
-    ins = r.take(LOADED["back"])
-    out, dxo = r.rest(2)
-    gup, gh, gmx, gv = r.rest(4)
-    reduced = r.rest(6) if dims else r.rest(1)
-    st = Store("back", r, ins, {})
-    s = st.s
-    s.datt, s.dv, s.dx, s.dup, s.dsec = s.gated, s.vslope, s.first, s.inner, s.dn
-    wsem, ssem = r.rest(2)
-    ws = {k: Stream(w, s.ring, wsem) for k, w in (("down", down), ("up", up), ("h", h), ("mx", mx), ("v", v))}
-    if dims:
-        arrive, gsend, grecv = r.rest(3)
-        rings = dict(zip(SCATTER_BUFS, r.rest(len(SCATTER_BUFS))))
-        p = Place(dims)
-        p.barrier_all(n)
+
         cols = lambda ref, lo, w: ref.at[:, :, :, pl.ds(lo, w)]
         up4, mx4 = blocks_of(gup, n), blocks_of(gmx, n)
         rv, rmx, rh, rup, rdown, rsmall = reduced
@@ -1171,79 +1101,137 @@
             (cols(mx4, 0, UNIT), [(rmx, 0, 0, 0, UNIT)]),
             (cols(mx4, UNIT, WIDE), [(rmx, 0, UNIT, 0, WIDE)]),
         ]
-        sc = Scatter(p, [u[0] for u in units], rings, DEPTH, [u[1] for u in units], *r.rest(4))
+        sc = Scatter(p, [u[0] for u in units], s.pool, DEPTH, [u[1] for u in units], *r.rest(5))
         S = sc.stages()
 
-        def step(t):
+        def put(t):
             for k, q in enumerate(UNIT_STARTS):
                 if 0 <= t - q < S:
                     sc.stage(k, t - q)
 
         def give(i, dev, slot):
             return pltpu.make_async_remote_copy(
-                src_ref=s.gsmall.at[dev // 2, dev % 2], dst_ref=arrive.at[slot], send_sem=gsend.at[i], recv_sem=grecv.at[i],
+                src_ref=s.gsmall.at[dev // 2, dev % 2], dst_ref=arrive.at[slot], send_sem=hsend.at[i], recv_sem=hrecv.at[i],
                 device_id=(dev,), device_id_type=MESH,
             )
     else:
         S = 8
-        step = lambda t: None
-    st.fetch()
+        get = put = lambda t: None
+
+        def small_here():
+            small = pltpu.make_async_copy(ins[0], s.packed, lsem.at[0])
+            small.start()
+            small.wait()
+
+    G = dims[0] + 2 if dims else 6
+    q = lambda i, w=UNIT, lo=0: s.pool.at[i * D : (i + 1) * D, lo : lo + w]
+    w = Names(v=q(0), mx1=q(1, WIDE), mx2=q(2), up1=q(3), up2=q(4), h1=q(5, D), h2=q(5, D, D))
+    jobs = [
+        [(v, w.v)],
+        [(mx.at[:, 0:WIDE], w.mx1), (mx.at[:, WIDE:MXW], w.mx2)],
+        [(h.at[0:D], w.h1), (h.at[D : 2 * D], w.h2)],
+        [(up.at[:, 0:UNIT], w.up1), (up.at[:, UNIT:FF], w.up2)],
+    ]
+    load, i = [], 0
+    for pairs in jobs:
+        load.append([pltpu.make_async_copy(a, b, lsem.at[1 + i + e]) for e, (a, b) in enumerate(pairs)])
+        i += len(pairs)
+
+    def begin(k):
+        for c in load[k]:
+            c.start()
+
+    f = Forward(x, valid, s.prow, s.ema, w, s)
+    b = Backward(x, g, valid, s.prow, s.ema, None, s, s, s.grow, s.gema)
+    grad = lambda *a, **kw: weight_grad(*a[:3], s.turned, s.stage, ssem, **kw)
+    s.grow[...] = jnp.zeros(s.grow.shape, F32)
+    get(0)
+    b.cot()
+    get(1)
+    small_here()
+    unpack_params(n, count, s.packed, s.full, s.prow, s.ema)
+    f.norm_one()
+    get(2)
+    f.ema_kernel()
+    get(3)
+    f.smooth(0)
+    get(4)
+    f.smooth(1)
+    f.mix()
+    for t in range(5, G + 1):
+        get(t)
+    begin(0)
+    get(G + 1)
+    begin(1)
+    load[0][0].wait()
+    f.values()
+    get(G + 2)
+    begin(2)
+    load[1][0].wait()
+    f.base_one()
+    load[1][1].wait()
+    f.base_two()
+    f.attend()
+    get(G + 3)
+    begin(3)
+    for c in load[2]:
+        c.wait()
+    f.hidden()
+    f.norm_two()
+    get(G + 4)
+    load[3][0].wait()
+    f.up(0)
+    for t in range(G + 5, G + LAG):
+        get(t)
+    load[3][1].wait()
+    f.up(1)
+    if dims:
+        sc.open()
+    grad(s.inner, s.dd, gdown, place=unit_place(n, FF) if dims else None)
+    put(0)
+    get(G + LAG)
     ws["down"].prefetch()
-    b = Backward(x, g, valid, s.prow, s.ema, None, s, s, s.grow, s.gema)
-    grad = lambda *q, **kw: weight_grad(*q[:3], s.turned, s.stage, ssem, **kw)
-    step(0)
     s.dn[...] = jnp.zeros(s.dn.shape, F32)
     b.pad_tail()
-    st.need("inner", "uslope", "first", "dd", "prow", "grow")
-    step(1)
+    put(1)
     ws["down"].run(b.down_tile)
     ws["up"].prefetch()
-    step(2)
-    st.need("second")
+    put(2)
     grad(s.second, s.dup, gup, start=0, stop=UNIT)
-    step(3)
+    put(3)
     grad(s.second, s.dup, gup, start=UNIT, stop=FF)
-    step(4)
+    put(4)
     b.output(out)
     ws["up"].run(b.second_tile)
     ws["h"].prefetch()
-    step(5)
-    st.need("hpre", "upd")
+    put(5)
     b.norm_two()
-    step(6)
-    st.need("gated")
+    put(6)
     grad(s.gated, s.dbase, gh, lo=C_HX, place=unit_place(n, VALUE_WIDTH) if dims else None)
-    step(7)
-    st.need("res", "ars")
+    put(7)
     ws["h"].run(b.gated_tile)
     ws["mx"].prefetch()
-    step(8)
-    st.need("lat", "val", "vslope", "probs", "query", "keys")
+    put(8)
     b.attend()
-    st.need("normed")
     grad(s.normed, s.dv, gv)
-    step(9)
-    st.need("mixed")
+    put(9)
     grad(s.mixed, s.dbase, gmx, start=0, stop=UNIT)
-    step(10)
+    put(10)
     grad(s.mixed, s.dbase, gmx, start=UNIT)
-    step(11)
-    st.need("e", "mpad")
+    put(11)
     ws["mx"].run(b.mixed_tile)
     ws["v"].prefetch()
-    step(12)
+    put(12)
     ws["v"].run(b.normed_tile)
-    st.need("kern")
     b.smooth_signal(0)
-    step(13)
+    put(13)
     b.smooth_signal(1)
-    step(14)
+    put(14)
     b.smooth_filter()
-    step(15)
-    st.need("ema")
+    put(15)
     b.ema_grads()
     b.norm_one(dxo)
-    step(16)
+    put(16)
     pack_grads(n, count, s.grow, s.gema, s.full, s.gsmall)
     if dims:
         me = p.me
@@ -1253,19 +1241,24 @@
             give(i, (me + i) % n, i).start()
 
         for t in range(17, UNIT_STARTS[-1] + S):
-            step(t)
+            put(t)
         rsmall[...] = s.gsmall[me // 2, me % 2].astype(F32)
 
         @pl.loop(1, n)
         def _(i):
             give(i, me, i).wait()
             rsmall[...] += arrive[i].astype(F32)
+
+        gat.finish()
     else:
-        reduced[0][...] = s.gsmall[...]
-    st.close()
+        keep = pltpu.make_async_copy(s.gsmall, reduced[0], lsem.at[0])
+        keep.start()
+        keep.wait()
 
 
 UNIT_STARTS = (0, 1, 3, 4, 8, 9, 11, 12)
+GATHER_STARTS = (0, 1, 2, 3, 6)
+LAG = GATHER_STARTS[-1]
 
 
 def run_kernel(body, ins, outs, scratch, cid):
@@ -1308,50 +1301,35 @@
     table = size_table(n, count, m)
     dma = pltpu.SemaphoreType.DMA
     tmp = lambda names: [VM(*table[k]) for k in names]
-    saved = lambda kind: [table[k] + (False,) for k in SAVED[kind]]
     whole = [(n * a.shape[0], a.shape[1]) if dims else a.shape for a in arrays]
     parts = [(q[0] // n, q[1]) for q in whole]
-    split = lambda a: a.reshape(n // 2, 2, a.shape[0] // n, a.shape[1])
-    held = lambda kind, k: tmp(HELD[kind]) + [dma((max(1, len(LOADED.get(kind, ()))),)), dma((max(1, len(SAVED[kind])),))] + [dma((k,)), dma((2,))]
-    a = {}
+    scratch = tmp(HELD) + [dma((8,)), dma((2,)), dma((4,))]
     unit = lambda k: (k, n // 2, 2, 32, UNIT)
-
-    scratch = held("front", 6)
-    o = saved("front") + [(unit(2) if dims else whole[5], BF16, False)]
+    o = [((m, D), BF16, True)] * 2
+    o += [(q, BF16, False) for q in (whole[4], unit(1) if dims else whole[3], whole[2], whole[1], unit(2) if dims else whole[5])]
     if dims:
+        o += [(parts[i], F32, True) for i in (1, 2, 3, 4, 5)] + [((slot_rows(count), 128), F32, True)]
+        o += [(q, BF16, False) for q in whole[1:]]
         ns = sems_needed(dims, 5)
-        scratch += [dma((5,)), dma((n,)), dma((n,)), dma((ns,)), dma((ns,))]
-        o += [(q, BF16, False) for q in whole[1:]]
+        scratch += [dma((5,)), dma((n,)), dma((n,)), dma((n,)), dma((n,)), dma((ns,)), dma((ns,)), VM((n, slot_rows(count), 128), BF16)]
+        scratch += scatter_sems(dims, len(UNIT_STARTS))
+    else:
+        o += [table["gsmall"] + (False,)]
     ins = [(x, True), (g, True), (valid, True)] + [(q, False) for q in arrays]
-    res = run_kernel(functools.partial(front_kernel, dims, n, count), ins, o, scratch, 0 if dims else None)
-    a.update(zip(SAVED["front"], res))
-    res = res[len(SAVED["front"]) :]
-    gdown = res[0]
-    v, mx, h, up, down = res[1:] if dims else arrays[1:]
-
-    ins = [(x, True), (g, True), (valid, True)] + [(q, False) for q in (v, mx, h, up, down, gdown)] + [(a[k], False) for k in LOADED["back"]]
-    o = [((m, D), BF16, True)] * 2 + [(whole[4], BF16, False), (unit(1) if dims else whole[3], BF16, False), (whole[2], BF16, False), (whole[1], BF16, False)]
-    scratch = held("back", 2)
-    if dims:
-        o += [(parts[i], F32, True) for i in (1, 2, 3, 4, 5)] + [((SMALL_ROWS, 128), F32, True)]
-        scratch += [VM((n, SMALL_ROWS, 128), BF16), dma((n,)), dma((n,))]
-        scratch += scatter_scratch(dims, 32, WIDE, DEPTH, len(UNIT_STARTS))
-    else:
-        o += [table["gsmall"] + (True,)]
-    res = run_kernel(functools.partial(back_kernel, dims, n, count), ins, o, scratch, 1 if dims else None)
+    res = run_kernel(functools.partial(layer_kernel, dims, n, count), ins, o, scratch, 0 if dims else None)
     out, dx = res[:2]
     if dims:
-        gv, gmx, gh, gup, gdown, gs = res[6:]
+        gv, gmx, gh, gup, gdown, gs = res[7:13]
     else:
-        gup, gh, gmx, gv = res[2:6]
-        gs = res[6].reshape(n * SMALL_ROWS, 128)
+        gup, gh, gmx, gv, gdown = res[2:7]
+        gs = res[7].reshape(n * slot_rows(count), 128)
     return out, dx, gv, gmx, gh, gup, gdown, gs
 
 
 def frame_in(small, me):
     count = small.shape[0]
-    line = lax.dynamic_update_slice(jnp.zeros((FRAME * 128,), small.dtype), small, ((me * count) % 128,))
-    return jnp.pad(line.reshape(FRAME, 128), ((0, SMALL_ROWS - FRAME), (0, 0)))
+    line = lax.dynamic_update_slice(jnp.zeros((frame(count) * 128,), small.dtype), small, ((me * count) % 128,))
+    return jnp.pad(line.reshape(frame(count), 128), ((0, slot_rows(count) - frame(count)), (0, 0)))
 
 
 def frame_out(block, me, count):

time: 374 us -> 349 us (0.933)
  the two profiles are of different devices: /device:TPU:0 before, /device:TPU:1 now
where the time goes in v6:
time: 349 us; the launch traced here: 343 us
  Pallas kernels  337 us (97%)
  local copies, waits for them, and re-layouts  3.65 us (1%)
    pallas_call x2, Pallas kernels, run_kernel(): pl.pallas_call(body, out_shape=[jax.ShapeDtypeStruct(o[0], o[1]) for o in...  337 us

profile of v6, /device:TPU:1, one launch (start us, length us, event | category | flops | bytes accessed | tf_op | source)
XLA Modules:
  0.0 343.0 jit_solution(159253986101695739)
XLA Ops:
  0.7 0.7 compare_convert_fusion
  1.4 0.9 dynamic_update_slice.3
  2.3 0.6 pad.4.refs_3_
  2.9 0.8 broadcast_in_dim.4.refs_2_
  3.6 334.7 %shard_map.155 = (bf16[256,1024]{1,0:T(8,128)(2,1)}, bf16[256,1024]{1,0:T(8,128)(2,1)}, bf16[1024,4096]{1,0:T(8,128)(2,1)}, bf16[1,16,2,32,2048]{4,3,2,1,0:T(8,1...) custom-call(bf16[256,1024]{1,0:T(8,128)(2,1)} %bitcast.12, ...), custom_call_target="tpu_custom_call" | custom-call | tf_op jit(solution)/shard_map/pallas_call | solution.py:1269
  338.3 2.8 shard_map.156
  341.1 1.4 dynamic_slice.3
  (1 shorter events, 0.0 us)

commit v7 on v6

--- a/solution.py
+++ b/solution.py
@@ -883,15 +883,15 @@
     for i in range(a.shape[1] // D):
         turned[...] = a[:, i * D : (i + 1) * D].T
 
-        @pl.loop(0, rounds)
+        @pl.loop(0, rounds * slots)
         def _(j):
-            for slot in range(slots):
-
-                @pl.when(jnp.logical_or(j > 0, i > 0))
-                def _():
-                    wait(slot, TILE)
-
-                block(slot, i, start + (j * slots + slot) * TILE, TILE)
+            slot = j % slots
+
+            @pl.when(jnp.logical_or(j >= slots, i > 0))
+            def _():
+                wait(slot, TILE)
+
+            block(slot, i, start + j * TILE, TILE)
 
     rest = stop - start - rounds * slots * TILE
     wait(0, TILE)

time: 349 us -> 344 us (0.986)
  the two profiles are of different devices: /device:TPU:1 before, /device:TPU:0 now
where the time goes in v7:
time: 344 us; the launch traced here: 343 us
  Pallas kernels  338 us (98%)
  local copies, waits for them, and re-layouts  3.65 us (1%)
    pallas_call x2, Pallas kernels, run_kernel(): pl.pallas_call(body, out_shape=[jax.ShapeDtypeStruct(o[0], o[1]) for o in...  338 us

profile of v7, /device:TPU:0, one launch (start us, length us, event | category | flops | bytes accessed | tf_op | source)
XLA Modules:
  0.0 343.2 jit_solution(1161643107691883248)
XLA Ops:
  0.7 0.7 compare_convert_fusion
  1.4 0.9 dynamic_update_slice.3
  2.3 0.6 pad.4.refs_3_
  2.9 0.8 broadcast_in_dim.4.refs_2_
  3.6 335.4 %shard_map.155 = (bf16[256,1024]{1,0:T(8,128)(2,1)}, bf16[256,1024]{1,0:T(8,128)(2,1)}, bf16[1024,4096]{1,0:T(8,128)(2,1)}, bf16[1,16,2,32,2048]{4,3,2,1,0:T(8,1...) custom-call(bf16[256,1024]{1,0:T(8,128)(2,1)} %bitcast.12, ...), custom_call_target="tpu_custom_call" | custom-call | tf_op jit(solution)/shard_map/pallas_call | solution.py:1269
  339.0 2.8 shard_map.156
  341.8 1.4 dynamic_slice.3
  (1 shorter events, 0.0 us)
